TPU v7x, 256 devices: a whole 4x4x8 slice. The times are simulated.
256 devices in a mesh: seq: 64 (over x, z, core), tensor: 4 (over y).
Axes of the slice: x: 4, y: 4, z: 8, core: 2. Of those that a mesh axis runs over, the one named last changes fastest.
Arguments:
- queries: bfloat16 [32768, 16384], P(('seq', 'tensor')), may hold values from -200 to 200
- keys: bfloat16 [32768, 1024], P(('seq', 'tensor')), may hold values from -6 to 6
- values: bfloat16 [32768, 1024], P(('seq', 'tensor')), may hold values from -6 to 6
- lengths: int32 [48], replicated, may hold values from 1 to 7, 256 in all
- parents: int32 [48], replicated, may hold values from 0 to 46, as said below
- headers: int32 [48], replicated, may hold values from 1 to 2
Outputs:
- attention: bfloat16 [32768, 16384], P(('seq', 'tensor'))
Inputs may be any that keep to these rules, and one draw needn't show every extreme that they name: parents[0] is 0, the root; every other child c has parents[c] < c; from every child the root is reached in at most 3 steps, and some child needs exactly 3.
All inputs are finite; a program needn't handle non-finite values.
Results may differ from a plain program's by a relative error of at most 0.0055.
Values may be sent and summed in bfloat16 or wider, within the bound.
No kernel may reach another device: no remote copies, remote signals or barrier semaphores. Data moves between devices by JAX's collectives and lax.ppermute only.
A program may use at most 128 MiB of HBM per device.

v0:
```python
import jax
import jax.numpy as jnp
from jax import lax
from jax.sharding import PartitionSpec as P

HEAD_SIZE = 128
MASK_BLOCK_SIZE = 128
MAXLEN = 7
HDR = 2
DEPTH = 4


def for_sending(x):
    return jax.tree.map(lambda a: a.astype(jnp.bfloat16) if a.dtype == jnp.float32 else a, x)


def lookup(small_table, where_ids):
    slot_ids = jnp.arange(small_table.shape[0], dtype=jnp.int32)
    picked = jnp.where(where_ids[..., None] == slot_ids, small_table, 0)
    return jnp.sum(picked, axis=-1)


def block_lists(lengths, parents, headers, block_ids):
    starts = jnp.cumsum(lengths) - lengths
    header_len = jnp.minimum(headers, lengths)
    owner_child = jnp.sum((starts[None, :] <= block_ids[:, None]).astype(jnp.int32), axis=1) - 1
    entry_list = []
    flag_list = []
    current = owner_child
    for level_step in range(DEPTH - 1):
        has_parent = current != 0
        current = lookup(parents, current)
        first_block = lookup(starts, current)
        header_count = lookup(header_len, current)
        for offset in range(HDR):
            entry_list.append(first_block + offset)
            flag_list.append(has_parent & (offset < header_count))
    first_block = lookup(starts, owner_child)
    for offset in range(MAXLEN):
        entry_list.append(first_block + offset)
        flag_list.append(first_block + offset <= block_ids)
    entries = jnp.stack(entry_list, axis=1)
    flags = jnp.stack(flag_list, axis=1)
    entries = jnp.where(flags, entries, 0)
    return (entries, flags)


def body(queries, keys, values, lengths, parents, headers):
    tok_rows = queries.shape[0]
    seq_count = lax.axis_size("seq")
    ten_count = lax.axis_size("tensor")
    ten_index = lax.axis_index("tensor")
    head_count = queries.shape[1] // HEAD_SIZE
    kv_count = keys.shape[1] // HEAD_SIZE
    per_device = head_count // seq_count
    block_count = tok_rows * seq_count * ten_count // MASK_BLOCK_SIZE
    per_shard = tok_rows // MASK_BLOCK_SIZE
    my_queries = lax.all_to_all(queries, "seq", split_axis=1, concat_axis=0, tiled=True)

    def widen_heads(source):
        row_count = source.shape[0]
        spread = jnp.repeat(
            source.reshape(row_count, kv_count, HEAD_SIZE), seq_count // kv_count, axis=1
        )
        return spread.reshape(row_count, seq_count * HEAD_SIZE)

    key_part, value_part = (
        lax.all_to_all(widen_heads(keys), "seq", split_axis=1, concat_axis=0, tiled=True),
        lax.all_to_all(widen_heads(values), "seq", split_axis=1, concat_axis=0, tiled=True),
    )
    key_all, value_all = (
        lax.all_gather(
            key_part.reshape(seq_count, 1, tok_rows, HEAD_SIZE), "tensor", axis=1, tiled=True
        ),
        lax.all_gather(
            value_part.reshape(seq_count, 1, tok_rows, HEAD_SIZE), "tensor", axis=1, tiled=True
        ),
    )
    blocked_keys = key_all.reshape(block_count, MASK_BLOCK_SIZE, HEAD_SIZE)
    blocked_values = value_all.reshape(block_count, MASK_BLOCK_SIZE, HEAD_SIZE)
    local_blocks = seq_count * per_shard
    blocked_queries = my_queries.reshape(local_blocks, MASK_BLOCK_SIZE, per_device, HEAD_SIZE)
    local_ids = jnp.arange(local_blocks, dtype=jnp.int32)
    block_ids = (local_ids // per_shard * ten_count + ten_index) * per_shard + local_ids % per_shard
    entries, flags = block_lists(lengths, parents, headers, block_ids)
    positions = jnp.arange(MASK_BLOCK_SIZE, dtype=jnp.int32)
    causal = positions[None, :] <= positions[:, None]
    score_scale = HEAD_SIZE ** (-0.5)

    def attend(record):
        query_block, entry_row, flag_row, block_id = record
        key_tile = jnp.take(blocked_keys, entry_row, axis=0)
        value_tile = jnp.take(blocked_values, entry_row, axis=0)
        scores = (
            jnp.einsum("tpd,ksd->ptks", query_block, key_tile, preferred_element_type=jnp.float32)
            * score_scale
        )
        usable = flag_row[None, :, None] & (
            (entry_row[None, :, None] != block_id) | causal[:, None, :]
        )
        scores = jnp.where(usable[None], scores, -jnp.inf)
        row_max = jnp.max(scores, axis=(2, 3))
        weights = jnp.exp(scores - row_max[:, :, None, None])
        weight_sum = jnp.sum(weights, axis=(2, 3))
        mixed = jnp.einsum(
            "ptks,ksd->tpd",
            weights.astype(jnp.bfloat16),
            value_tile,
            preferred_element_type=jnp.float32,
        )
        return (mixed / jnp.transpose(weight_sum)[:, :, None]).astype(jnp.bfloat16)

    output = lax.map(attend, (blocked_queries, entries, flags, block_ids), batch_size=8)
    attention_local = output.reshape(local_blocks * MASK_BLOCK_SIZE, per_device * HEAD_SIZE)
    return lax.all_to_all(
        for_sending(attention_local), "seq", split_axis=0, concat_axis=1, tiled=True
    ).astype(attention_local.dtype)


def solution(mesh):
    in_specs = (
        P(("seq", "tensor"), None),
        P(("seq", "tensor"), None),
        P(("seq", "tensor"), None),
        P(),
        P(),
        P(),
    )
    out_specs = P(("seq", "tensor"), None)
    return jax.shard_map(body, mesh=mesh, in_specs=in_specs, out_specs=out_specs, check_vma=False)
```

profile of v0, /device:TPU:65, one launch (start us, length us, event | category | flops | bytes accessed | tf_op | source)
XLA Modules:
  0.0 754.1 jit_solution(14068019234546030149)
XLA Ops:
  8.1 59.9 %all_to_all.67 = bf16[128,64,128]{2,0,1:T(8,128)(2,1)} all-to-all(bf16[128,64,128]{2,0,1:T(8,128)(2,1)S(1)} %bitcast.135), channel_id=1, replica_groups=mesh['seq'=64,'tensor'=4] {'seq'}, dimensions={1} | all-to-all | bytes 4194304 | tf_op jit(solution)/shard_map/all_to_all | solution.py:69
  68.5 56.9 %all_to_all.68 = bf16[128,64,128]{2,0,1:T(8,128)(2,1)} all-to-all(bf16[128,64,128]{2,0,1:T(8,128)(2,1)S(1)} %bitcast.136), channel_id=1, replica_groups=mesh['seq'=64,'tensor'=4] {'seq'}, dimensions={1} | all-to-all | bytes 4194304 | tf_op jit(solution)/shard_map/all_to_all | solution.py:68
  125.5 6.4 copy.52
  131.9 8.8 %all-to-all-start.2 = ((bf16[128,64,256]{0,2,1:T(8,128)(2,1)}), bf16[128,64,256]{0,2,1:T(8,128)(2,1)}, u32[]{:S(2)}, u32[]{:S(2)}) async-start(bf16[128,64,256]{0,2,1:T(8,128)(2,1)} %bitcast.131), calls=%async_computation.2 | async-start | bytes 8388608 | tf_op jit(solution)/shard_map/all_to_all | solution.py:58
  143.1 90.9 %all-to-all-done.2 = bf16[128,64,256]{0,2,1:T(8,128)(2,1)} async-done(((bf16[128,64,256]{0,2,1:T(8,128)(2,1)}), bf16[128,64,256]{0,2,1:T(8,128)(2,1)}, u32[]{:S(2)}, u32[]{:S(2)}) %all-to-all-start.2) | async-done | bytes 4194336 | tf_op jit(solution)/shard_map/all_to_all | solution.py:58
  234.0 7.3 all-gather.7.cloned.1.call-done
  241.3 382.3 %while.11 = (s32[]{:T(128)}, bf16[8,8,128,2,128]{2,4,3,1,0:T(8,128)(2,1)}, s32[8,8,13]{2,1,0:T(8,128)S(1)}, bf16[256,128,128]{2,1,0:T(8,128)(2,1)}, pred[8,8,13]...) while((s32[]{:T(128)}, ...), condition=%wide.region_15.17_spmd.clone, body=%wide.region_12.16_spmd.clone.sunk | while | flops 1789671168 | bytes 76104552 | solution.py:113
  242.7 6.3 gather_fusion
  249.0 9.5 %fusion.63 = (f32[8,2,128]{2,1,0:T(2,128)S(1)}, f32[8,13,128,128,2]{3,2,4,1,0:T(8,128)}) fusion(pred[8,128,13,128]{1,3,2,0:T(8,128)(4,1)S(1)} %or_and_fusion.2, bf16[8,8,128,2,128]{2,4,3,1,0:T(8,128)(2,1)} %get-tuple-element.234, s32[]{:T(128)} %get-tuple-element.218, bf16[8,13,128,128]{3,2,1,0:T(8,128)(2,1)} %bitcast.128, ...), kind=kOutput, calls=%fused_computation.7.clone.1 | convolution fusion | flops 884340736 | bytes 19276392 | tf_op jit(solution)/shard_map/while/body/eval_jaxpr/vmap(tpd,ksd->ptks)/dot_general | solution.py:95
  258.5 8.6 %fusion.64 = f32[8,2,128]{2,1,0:T(2,128)S(1)} fusion(f32[8,13,128,128,2]{3,2,4,1,0:T(8,128)} %get-tuple-element.207, f32[8,2,128]{2,1,0:T(2,128)S(1)} %get-tuple-element.208, pred[8,128,13,128]{1,3,2,0:T(8,128)(4,1)S(1)} %or_and_fusion.2), kind=kLoop, calls=%fused_computation.5.clone.1 | loop fusion | flops 13629440 | bytes 15351808 | tf_op jit(solution)/shard_map/while/body/eval_jaxpr/vmap()/reduce_sum | solution.py:104
  267.0 6.1 gather_fusion.1
  278.8 10.4 %fusion.65 = bf16[8,8,128,2,128]{2,4,3,1,0:T(8,128)(2,1)} fusion(bf16[8,8,128,2,128]{2,4,3,1,0:T(8,128)(2,1)} %get-tuple-element.219, s32[]{:T(128)} %get-tuple-element.218, f32[8,13,128,128,2]{3,2,4,1,0:T(8,128)} %get-tuple-element.207, f32[8,2,128]{2,1,0:T(2,128)S(1)} %get-tuple-element.208, pred[8,128,13,128]{1,3,2,0:T(8,128)(4,1)S(1)} %or_and_fusion.2, ...), kind=kOutput, calls=%fused_computation.23.clone.1 | convolution fusion | flops 888274944 | bytes 19284584 | tf_op jit(solution)/shard_map/while/body/eval_jaxpr/vmap(ptks,ksd->tpd)/dot_general | solution.py:105
  290.5 6.3 gather_fusion
  296.8 9.5 %fusion.63 = (f32[8,2,128]{2,1,0:T(2,128)S(1)}, f32[8,13,128,128,2]{3,2,4,1,0:T(8,128)}) fusion(pred[8,128,13,128]{1,3,2,0:T(8,128)(4,1)S(1)} %or_and_fusion.2, bf16[8,8,128,2,128]{2,4,3,1,0:T(8,128)(2,1)} %get-tuple-element.234, s32[]{:T(128)} %get-tuple-element.218, bf16[8,13,128,128]{3,2,1,0:T(8,128)(2,1)} %bitcast.128, ...), kind=kOutput, calls=%fused_computation.7.clone.1 | convolution fusion | flops 884340736 | bytes 19276392 | tf_op jit(solution)/shard_map/while/body/eval_jaxpr/vmap(tpd,ksd->ptks)/dot_general | solution.py:95
  306.3 8.6 %fusion.64 = f32[8,2,128]{2,1,0:T(2,128)S(1)} fusion(f32[8,13,128,128,2]{3,2,4,1,0:T(8,128)} %get-tuple-element.207, f32[8,2,128]{2,1,0:T(2,128)S(1)} %get-tuple-element.208, pred[8,128,13,128]{1,3,2,0:T(8,128)(4,1)S(1)} %or_and_fusion.2), kind=kLoop, calls=%fused_computation.5.clone.1 | loop fusion | flops 13629440 | bytes 15351808 | tf_op jit(solution)/shard_map/while/body/eval_jaxpr/vmap()/reduce_sum | solution.py:104
  314.8 6.1 gather_fusion.1
  326.6 10.4 %fusion.65 = bf16[8,8,128,2,128]{2,4,3,1,0:T(8,128)(2,1)} fusion(bf16[8,8,128,2,128]{2,4,3,1,0:T(8,128)(2,1)} %get-tuple-element.219, s32[]{:T(128)} %get-tuple-element.218, f32[8,13,128,128,2]{3,2,4,1,0:T(8,128)} %get-tuple-element.207, f32[8,2,128]{2,1,0:T(2,128)S(1)} %get-tuple-element.208, pred[8,128,13,128]{1,3,2,0:T(8,128)(4,1)S(1)} %or_and_fusion.2, ...), kind=kOutput, calls=%fused_computation.23.clone.1 | convolution fusion | flops 888274944 | bytes 19284584 | tf_op jit(solution)/shard_map/while/body/eval_jaxpr/vmap(ptks,ksd->tpd)/dot_general | solution.py:105
  338.3 6.3 gather_fusion
  344.5 9.5 %fusion.63 = (f32[8,2,128]{2,1,0:T(2,128)S(1)}, f32[8,13,128,128,2]{3,2,4,1,0:T(8,128)}) fusion(pred[8,128,13,128]{1,3,2,0:T(8,128)(4,1)S(1)} %or_and_fusion.2, bf16[8,8,128,2,128]{2,4,3,1,0:T(8,128)(2,1)} %get-tuple-element.234, s32[]{:T(128)} %get-tuple-element.218, bf16[8,13,128,128]{3,2,1,0:T(8,128)(2,1)} %bitcast.128, ...), kind=kOutput, calls=%fused_computation.7.clone.1 | convolution fusion | flops 884340736 | bytes 19276392 | tf_op jit(solution)/shard_map/while/body/eval_jaxpr/vmap(tpd,ksd->ptks)/dot_general | solution.py:95
  354.0 8.6 %fusion.64 = f32[8,2,128]{2,1,0:T(2,128)S(1)} fusion(f32[8,13,128,128,2]{3,2,4,1,0:T(8,128)} %get-tuple-element.207, f32[8,2,128]{2,1,0:T(2,128)S(1)} %get-tuple-element.208, pred[8,128,13,128]{1,3,2,0:T(8,128)(4,1)S(1)} %or_and_fusion.2), kind=kLoop, calls=%fused_computation.5.clone.1 | loop fusion | flops 13629440 | bytes 15351808 | tf_op jit(solution)/shard_map/while/body/eval_jaxpr/vmap()/reduce_sum | solution.py:104
  362.6 6.1 gather_fusion.1
  374.4 10.4 %fusion.65 = bf16[8,8,128,2,128]{2,4,3,1,0:T(8,128)(2,1)} fusion(bf16[8,8,128,2,128]{2,4,3,1,0:T(8,128)(2,1)} %get-tuple-element.219, s32[]{:T(128)} %get-tuple-element.218, f32[8,13,128,128,2]{3,2,4,1,0:T(8,128)} %get-tuple-element.207, f32[8,2,128]{2,1,0:T(2,128)S(1)} %get-tuple-element.208, pred[8,128,13,128]{1,3,2,0:T(8,128)(4,1)S(1)} %or_and_fusion.2, ...), kind=kOutput, calls=%fused_computation.23.clone.1 | convolution fusion | flops 888274944 | bytes 19284584 | tf_op jit(solution)/shard_map/while/body/eval_jaxpr/vmap(ptks,ksd->tpd)/dot_general | solution.py:105
  386.1 6.3 gather_fusion
  392.3 9.5 %fusion.63 = (f32[8,2,128]{2,1,0:T(2,128)S(1)}, f32[8,13,128,128,2]{3,2,4,1,0:T(8,128)}) fusion(pred[8,128,13,128]{1,3,2,0:T(8,128)(4,1)S(1)} %or_and_fusion.2, bf16[8,8,128,2,128]{2,4,3,1,0:T(8,128)(2,1)} %get-tuple-element.234, s32[]{:T(128)} %get-tuple-element.218, bf16[8,13,128,128]{3,2,1,0:T(8,128)(2,1)} %bitcast.128, ...), kind=kOutput, calls=%fused_computation.7.clone.1 | convolution fusion | flops 884340736 | bytes 19276392 | tf_op jit(solution)/shard_map/while/body/eval_jaxpr/vmap(tpd,ksd->ptks)/dot_general | solution.py:95
  401.8 8.6 %fusion.64 = f32[8,2,128]{2,1,0:T(2,128)S(1)} fusion(f32[8,13,128,128,2]{3,2,4,1,0:T(8,128)} %get-tuple-element.207, f32[8,2,128]{2,1,0:T(2,128)S(1)} %get-tuple-element.208, pred[8,128,13,128]{1,3,2,0:T(8,128)(4,1)S(1)} %or_and_fusion.2), kind=kLoop, calls=%fused_computation.5.clone.1 | loop fusion | flops 13629440 | bytes 15351808 | tf_op jit(solution)/shard_map/while/body/eval_jaxpr/vmap()/reduce_sum | solution.py:104
  410.4 6.1 gather_fusion.1
  422.1 10.4 %fusion.65 = bf16[8,8,128,2,128]{2,4,3,1,0:T(8,128)(2,1)} fusion(bf16[8,8,128,2,128]{2,4,3,1,0:T(8,128)(2,1)} %get-tuple-element.219, s32[]{:T(128)} %get-tuple-element.218, f32[8,13,128,128,2]{3,2,4,1,0:T(8,128)} %get-tuple-element.207, f32[8,2,128]{2,1,0:T(2,128)S(1)} %get-tuple-element.208, pred[8,128,13,128]{1,3,2,0:T(8,128)(4,1)S(1)} %or_and_fusion.2, ...), kind=kOutput, calls=%fused_computation.23.clone.1 | convolution fusion | flops 888274944 | bytes 19284584 | tf_op jit(solution)/shard_map/while/body/eval_jaxpr/vmap(ptks,ksd->tpd)/dot_general | solution.py:105
  433.9 6.3 gather_fusion
  440.1 9.5 %fusion.63 = (f32[8,2,128]{2,1,0:T(2,128)S(1)}, f32[8,13,128,128,2]{3,2,4,1,0:T(8,128)}) fusion(pred[8,128,13,128]{1,3,2,0:T(8,128)(4,1)S(1)} %or_and_fusion.2, bf16[8,8,128,2,128]{2,4,3,1,0:T(8,128)(2,1)} %get-tuple-element.234, s32[]{:T(128)} %get-tuple-element.218, bf16[8,13,128,128]{3,2,1,0:T(8,128)(2,1)} %bitcast.128, ...), kind=kOutput, calls=%fused_computation.7.clone.1 | convolution fusion | flops 884340736 | bytes 19276392 | tf_op jit(solution)/shard_map/while/body/eval_jaxpr/vmap(tpd,ksd->ptks)/dot_general | solution.py:95
  449.6 8.6 %fusion.64 = f32[8,2,128]{2,1,0:T(2,128)S(1)} fusion(f32[8,13,128,128,2]{3,2,4,1,0:T(8,128)} %get-tuple-element.207, f32[8,2,128]{2,1,0:T(2,128)S(1)} %get-tuple-element.208, pred[8,128,13,128]{1,3,2,0:T(8,128)(4,1)S(1)} %or_and_fusion.2), kind=kLoop, calls=%fused_computation.5.clone.1 | loop fusion | flops 13629440 | bytes 15351808 | tf_op jit(solution)/shard_map/while/body/eval_jaxpr/vmap()/reduce_sum | solution.py:104
  458.2 6.1 gather_fusion.1
  469.9 10.4 %fusion.65 = bf16[8,8,128,2,128]{2,4,3,1,0:T(8,128)(2,1)} fusion(bf16[8,8,128,2,128]{2,4,3,1,0:T(8,128)(2,1)} %get-tuple-element.219, s32[]{:T(128)} %get-tuple-element.218, f32[8,13,128,128,2]{3,2,4,1,0:T(8,128)} %get-tuple-element.207, f32[8,2,128]{2,1,0:T(2,128)S(1)} %get-tuple-element.208, pred[8,128,13,128]{1,3,2,0:T(8,128)(4,1)S(1)} %or_and_fusion.2, ...), kind=kOutput, calls=%fused_computation.23.clone.1 | convolution fusion | flops 888274944 | bytes 19284584 | tf_op jit(solution)/shard_map/while/body/eval_jaxpr/vmap(ptks,ksd->tpd)/dot_general | solution.py:105
  481.7 6.3 gather_fusion
  487.9 9.5 %fusion.63 = (f32[8,2,128]{2,1,0:T(2,128)S(1)}, f32[8,13,128,128,2]{3,2,4,1,0:T(8,128)}) fusion(pred[8,128,13,128]{1,3,2,0:T(8,128)(4,1)S(1)} %or_and_fusion.2, bf16[8,8,128,2,128]{2,4,3,1,0:T(8,128)(2,1)} %get-tuple-element.234, s32[]{:T(128)} %get-tuple-element.218, bf16[8,13,128,128]{3,2,1,0:T(8,128)(2,1)} %bitcast.128, ...), kind=kOutput, calls=%fused_computation.7.clone.1 | convolution fusion | flops 884340736 | bytes 19276392 | tf_op jit(solution)/shard_map/while/body/eval_jaxpr/vmap(tpd,ksd->ptks)/dot_general | solution.py:95
  497.4 8.6 %fusion.64 = f32[8,2,128]{2,1,0:T(2,128)S(1)} fusion(f32[8,13,128,128,2]{3,2,4,1,0:T(8,128)} %get-tuple-element.207, f32[8,2,128]{2,1,0:T(2,128)S(1)} %get-tuple-element.208, pred[8,128,13,128]{1,3,2,0:T(8,128)(4,1)S(1)} %or_and_fusion.2), kind=kLoop, calls=%fused_computation.5.clone.1 | loop fusion | flops 13629440 | bytes 15351808 | tf_op jit(solution)/shard_map/while/body/eval_jaxpr/vmap()/reduce_sum | solution.py:104
  517.7 10.4 %fusion.65 = bf16[8,8,128,2,128]{2,4,3,1,0:T(8,128)(2,1)} fusion(bf16[8,8,128,2,128]{2,4,3,1,0:T(8,128)(2,1)} %get-tuple-element.219, s32[]{:T(128)} %get-tuple-element.218, f32[8,13,128,128,2]{3,2,4,1,0:T(8,128)} %get-tuple-element.207, f32[8,2,128]{2,1,0:T(2,128)S(1)} %get-tuple-element.208, pred[8,128,13,128]{1,3,2,0:T(8,128)(4,1)S(1)} %or_and_fusion.2, ...), kind=kOutput, calls=%fused_computation.23.clone.1 | convolution fusion | flops 888274944 | bytes 19284584 | tf_op jit(solution)/shard_map/while/body/eval_jaxpr/vmap(ptks,ksd->tpd)/dot_general | solution.py:105
  529.5 6.3 gather_fusion
  535.7 9.5 %fusion.63 = (f32[8,2,128]{2,1,0:T(2,128)S(1)}, f32[8,13,128,128,2]{3,2,4,1,0:T(8,128)}) fusion(pred[8,128,13,128]{1,3,2,0:T(8,128)(4,1)S(1)} %or_and_fusion.2, bf16[8,8,128,2,128]{2,4,3,1,0:T(8,128)(2,1)} %get-tuple-element.234, s32[]{:T(128)} %get-tuple-element.218, bf16[8,13,128,128]{3,2,1,0:T(8,128)(2,1)} %bitcast.128, ...), kind=kOutput, calls=%fused_computation.7.clone.1 | convolution fusion | flops 884340736 | bytes 19276392 | tf_op jit(solution)/shard_map/while/body/eval_jaxpr/vmap(tpd,ksd->ptks)/dot_general | solution.py:95
  545.2 8.6 %fusion.64 = f32[8,2,128]{2,1,0:T(2,128)S(1)} fusion(f32[8,13,128,128,2]{3,2,4,1,0:T(8,128)} %get-tuple-element.207, f32[8,2,128]{2,1,0:T(2,128)S(1)} %get-tuple-element.208, pred[8,128,13,128]{1,3,2,0:T(8,128)(4,1)S(1)} %or_and_fusion.2), kind=kLoop, calls=%fused_computation.5.clone.1 | loop fusion | flops 13629440 | bytes 15351808 | tf_op jit(solution)/shard_map/while/body/eval_jaxpr/vmap()/reduce_sum | solution.py:104
  565.5 10.4 %fusion.65 = bf16[8,8,128,2,128]{2,4,3,1,0:T(8,128)(2,1)} fusion(bf16[8,8,128,2,128]{2,4,3,1,0:T(8,128)(2,1)} %get-tuple-element.219, s32[]{:T(128)} %get-tuple-element.218, f32[8,13,128,128,2]{3,2,4,1,0:T(8,128)} %get-tuple-element.207, f32[8,2,128]{2,1,0:T(2,128)S(1)} %get-tuple-element.208, pred[8,128,13,128]{1,3,2,0:T(8,128)(4,1)S(1)} %or_and_fusion.2, ...), kind=kOutput, calls=%fused_computation.23.clone.1 | convolution fusion | flops 888274944 | bytes 19284584 | tf_op jit(solution)/shard_map/while/body/eval_jaxpr/vmap(ptks,ksd->tpd)/dot_general | solution.py:105
  577.2 6.3 gather_fusion
  583.5 9.5 %fusion.63 = (f32[8,2,128]{2,1,0:T(2,128)S(1)}, f32[8,13,128,128,2]{3,2,4,1,0:T(8,128)}) fusion(pred[8,128,13,128]{1,3,2,0:T(8,128)(4,1)S(1)} %or_and_fusion.2, bf16[8,8,128,2,128]{2,4,3,1,0:T(8,128)(2,1)} %get-tuple-element.234, s32[]{:T(128)} %get-tuple-element.218, bf16[8,13,128,128]{3,2,1,0:T(8,128)(2,1)} %bitcast.128, ...), kind=kOutput, calls=%fused_computation.7.clone.1 | convolution fusion | flops 884340736 | bytes 19276392 | tf_op jit(solution)/shard_map/while/body/eval_jaxpr/vmap(tpd,ksd->ptks)/dot_general | solution.py:95
  593.0 8.6 %fusion.64 = f32[8,2,128]{2,1,0:T(2,128)S(1)} fusion(f32[8,13,128,128,2]{3,2,4,1,0:T(8,128)} %get-tuple-element.207, f32[8,2,128]{2,1,0:T(2,128)S(1)} %get-tuple-element.208, pred[8,128,13,128]{1,3,2,0:T(8,128)(4,1)S(1)} %or_and_fusion.2), kind=kLoop, calls=%fused_computation.5.clone.1 | loop fusion | flops 13629440 | bytes 15351808 | tf_op jit(solution)/shard_map/while/body/eval_jaxpr/vmap()/reduce_sum | solution.py:104
  613.3 10.4 %fusion.65 = bf16[8,8,128,2,128]{2,4,3,1,0:T(8,128)(2,1)} fusion(bf16[8,8,128,2,128]{2,4,3,1,0:T(8,128)(2,1)} %get-tuple-element.219, s32[]{:T(128)} %get-tuple-element.218, f32[8,13,128,128,2]{3,2,4,1,0:T(8,128)} %get-tuple-element.207, f32[8,2,128]{2,1,0:T(2,128)S(1)} %get-tuple-element.208, pred[8,128,13,128]{1,3,2,0:T(8,128)(4,1)S(1)} %or_and_fusion.2, ...), kind=kOutput, calls=%fused_computation.23.clone.1 | convolution fusion | flops 888274944 | bytes 19284584 | tf_op jit(solution)/shard_map/while/body/eval_jaxpr/vmap(ptks,ksd->tpd)/dot_general | solution.py:105
  623.7 6.4 copy.64
  630.1 104.4 %all_to_all.69 = bf16[64,128,256]{2,1,0:T(8,128)(2,1)} all-to-all(bf16[64,128,256]{2,1,0:T(8,128)(2,1)} %copy.64), channel_id=1, replica_groups=mesh['seq'=64,'tensor'=4] {'seq'}, dimensions={0} | all-to-all | bytes 8388608 | tf_op jit(solution)/shard_map/all_to_all | solution.py:115
  734.4 6.4 copy.57
  740.8 6.4 copy.58
  (142 shorter events, 78.3 us)
Async XLA Ops:
  6.5 1.0 copy-start
  6.5 227.5 %all-gather.5.cloned.1.call-start = ((), (), s32[]{:S(2)}) async-start(), calls=%async_computation.4 | async-start | bytes 10485760 | tf_op jit(solution)/shard_map/all_gather | solution.py:75
  7.5 60.4 %copy-start.2 = (bf16[128,1024]{1,0:T(8,128)(2,1)S(1)}, bf16[128,1024]{1,0:T(8,128)(2,1)}, u32[]{:S(2)}) copy-start(bf16[128,1024]{1,0:T(8,128)(2,1)} %param.11) | copy-start | bytes 786436
  67.9 173.4 %all-gather.7.cloned.1.call-start = ((), (), s32[]{:S(2)}) async-start(), calls=%async_computation.5 | async-start | bytes 10485760 | tf_op jit(solution)/shard_map/all_gather | solution.py:72
  131.9 8.9 %copy-start.3 = (s32[48]{0:T(128)S(1)}, s32[48]{0:T(128)}, u32[]{:S(2)}) copy-start(s32[48]{0:T(128)} %param.13) | copy-start | bytes 580
  131.9 9.2 %copy-start.4 = (s32[48]{0:T(128)S(1)}, s32[48]{0:T(128)}, u32[]{:S(2)}) copy-start(s32[48]{0:T(128)} %param.15) | copy-start | bytes 580
  131.9 9.3 %copy-start.5 = (s32[48]{0:T(128)S(1)}, s32[48]{0:T(128)}, u32[]{:S(2)}) copy-start(s32[48]{0:T(128)} %param.14) | copy-start | bytes 580
  131.9 102.1 %all-to-all-start.2 = ((bf16[128,64,256]{0,2,1:T(8,128)(2,1)}), bf16[128,64,256]{0,2,1:T(8,128)(2,1)}, u32[]{:S(2)}, u32[]{:S(2)}) async-start(bf16[128,64,256]{0,2,1:T(8,128)(2,1)} %bitcast.131), calls=%async_computation.2 | async-start | bytes 8388608 | tf_op jit(solution)/shard_map/all_to_all | solution.py:58
  740.8 6.4 copy-start.1
Sparse Core Ops, SparseCore 0:
  68.0 84.7 all-gather.4
  154.7 86.5 all-gather.6
where the time goes:
time: 761 us; the launch traced here: 754 us
  blocking collectives  221 us (29%)
  local copies, waits for them, and re-layouts  174 us (23%)
  matrix products  159 us (21%)
  waiting for transfers between devices  98.3 us (13%)
  other arithmetic  79.5 us (10%)
  between operations  13.7 us (2%)
  starting transfers between devices  8.87 us (1%)
    all_to_all x1, blocking collectives, body(): lax.all_to_all(for_sending(attention_local), 'seq', split_axis=0, concat_...  104 us
    gather x16, local copies, waits for them, and re-layouts, attend(): value_tile = jnp.take(blocked_values, entry_row, axis=0)  94 us
    all_to_all x1, waiting for transfers between devices, body(): lax.all_to_all(queries, 'seq', split_axis=1, concat_axis=0, tiled=True)  90.9 us
    dot_general x8, matrix products, attend(): jnp.einsum('ptks,ksd->tpd', weights.astype(jnp.bfloat16), value_tile, pre...  82.8 us
    dot_general x8, matrix products, attend(): jnp.einsum('tpd,ksd->ptks', query_block, key_tile, preferred_element_type...  76 us
    reduce_sum x8, other arithmetic, attend(): weight_sum = jnp.sum(weights, axis=(2, 3))  68.5 us
    all_to_all x1, blocking collectives, body(): lax.all_to_all(widen_heads(values), 'seq', split_axis=1, concat_axis=0, t...  59.9 us
    all_to_all x1, blocking collectives, body(): lax.all_to_all(widen_heads(keys), 'seq', split_axis=1, concat_axis=0, til...  56.9 us
  transfers between devices with their start and end apart: 3, of which 2 were waited for; matrix products, arithmetic and copies ran while one was open for 1% of the time, Pallas kernels for 0%

commit v1 on v0

v1 whole, which is shorter than its diff:
```python
import functools

import jax
import jax.numpy as jnp
from jax import lax
from jax.experimental import pallas as pl
from jax.experimental.pallas import tpu as pltpu
from jax.sharding import Mesh
from jax.sharding import PartitionSpec as P

HEAD = 128
BLK = 128
MAXLEN = 7
HDR = 2
DEPTH = 4
GROUP = 8
WINDOW = MAXLEN - 1
NEAR = WINDOW + GROUP
FAST_SLOTS = 32
ALL_SLOTS = 64
LIST = WINDOW + (DEPTH - 1) * HDR
NEG = -1e30
EXP_SCALE = HEAD ** (-0.5) * 1.4426950408889634


def lookup(table, ids):
    slots = jnp.arange(table.shape[0], dtype=jnp.int32)
    return jnp.sum(jnp.where(ids[..., None] == slots, table, 0), axis=-1)


def tree_tables(lengths, parents, headers, group_id):
    child_count = lengths.shape[0]
    child = jnp.arange(child_count, dtype=jnp.int32)
    before = child[None, :] < child[:, None]
    starts = jnp.sum(jnp.where(before, lengths[None, :], 0), axis=1)
    header_len = jnp.minimum(headers, lengths)
    inner = jnp.any((parents[None, :] == child[:, None]) & (child[None, :] > 0), axis=1)
    kept = jnp.where(inner, header_len, 0)
    slot_of = jnp.sum(jnp.where(before, kept[None, :], 0), axis=1)
    total = jnp.sum(kept)
    slot = jnp.arange(ALL_SLOTS, dtype=jnp.int32)
    inside = (slot[:, None] >= slot_of[None, :]) & (slot[:, None] < (slot_of + kept)[None, :])
    slot_block = jnp.sum(
        jnp.where(inside, starts[None, :] + slot[:, None] - slot_of[None, :] + 1, 0), axis=1
    ) - 1

    block = group_id * GROUP + jnp.arange(GROUP, dtype=jnp.int32)
    owner = jnp.sum((starts[None, :] <= block[:, None]).astype(jnp.int32), axis=1) - 1
    start = lookup(starts, owner)
    own_full = block - start
    k = jnp.arange(LIST, dtype=jnp.int32)[None, :]
    entries = jnp.where(k < own_full[:, None], (start - group_id * GROUP + WINDOW)[:, None] + k, 0)
    filled = own_full
    current = owner
    for _ in range(DEPTH - 1):
        has_parent = current != 0
        current = lookup(parents, current)
        count = jnp.where(has_parent, lookup(header_len, current), 0)
        first = NEAR + lookup(slot_of, current)
        here = (k >= filled[:, None]) & (k < (filled + count)[:, None])
        entries = jnp.where(here, first[:, None] + k - filled[:, None], entries)
        filled = filled + count
    return slot_block, total, entries, filled


def attend_kernel(heads, filled_ref, entries_ref, near_ref, fast_ref, rest_ref, query_ref, out_ref,
                  pool, sems, scores, top, acc, den):
    step = pl.program_id(0)
    rows = heads * BLK

    @pl.when(step == 0)
    def _():
        copies = [
            pltpu.make_async_copy(near_ref, pool.at[pl.ds(0, NEAR)], sems.at[0]),
            pltpu.make_async_copy(fast_ref, pool.at[pl.ds(NEAR, FAST_SLOTS)], sems.at[1]),
            pltpu.make_async_copy(
                rest_ref, pool.at[pl.ds(NEAR + FAST_SLOTS, ALL_SLOTS - FAST_SLOTS)], sems.at[2]
            ),
        ]
        for c in copies:
            c.start()
        for c in copies:
            c.wait()

    filled = filled_ref[step]
    pairs = filled // 2
    odd = filled - 2 * pairs
    last = entries_ref[step, jnp.maximum(filled - 1, 0)]
    diagonal = step + WINDOW

    def tile(which, a, b):
        return jnp.concatenate([pool[a, which], pool[b, which]], axis=0)

    def queries(h):
        return query_ref[0, :, h * HEAD:(h + 1) * HEAD]

    def score(q, keys):
        return lax.dot_general(q, keys, (((1,), (1,)), ((), ())), preferred_element_type=jnp.float32)

    row = lax.broadcasted_iota(jnp.int32, (BLK, 2 * BLK), 0)
    col = lax.broadcasted_iota(jnp.int32, (BLK, 2 * BLK), 1)
    usable = (col <= row) | ((col >= BLK) & (odd == 1))
    keys = tile(0, diagonal, last)
    for h in range(heads):
        s = jnp.where(usable, score(queries(h), keys), NEG)
        r = slice(h * BLK, (h + 1) * BLK)
        scores[0, r, :] = s
        top[r, :] = jnp.maximum(s[:, :BLK], s[:, BLK:])

    def first_pass(p, carry):
        keys = tile(0, entries_ref[step, 2 * p], entries_ref[step, 2 * p + 1])
        for h in range(heads):
            s = score(queries(h), keys)
            r = slice(h * BLK, (h + 1) * BLK)
            scores[p + 1, r, :] = s
            top[r, :] = jnp.maximum(top[r, :], jnp.maximum(s[:, :BLK], s[:, BLK:]))
        return carry

    lax.fori_loop(0, pairs, first_pass, 0)

    def weigh(p, a, b, fresh):
        vals = tile(1, a, b)
        for h in range(heads):
            r = slice(h * BLK, (h + 1) * BLK)
            t = top[r, :]
            s = scores[p, r, :]
            w0 = jnp.exp2((s[:, :BLK] - t) * EXP_SCALE)
            w1 = jnp.exp2((s[:, BLK:] - t) * EXP_SCALE)
            mixed = jnp.dot(
                jnp.concatenate([w0, w1], axis=1).astype(jnp.bfloat16), vals,
                preferred_element_type=jnp.float32,
            )
            if fresh:
                den[r, :] = w0 + w1
                acc[r, :] = mixed
            else:
                den[r, :] += w0 + w1
                acc[r, :] += mixed

    for h in range(heads):
        r = slice(h * BLK, (h + 1) * BLK)
        top[r, :] = jnp.broadcast_to(jnp.max(top[r, :], axis=1, keepdims=True), (BLK, BLK))
    weigh(0, diagonal, last, True)

    def second_pass(p, carry):
        weigh(p + 1, entries_ref[step, 2 * p], entries_ref[step, 2 * p + 1], False)
        return carry

    lax.fori_loop(0, pairs, second_pass, 0)
    for h in range(heads):
        r = slice(h * BLK, (h + 1) * BLK)
        total = jnp.sum(den[r, :], axis=1, keepdims=True)
        out_ref[0, :, h * HEAD:(h + 1) * HEAD] = (acc[r, :] / total).astype(out_ref.dtype)


def attend(filled, entries, near, fast, rest, query):
    width = query.shape[2]
    heads = width // HEAD
    rows = heads * BLK
    longest = 1 + LIST // 2
    return pl.pallas_call(
        functools.partial(attend_kernel, heads),
        out_shape=jax.ShapeDtypeStruct(query.shape, query.dtype),
        grid_spec=pltpu.PrefetchScalarGridSpec(
            num_scalar_prefetch=2,
            grid=(GROUP,),
            in_specs=[
                pl.BlockSpec(memory_space=pl.ANY),
                pl.BlockSpec(memory_space=pl.ANY),
                pl.BlockSpec(memory_space=pl.ANY),
                pl.BlockSpec((1, BLK, width), lambda i, *_: (i, 0, 0)),
            ],
            out_specs=pl.BlockSpec((1, BLK, width), lambda i, *_: (i, 0, 0)),
            scratch_shapes=[
                pltpu.VMEM((NEAR + ALL_SLOTS, 2, BLK, HEAD), jnp.bfloat16),
                pltpu.SemaphoreType.DMA((3,)),
                pltpu.VMEM((longest, rows, 2 * BLK), jnp.float32),
                pltpu.VMEM((rows, BLK), jnp.float32),
                pltpu.VMEM((rows, HEAD), jnp.float32),
                pltpu.VMEM((rows, BLK), jnp.float32),
            ],
        ),
        compiler_params=pltpu.CompilerParams(vmem_limit_bytes=60 * 1024 * 1024),
        name="attend",
    )(filled, entries, near, fast, rest, query)


def body(queries, keys, values, lengths, parents, headers):
    group_id = lax.axis_index(("x", "z"))
    groups = lax.axis_size(("x", "z"))
    inside = ("c", "t")
    across = ("x", "z")
    slot_block, total, entries, filled = tree_tables(lengths, parents, headers, group_id)

    def split_heads(a):
        return jnp.transpose(a.reshape(BLK, GROUP, HEAD), (1, 0, 2))

    own = jnp.stack([split_heads(keys), split_heads(values)], axis=1)
    own = lax.all_to_all(own, inside, split_axis=0, concat_axis=0, tiled=True)
    before = lax.ppermute(own[GROUP - WINDOW:], across, [(j, j + 1) for j in range(groups - 1)])
    near = jnp.concatenate([before, own], axis=0)

    def gather_slots(first, count):
        blocks = slot_block[first:first + count]
        mine = blocks - group_id * GROUP
        picked = jnp.take(own, jnp.clip(mine, 0, GROUP - 1), axis=0)
        here = (mine >= 0) & (mine < GROUP)
        picked = jnp.where(here[:, None, None, None], picked, jnp.zeros((), own.dtype))
        return lax.psum(picked, across)

    fast = gather_slots(0, FAST_SLOTS)
    rest_count = ALL_SLOTS - FAST_SLOTS
    rest = lax.cond(
        total > FAST_SLOTS,
        lambda: gather_slots(FAST_SLOTS, rest_count),
        lambda: jnp.zeros((rest_count,) + own.shape[1:], own.dtype),
    )

    wide = jnp.transpose(queries.reshape(BLK, GROUP, -1), (1, 0, 2))
    mine = lax.all_to_all(wide, inside, split_axis=0, concat_axis=0, tiled=True)
    result = attend(filled, entries, near, fast, rest, mine)
    back = lax.all_to_all(result, inside, split_axis=0, concat_axis=0, tiled=True)
    return jnp.transpose(back, (1, 0, 2)).reshape(BLK, -1)


def solution(mesh):
    inner = Mesh(mesh.devices.reshape(4, 8, 2, 4), ("x", "z", "c", "t"))
    rows = P(("x", "z", "c", "t"), None)
    return jax.shard_map(
        body, mesh=inner, in_specs=(rows, rows, rows, P(), P(), P()), out_specs=rows, check_vma=False
    )
```

time: 761 us -> 308 us (0.40)
  blocking collectives: 221 us -> 58 us
  matrix products: 159 us -> 0 us
  local copies, waits for them, and re-layouts: 174 us -> 31.1 us
  other arithmetic: 79.5 us -> 6.39 us
  waiting for transfers between devices: 98.3 us -> 146 us
  Pallas kernels: 0 us -> 36.3 us
    all_to_all x3 -> x1, blocking collectives: 221 us -> 58 us  [body(): lax.all_to_all(result, inside, split_axis=0, concat_axis=0, tiled=True)]
    dot_general x16 -> x0, matrix products: 159 us -> none  [the longest x8 82.8 us: attend(): jnp.einsum('ptks,ksd->tpd', weights.astype(jnp.bfloat16), value_tile, pre...]
    gather x24 -> x1, local copies, waits for them, and re-layouts: 144 us -> 0.95 us  [gather_slots(): picked = jnp.take(own, jnp.clip(mine, 0, GROUP - 1), axis=0)]
    psum x0 -> x1, waiting for transfers between devices: none -> 138 us  [gather_slots(): return lax.psum(picked, across)]
    all_to_all x1 -> x2, waiting for transfers between devices: 90.9 us -> 0.01 us  [the longest x1 0.01 us: body(): mine = lax.all_to_all(wide, inside, split_axis=0, concat_axis=0, tiled=True)]
    reduce_sum x13 -> x9, other arithmetic: 69 us -> 1.96 us  [the longest x4 0.81 us: lookup(): return jnp.sum(jnp.where(ids[..., None] == slots, table, 0), axis=-1)]
    pallas_call x0 -> x1, Pallas kernels: none -> 36.3 us  [attend(): pl.pallas_call(functools.partial(attend_kernel, heads), out_shape=jax.Sha...]
    all_to_all x3 -> x0, local copies, waits for them, and re-layouts: 19.1 us -> none  [body(): lax.all_to_all(for_sending(attention_local), 'seq', split_axis=0, concat_...]
  transfers between devices with their start and end apart: 3 -> 4, of which waited for: 2 -> 2; matrix products, arithmetic and copies ran while one was open for 1% -> 7% of each run, Pallas kernels for 0% -> 0%
where the time goes in v1:
time: 308 us; the launch traced here: 307 us
  waiting for transfers between devices  146 us (47%)
  blocking collectives  58 us (19%)
  Pallas kernels  36.3 us (12%)
  local copies, waits for them, and re-layouts  31.1 us (10%)
  between operations  15.6 us (5%)
  starting transfers between devices  13.6 us (4%)
  other arithmetic  6.39 us (2%)
    psum x1, waiting for transfers between devices, gather_slots(): return lax.psum(picked, across)  138 us
    all_to_all x1, blocking collectives, body(): lax.all_to_all(result, inside, split_axis=0, concat_axis=0, tiled=True)  58 us
    pallas_call x1, Pallas kernels, attend(): pl.pallas_call(functools.partial(attend_kernel, heads), out_shape=jax.Sha...  36.3 us
    unnamed x11, local copies, waits for them, and re-layouts  8.61 us
    ppermute x1, waiting for transfers between devices, body(): lax.ppermute(own[GROUP - WINDOW:], across, [(j, j + 1) for j in range(gro...  8.42 us
    reshape x1, local copies, waits for them, and re-layouts, body(): wide = jnp.transpose(queries.reshape(BLK, GROUP, -1), (1, 0, 2))  6.5 us
    transpose x1, local copies, waits for them, and re-layouts, body(): return jnp.transpose(back, (1, 0, 2)).reshape(BLK, -1)  6.45 us
    reshape x1, local copies, waits for them, and re-layouts, body(): return jnp.transpose(back, (1, 0, 2)).reshape(BLK, -1)  6.36 us
  transfers between devices with their start and end apart: 4, of which 2 were waited for; matrix products, arithmetic and copies ran while one was open for 7% of the time, Pallas kernels for 0%

profile of v1, /device:TPU:65, one launch (start us, length us, event | category | flops | bytes accessed | tf_op | source)
XLA Modules:
  0.0 307.2 jit_solution(5336459333445637448)
XLA Ops:
  7.4 1.1 copy.15
  8.5 0.2 copy.16
  8.7 1.1 copy.17
  9.8 0.2 copy.18
  10.0 0.8 pad_maximum_fusion.1
  10.8 5.1 %all-to-all-start = ((bf16[8,2,128,128]{3,2,1,0:T(8,128)(2,1)}), bf16[8,2,128,128]{3,2,1,0:T(8,128)(2,1)S(1)}, u32[]{:S(2)}, u32[]{:S(2)}) async-start(bf16[8,2,128,128]{3,2,1,0:T(8,128)(2,1)} %pad_maximum_fusion.1), calls=%async_computation | async-start | bytes 1048576 | tf_op jit(solution)/shard_map/all_to_all | solution.py:199
  16.0 6.4 %copy.19 = bf16[128,16384]{0,1:T(8,128)(2,1)} copy(bf16[128,16384]{1,0:T(8,128)(2,1)} %param.10) | data formatting | bytes 8388608 | tf_op args[0]
  22.3 6.5 %copy.20 = bf16[128,8,2048]{2,0,1:T(8,128)(2,1)} copy(bf16[128,8,2048]{0,2,1:T(8,128)(2,1)} %bitcast.15) | data formatting | bytes 8388608 | tf_op jit(solution)/shard_map/reshape | solution.py:219
  28.8 0.0 all-to-all-done
  28.8 0.0 copy-start.1
  28.8 0.0 copy-start.2
  28.8 0.0 copy-start.3
  28.9 4.9 %all-to-all-start.1 = ((bf16[8,128,2048]{2,1,0:T(8,128)(2,1)}), bf16[8,128,2048]{2,1,0:T(8,128)(2,1)}, u32[]{:S(2)}, u32[]{:S(2)}) async-start(bf16[8,128,2048]{2,1,0:T(8,128)(2,1)} %bitcast.12), calls=%async_computation.1 | async-start | bytes 8388608 | tf_op jit(solution)/shard_map/all_to_all | solution.py:220
  33.8 0.0 copy-done.1
  33.8 0.1 fusion.1
  33.9 0.0 copy-done.2
  33.9 0.0 copy-done.3
  33.9 0.6 fusion.10
  35.2 0.1 select_reduce_fusion.1
  35.4 0.1 select_reduce_fusion.2
  35.5 0.1 select_reduce_fusion
  35.6 1.8 conditional.1
  35.6 1.8 broadcast.131
  37.4 0.0 all-reduce.5.cloned.1.call-start
  37.4 0.9 gather_fusion.1
  38.4 1.7 select_select_fusion.1
  40.1 0.0 all-reduce.5.cloned.1.call-update
  40.1 0.2 convert_reduce_fusion
  40.3 0.2 select_reduce_fusion.11
  40.5 0.2 select_reduce_fusion.9
  40.7 0.2 select_reduce_fusion.7
  40.8 0.3 select_reduce_fusion.5
  41.1 0.0 copy-start
  41.2 3.5 %collective-permute-start = (bf16[6,2,128,128]{3,2,1,0:T(8,128)(2,1)S(1)}, bf16[6,2,128,128]{3,2,1,0:T(8,128)(2,1)S(1)}, u32[]{:S(2)}, u32[]{:S(2)}) collective-permute-start(bf16[6,2,128,128]{3,2,1,0:T(8,128)(2,1)S(1)} %slice.15), channel_id=1, source_target_pairs={{0,8},{8,16},{16,24},{24,32},{32,40},{40,48},{48,56},{56,64},{64,7... | collective-permute-start | bytes 1179656 | tf_op jit(solution)/shard_map/ppermute | solution.py:200
  44.7 0.7 select_select_fusion.2.entries_ref
  45.4 8.4 %collective-permute-done = bf16[6,2,128,128]{3,2,1,0:T(8,128)(2,1)S(1)} collective-permute-done((bf16[6,2,128,128]{3,2,1,0:T(8,128)(2,1)S(1)}, bf16[6,2,128,128]{3,2,1,0:T(8,128)(2,1)S(1)}, u32[]{:S(2)}, u32[]{:S(2)}) %collective-permute-start) | collective-permute-done | bytes 393248 | tf_op jit(solution)/shard_map/ppermute | solution.py:200
  53.8 1.1 pad_maximum_fusion.near_ref
  54.9 137.6 %all-reduce.5.cloned.1.call-done.fast_ref = bf16[32,2,128,128]{3,2,1,0:T(8,128)(2,1)} async-done(((bf16[32,2,128,128]{3,2,1,0:T(8,128)(2,1)}), bf16[32,2,128,128]{3,2,1,0:T(8,128)(2,1)}) %all-reduce.5.cloned.1.call-update) | async-done | bytes 2097168 | tf_op jit(solution)/shard_map/psum | solution.py:209
  192.5 0.0 all-to-all-done.1.query_ref
  192.5 0.0 copy-done
  192.5 36.3 %attend.1 = bf16[8,128,2048]{2,1,0:T(8,128)(2,1)} custom-call(s32[8]{0:T(128)} %copy-done, s32[8,12]{1,0:T(8,128)} %select_select_fusion.2.entries_ref, bf16[14,2,128,128]{3,2,1,0:T(8,128)(2,1)} %pad_maximum_fusion.near_ref, bf16[32,2,128,128]{3,2,1,0:T(8,128)(2,1)} %all-reduce.5.cloned.1.call-done.fast_ref, ...), custom_call_target="tpu_custom_call" | custom-call | tf_op jit(solution)/shard_map/attend/pallas_call | solution.py:161
  228.9 58.0 %all_to_all.15 = bf16[8,128,2048]{2,1,0:T(8,128)(2,1)} all-to-all(bf16[8,128,2048]{2,1,0:T(8,128)(2,1)} %attend.1), channel_id=1, replica_groups=mesh['x'=4,'z'=8,'c'=2,'t'=4] {'c','t'}, dimensions={0} | all-to-all | bytes 8388608 | tf_op jit(solution)/shard_map/all_to_all | solution.py:222
  286.9 6.4 %copy.21 = bf16[128,8,2048]{0,2,1:T(8,128)(2,1)} copy(bf16[128,8,2048]{2,0,1:T(8,128)(2,1)} %bitcast.13) | data formatting | bytes 8388608 | tf_op jit(solution)/shard_map/transpose | solution.py:223
  293.4 6.4 %copy.22 = bf16[128,16384]{1,0:T(8,128)(2,1)} copy(bf16[128,16384]{0,1:T(8,128)(2,1)} %bitcast.14) | data formatting | bytes 8388608 | tf_op jit(solution)/shard_map/reshape | solution.py:223
  (10 shorter events, 0.1 us)
Async XLA Ops:
  10.8 18.0 %all-to-all-start = ((bf16[8,2,128,128]{3,2,1,0:T(8,128)(2,1)}), bf16[8,2,128,128]{3,2,1,0:T(8,128)(2,1)S(1)}, u32[]{:S(2)}, u32[]{:S(2)}) async-start(bf16[8,2,128,128]{3,2,1,0:T(8,128)(2,1)} %pad_maximum_fusion.1), calls=%async_computation | async-start | bytes 1048576 | tf_op jit(solution)/shard_map/all_to_all | solution.py:199
  28.8 5.0 %copy-start.1 = (s32[48]{0:T(128)S(1)}, s32[48]{0:T(128)}, u32[]{:S(2)}) copy-start(s32[48]{0:T(128)} %param.14) | copy-start | bytes 580
  28.8 5.1 %copy-start.2 = (s32[48]{0:T(128)S(1)}, s32[48]{0:T(128)}, u32[]{:S(2)}) copy-start(s32[48]{0:T(128)} %param.15) | copy-start | bytes 580
  28.8 5.1 %copy-start.3 = (s32[48]{0:T(128)S(1)}, s32[48]{0:T(128)}, u32[]{:S(2)}) copy-start(s32[48]{0:T(128)} %param.13) | copy-start | bytes 580
  28.9 163.7 %all-to-all-start.1 = ((bf16[8,128,2048]{2,1,0:T(8,128)(2,1)}), bf16[8,128,2048]{2,1,0:T(8,128)(2,1)}, u32[]{:S(2)}, u32[]{:S(2)}) async-start(bf16[8,128,2048]{2,1,0:T(8,128)(2,1)} %bitcast.12), calls=%async_computation.1 | async-start | bytes 8388608 | tf_op jit(solution)/shard_map/all_to_all | solution.py:220
  37.4 155.1 %all-reduce.5.cloned.1.call-start = ((), (), s32[]{:S(2)}) async-start(), calls=%async_computation.4 | async-start | bytes 4194304 | tf_op jit(solution)/shard_map/psum | solution.py:209
  41.1 151.4 %copy-start = (s32[8]{0:T(128)}, s32[8]{0:T(128)S(1)}, u32[]{:S(2)}) copy-start(s32[8]{0:T(128)S(1)} %get-tuple-element.33.filled_ref) | copy-start | bytes 100
  41.2 12.7 %collective-permute-start = (bf16[6,2,128,128]{3,2,1,0:T(8,128)(2,1)S(1)}, bf16[6,2,128,128]{3,2,1,0:T(8,128)(2,1)S(1)}, u32[]{:S(2)}, u32[]{:S(2)}) collective-permute-start(bf16[6,2,128,128]{3,2,1,0:T(8,128)(2,1)S(1)} %slice.15), channel_id=1, source_target_pairs={{0,8},{8,16},{16,24},{24,32},{32,40},{40,48},{48,56},{56,64},{64,7... | collective-permute-start | bytes 1179656 | tf_op jit(solution)/shard_map/ppermute | solution.py:200
Sparse Core Ops, SparseCore 1:
  41.4 151.1 all-reduce.4

commit v2 on v1

v2 whole, which is shorter than its diff:
```python
import functools

import jax
import jax.numpy as jnp
from jax import lax
from jax.experimental import pallas as pl
from jax.experimental.pallas import tpu as pltpu
from jax.sharding import Mesh
from jax.sharding import PartitionSpec as P

HEAD = 128
BLK = 128
MAXLEN = 7
HDR = 2
DEPTH = 4
GROUP = 8
WINDOW = MAXLEN - 1
NEAR = 2 * GROUP
SLOTS = GROUP * (DEPTH - 2) * HDR + HDR
FAST_SLOTS = 8
REST_SLOTS = SLOTS - FAST_SLOTS
CHUNKS = 2
PACK_STEPS = 4
LIST = WINDOW + (DEPTH - 1) * HDR
NEG = -1e30
VMEM_LIMIT = 48 * 1024 * 1024
EXP_SCALE = HEAD ** (-0.5) * 1.4426950408889634


def lookup(table, ids):
    slots = jnp.arange(table.shape[0], dtype=jnp.int32)
    return jnp.sum(jnp.where(ids[..., None] == slots, table, 0), axis=-1)


def tree_tables(lengths, parents, headers, group_id, groups, order, place):
    child = jnp.arange(lengths.shape[0], dtype=jnp.int32)
    before = child[None, :] < child[:, None]
    starts = jnp.sum(jnp.where(before, lengths[None, :], 0), axis=1)
    header_len = jnp.minimum(headers, lengths)

    ancestor = jnp.zeros(before.shape, bool)
    climbed = child
    for _ in range(DEPTH - 1):
        has_parent = climbed != 0
        climbed = lookup(parents, climbed)
        ancestor |= has_parent[:, None] & (climbed[:, None] == child[None, :])

    first = jnp.arange(groups, dtype=jnp.int32)[:, None] * GROUP
    present = (starts[None, :] < first + GROUP) & ((starts + lengths)[None, :] > first)
    needed = jnp.any(present[:, :, None] & ancestor[None, :, :], axis=1)
    count = jnp.where(needed, header_len[None, :], 0)
    slot_of = jnp.sum(jnp.where(before[None, :, :], count[:, None, :], 0), axis=2)
    most = jnp.max(jnp.sum(count, axis=1))
    slot = jnp.arange(SLOTS, dtype=jnp.int32)[None, :, None]
    offset = slot - slot_of[:, None, :]
    inside = (offset >= 0) & (offset < count[:, None, :])
    slot_block = jnp.sum(jnp.where(inside, starts[None, None, :] + offset, 0), axis=2)

    block = group_id * GROUP + order
    owner = jnp.sum((starts[None, :] <= block[:, None]).astype(jnp.int32), axis=1) - 1
    start = lookup(starts, owner)
    filled = block - start
    my_slots = lax.dynamic_index_in_dim(slot_of, group_id, 0, keepdims=False)
    k = jnp.arange(LIST, dtype=jnp.int32)[None, :]
    near = (start - group_id * GROUP + GROUP)[:, None] + k
    half = near // GROUP
    near = half * GROUP + place(near - half * GROUP)
    entries = jnp.where(k < filled[:, None], near, 0)
    current = owner
    for _ in range(DEPTH - 1):
        has_parent = current != 0
        current = lookup(parents, current)
        size = jnp.where(has_parent, lookup(header_len, current), 0)
        at = NEAR + lookup(my_slots, current)
        here = (k >= filled[:, None]) & (k < (filled + size)[:, None])
        entries = jnp.where(here, at[:, None] + k - filled[:, None], entries)
        filled = filled + size
    return slot_block, most, entries, filled


def attend_kernel(chunk, filled_ref, entries_ref, order_ref, *refs):
    near_and_far, query_refs, refs = refs[:4], refs[4:4 + GROUP], refs[4 + GROUP:]
    out_ref, pool, asked, sems, query_sems, scores, top, acc, den = refs
    step = pl.program_id(0)
    rows = top.shape[0]
    heads = rows // BLK
    width = heads * HEAD

    def query_copy(n):
        return pltpu.make_async_copy(
            query_refs[n].at[:, pl.ds(chunk * width, width)], asked.at[n], query_sems.at[n]
        )

    @pl.when(step == 0)
    def _():
        copies = []
        at = 0
        for n, ref in enumerate(near_and_far):
            copies.append(pltpu.make_async_copy(ref, pool.at[pl.ds(at, ref.shape[0])], sems.at[n]))
            at += ref.shape[0]
        query_copy(0).start()
        for c in copies:
            c.start()
        for n in range(1, GROUP):
            query_copy(n).start()
        for c in copies:
            c.wait()

    for n in range(GROUP):
        @pl.when(step == n)
        def _():
            query_copy(n).wait()

    filled = filled_ref[step]
    pairs = filled // 2
    odd = filled - 2 * pairs
    last = entries_ref[step, jnp.maximum(filled - 1, 0)]
    diagonal = GROUP + step

    def tile(which, a, b):
        return jnp.concatenate([pool[a, which], pool[b, which]], axis=0)

    def queries(h):
        return asked[step, :, h * HEAD:(h + 1) * HEAD]

    def score(q, keys):
        return lax.dot_general(q, keys, (((1,), (1,)), ((), ())), preferred_element_type=jnp.float32)

    row = lax.broadcasted_iota(jnp.int32, (BLK, 2 * BLK), 0)
    col = lax.broadcasted_iota(jnp.int32, (BLK, 2 * BLK), 1)
    usable = (col <= row) | ((col >= BLK) & (odd == 1))
    keys = tile(0, diagonal, last)
    for h in range(heads):
        s = jnp.where(usable, score(queries(h), keys), NEG)
        r = slice(h * BLK, (h + 1) * BLK)
        scores[0, r, :] = s
        top[r, :] = jnp.maximum(s[:, :BLK], s[:, BLK:])

    def first_pass(p, carry):
        keys = tile(0, entries_ref[step, 2 * p], entries_ref[step, 2 * p + 1])
        for h in range(heads):
            s = score(queries(h), keys)
            r = slice(h * BLK, (h + 1) * BLK)
            scores[p + 1, r, :] = s
            top[r, :] = jnp.maximum(top[r, :], jnp.maximum(s[:, :BLK], s[:, BLK:]))
        return carry

    lax.fori_loop(0, pairs, first_pass, 0)

    def weigh(p, a, b, fresh):
        vals = tile(1, a, b)
        for h in range(heads):
            r = slice(h * BLK, (h + 1) * BLK)
            t = top[r, :]
            s = scores[p, r, :]
            w0 = jnp.exp2((s[:, :BLK] - t) * EXP_SCALE)
            w1 = jnp.exp2((s[:, BLK:] - t) * EXP_SCALE)
            mixed = jnp.dot(
                jnp.concatenate([w0, w1], axis=1).astype(jnp.bfloat16), vals,
                preferred_element_type=jnp.float32,
            )
            if fresh:
                den[r, :] = w0 + w1
                acc[r, :] = mixed
            else:
                den[r, :] += w0 + w1
                acc[r, :] += mixed

    for h in range(heads):
        r = slice(h * BLK, (h + 1) * BLK)
        top[r, :] = jnp.broadcast_to(jnp.max(top[r, :], axis=1, keepdims=True), (BLK, BLK))
    weigh(0, diagonal, last, True)

    def second_pass(p, carry):
        weigh(p + 1, entries_ref[step, 2 * p], entries_ref[step, 2 * p + 1], False)
        return carry

    lax.fori_loop(0, pairs, second_pass, 0)
    for h in range(heads):
        r = slice(h * BLK, (h + 1) * BLK)
        total = jnp.sum(den[r, :], axis=1, keepdims=True)
        out_ref[0, :, h * HEAD:(h + 1) * HEAD] = (acc[r, :] / total).astype(out_ref.dtype)


def copy_kernel(*refs):
    *sources, out_ref = refs
    at = 0
    for ref in sources:
        piece = ref[...].reshape(BLK, -1)
        width = piece.shape[1]
        if out_ref.ndim == 3:
            out_ref[0, :, at:at + width] = piece
        else:
            out_ref[:, at:at + width] = piece
        at += width


def pack_kernel(target_ref, query_ref, *out_refs):
    width = out_refs[0].shape[1]
    for n, out_ref in enumerate(out_refs):
        out_ref[...] = query_ref[:, pl.ds(pl.multiple_of(target_ref[n] * width, width), width)]


def pack(targets, queries):
    total = queries.shape[1]
    width = total // GROUP
    return pl.pallas_call(
        pack_kernel,
        out_shape=[jax.ShapeDtypeStruct((BLK, width), queries.dtype)] * GROUP,
        grid_spec=pltpu.PrefetchScalarGridSpec(
            num_scalar_prefetch=1,
            grid=(PACK_STEPS,),
            in_specs=[pl.BlockSpec((BLK // PACK_STEPS, total), lambda i, *_: (i, 0))],
            out_specs=[pl.BlockSpec((BLK // PACK_STEPS, width), lambda i, *_: (i, 0))] * GROUP,
        ),
        cost_estimate=pl.CostEstimate(flops=0, bytes_accessed=4 * BLK * total, transcendentals=0),
        name="pack",
    )(targets, queries)


def unpack(parts):
    width = parts[0].shape[2]
    total = GROUP * CHUNKS * width
    return pl.pallas_call(
        copy_kernel,
        out_shape=jax.ShapeDtypeStruct((BLK, total), parts[0].dtype),
        grid=(GROUP,),
        in_specs=[pl.BlockSpec((1, BLK, width), lambda i: (i, 0, 0))] * CHUNKS,
        out_specs=pl.BlockSpec((BLK, CHUNKS * width), lambda i: (0, i)),
        cost_estimate=pl.CostEstimate(flops=0, bytes_accessed=4 * BLK * total, transcendentals=0),
        name="unpack",
    )(*parts)


def attend(filled, entries, order, before, own, fast, rest, query, chunk):
    width = query[0].shape[1] // CHUNKS
    rows = width // HEAD * BLK
    longest = 1 + LIST // 2
    return pl.pallas_call(
        functools.partial(attend_kernel, chunk),
        out_shape=jax.ShapeDtypeStruct((GROUP, BLK, width), query[0].dtype),
        grid_spec=pltpu.PrefetchScalarGridSpec(
            num_scalar_prefetch=3,
            grid=(GROUP,),
            in_specs=[pl.BlockSpec(memory_space=pl.ANY)] * (4 + GROUP),
            out_specs=pl.BlockSpec((1, BLK, width), lambda i, f, e, order_ref: (order_ref[i], 0, 0)),
            scratch_shapes=[
                pltpu.VMEM((NEAR + SLOTS, 2, BLK, HEAD), jnp.bfloat16),
                pltpu.VMEM((GROUP, BLK, width), jnp.bfloat16),
                pltpu.SemaphoreType.DMA((4,)),
                pltpu.SemaphoreType.DMA((GROUP,)),
                pltpu.VMEM((longest, rows, 2 * BLK), jnp.float32),
                pltpu.VMEM((rows, BLK), jnp.float32),
                pltpu.VMEM((rows, HEAD), jnp.float32),
                pltpu.VMEM((rows, BLK), jnp.float32),
            ],
        ),
        compiler_params=pltpu.CompilerParams(vmem_limit_bytes=VMEM_LIMIT),
        cost_estimate=pl.CostEstimate(
            flops=GROUP * rows * 4 * 8 * BLK * HEAD, bytes_accessed=6 << 20, transcendentals=0
        ),
        name="attend",
    )(filled, entries, order, before, own, fast, rest, *query)


def body(queries, keys, values, lengths, parents, headers):
    inside = ("c", "t")
    across = ("x", "z")
    group_id = lax.axis_index(across)
    groups = lax.axis_size(across)
    pieces = 2 * BLK // groups

    def tiles(a):
        return jnp.transpose(a.reshape(-1, pieces, GROUP, HEAD), (0, 2, 1, 3))

    def exchange(a):
        return lax.all_to_all(a, inside, split_axis=0, concat_axis=0, tiled=True)

    sent = jnp.concatenate([tiles(keys), tiles(values)], axis=0)
    everyone = lax.all_to_all(sent.reshape(-1, pieces, HEAD), across + inside, split_axis=0, concat_axis=0, tiled=True)
    core = lax.axis_index("c")
    ring = lax.axis_index("t")
    ring_size = lax.axis_size("t")
    core_size = lax.axis_size("c")
    moves = [(dc, dt) for dc in range(core_size) for dt in range(ring_size)]

    def place(r):
        return (core ^ (r // ring_size)) * ring_size + (ring - r % ring_size) % ring_size

    def move(piece, dc, dt):
        pairs = [
            (c * ring_size + t, (c ^ dc) * ring_size + (t + dt) % ring_size)
            for c in range(core_size)
            for t in range(ring_size)
        ]
        return lax.ppermute(piece, inside, pairs)

    def indices(sign):
        return jnp.stack([(core ^ dc) * ring_size + (ring + sign * dt) % ring_size for dc, dt in moves])

    targets = indices(1)
    order = indices(-1)
    packed = pack(targets, queries)
    mine = []
    for n, (dc, dt) in enumerate(moves):
        piece = packed[n]
        if dt == 2:
            hop = 1 - 2 * dc
            piece = move(piece, 0, hop)
            piece = move(piece, dc, hop)
        elif dc or dt:
            piece = move(piece, dc, dt)
        mine.append(piece)

    slot_block, most, entries, filled = tree_tables(lengths, parents, headers, group_id, groups, order, place)
    blocks = (-1, 2, BLK, HEAD)
    own = []
    for n, (dc, dt) in enumerate(moves):
        piece = lax.dynamic_index_in_dim(sent, targets[n], 1, keepdims=False)
        own.append(move(piece, dc, dt) if dc or dt else piece)
    own = jnp.stack(own).reshape(blocks)
    before = lax.ppermute(own, across, [(j, j + 1) for j in range(groups - 1)])

    def fetch(first, count):
        wanted = slot_block[:, first:first + count].reshape(-1)
        picked = jnp.take(everyone, wanted, axis=0, mode="clip").reshape(groups, count, pieces, HEAD)
        got = lax.all_to_all(picked, across, split_axis=0, concat_axis=0, tiled=True)
        return jnp.transpose(got, (1, 0, 2, 3)).reshape(blocks)

    fast = fetch(0, FAST_SLOTS)
    rest = lax.cond(
        most > FAST_SLOTS,
        lambda: fetch(FAST_SLOTS, REST_SLOTS),
        lambda: jnp.zeros((REST_SLOTS,) + own.shape[1:], own.dtype),
    )

    parts = []
    for chunk in range(CHUNKS):
        parts.append(exchange(attend(filled, entries, order, before, own, fast, rest, mine, chunk)))
    return unpack(parts)


def solution(mesh):
    inner = Mesh(mesh.devices.reshape(4, 8, 2, 4), ("x", "z", "c", "t"))
    rows = P(("x", "z", "c", "t"), None)
    return jax.shard_map(body, mesh=inner, in_specs=(rows, rows, rows, P(), P(), P()), out_specs=rows, check_vma=False)
```

time: 308 us -> 192 us (0.62)
  the two profiles are of different devices: /device:TPU:65 before, /device:TPU:3 now
where the time goes in v2:
time: 192 us; the launch traced here: 191 us
  Pallas kernels  67.2 us (35%)
  starting transfers between devices  54.7 us (28%)
  blocking collectives  31.1 us (16%)
  waiting for transfers between devices  17.8 us (9%)
  local copies, waits for them, and re-layouts  11.4 us (6%)
  other arithmetic  7.9 us (4%)
    pallas_call x2, Pallas kernels, attend(): pl.pallas_call(functools.partial(attend_kernel, chunk), out_shape=jax.Sha...  55.2 us
    all_to_all x1, blocking collectives, exchange(): return lax.all_to_all(a, inside, split_axis=0, concat_axis=0, tiled=True)  31.1 us
    ppermute x16, starting transfers between devices, move(): return lax.ppermute(piece, inside, pairs)  21.5 us
    all_to_all x1, starting transfers between devices, body(): lax.all_to_all(sent.reshape(-1, pieces, HEAD), across + inside, split_axi...  14.3 us
    ppermute x16, waiting for transfers between devices, move(): return lax.ppermute(piece, inside, pairs)  12.3 us
    all_to_all x1, starting transfers between devices, fetch(): lax.all_to_all(picked, across, split_axis=0, concat_axis=0, tiled=True)  10.2 us
    pallas_call x1, Pallas kernels, unpack(): pl.pallas_call(copy_kernel, out_shape=jax.ShapeDtypeStruct((BLK, total),...  6.53 us
    ppermute x1, waiting for transfers between devices, body(): before = lax.ppermute(own, across, [(j, j + 1) for j in range(groups - 1)])  5.5 us
  transfers between devices with their start and end apart: 20, of which 6 were waited for; matrix products, arithmetic and copies ran while one was open for 8% of the time, Pallas kernels for 17%

profile of v2, /device:TPU:3, one launch (start us, length us, event | category | flops | bytes accessed | tf_op | source)
XLA Modules:
  0.0 191.2 jit_solution(2950128039873652858)
XLA Ops:
  0.0 0.9 copy-done
  1.0 1.1 copy_bitcast_fusion
  2.1 3.6 %collective-permute-start.5 = (bf16[32,8,128]{2,1,0:T(8,128)(2,1)S(1)}, bf16[32,8,128]{2,1,0:T(8,128)(2,1)S(1)}, u32[]{:S(2)}, u32[]{:S(2)}) collective-permute-start(bf16[32,8,128]{2,1,0:T(8,128)(2,1)S(1)} %get-tuple-element.50), channel_id=1, source_target_pairs={{0,6},{1,7},{2,4},{3,5},{4,2},{5,3},{6,0},{7,1},{8,14},{9,15},{10,... | collective-permute-start | bytes 196616 | tf_op jit(solution)/shard_map/ppermute | solution.py:296
  5.8 0.9 copy.29
  6.8 14.3 %all-to-all-start.1 = ((bf16[256,8,128]{2,1,0:T(8,128)(2,1)}), bf16[256,8,128]{2,1,0:T(8,128)(2,1)S(1)}, u32[]{:S(2)}, u32[]{:S(2)}) async-start(bf16[256,8,128]{2,1,0:T(8,128)(2,1)} %bitcast.32), calls=%async_computation.1 | async-start | bytes 1048576 | tf_op jit(solution)/shard_map/all_to_all | solution.py:280
  21.2 2.8 %collective-permute-start.6 = (bf16[32,8,128]{2,1,0:T(8,128)(2,1)S(1)}, bf16[32,8,128]{2,1,0:T(8,128)(2,1)S(1)}, u32[]{:S(2)}, u32[]{:S(2)}) collective-permute-start(bf16[32,8,128]{2,1,0:T(8,128)(2,1)S(1)} %get-tuple-element.44), channel_id=1, source_target_pairs={{0,7},{1,4},{2,5},{3,6},{4,3},{5,0},{6,1},{7,2},{8,15},{9,12},{10,... | collective-permute-start | bytes 196616 | tf_op jit(solution)/shard_map/ppermute | solution.py:296
  24.1 1.7 collective-permute-start.1
  26.7 0.8 select_reduce_fusion.14
  28.5 0.6 select_reduce_fusion
  29.1 0.7 select_reduce_fusion.1
  29.8 0.7 reduce_max.9
  31.3 0.6 stack.101.target_ref
  32.0 5.4 %pack.1 = (bf16[128,2048]{1,0:T(8,128)(2,1)}, bf16[128,2048]{1,0:T(8,128)(2,1)}, bf16[128,2048]{1,0:T(8,128)(2,1)}, bf16[128,2048]{1,0:T(8,128)(2,1)}, bf16[128,...) custom-call(s32[8]{0:T(128)} %stack.101.target_ref, ...), custom_call_target="tpu_custom_call" | custom-call | bytes 8388608 | tf_op jit(solution)/shard_map/pack/pallas_call | solution.py:207
  37.4 0.8 select_reduce_fusion.8
  39.3 1.1 collective-permute-start.2
  40.4 0.9 collective-permute-start.3
  41.3 0.7 collective-permute-start.8
  42.0 1.6 collective-permute-start.9
  43.6 0.6 copy-done.3
  44.2 1.1 collective-permute-start.11
  45.3 0.9 collective-permute-start.12
  46.2 0.9 collective-permute-start.14
  47.1 1.6 conditional.1
  47.1 1.6 broadcast.268
  48.7 1.6 gather_fusion.1
  50.3 10.2 %all-to-all-start.2 = ((bf16[32,8,8,128]{3,2,1,0:T(8,128)(2,1)}), bf16[32,8,8,128]{3,2,1,0:T(8,128)(2,1)S(1)}, u32[]{:S(2)}, u32[]{:S(2)}) async-start(bf16[32,8,8,128]{3,2,1,0:T(8,128)(2,1)} %bitcast.59), calls=%async_computation.2 | async-start | bytes 1048576 | tf_op jit(solution)/shard_map/all_to_all | solution.py:327
  60.5 0.9 constant_dynamic-update-slice_fusion.3
  61.4 0.9 constant_dynamic-update-slice_fusion.refs_1_
  62.3 1.7 collective-permute-start.13
  64.0 3.6 %collective-permute-done.9 = bf16[128,2048]{1,0:T(8,128)(2,1)} collective-permute-done((bf16[128,2048]{1,0:T(8,128)(2,1)}, bf16[128,2048]{1,0:T(8,128)(2,1)}, u32[]{:S(2)}, u32[]{:S(2)}) %collective-permute-start.9) | collective-permute-done | bytes 524320 | tf_op jit(solution)/shard_map/ppermute | solution.py:296
  67.6 1.0 collective-permute-start.16
  68.7 3.3 %collective-permute-start.7 = (bf16[8,2,128,128]{3,2,1,0:T(8,128)(2,1)S(1)}, bf16[8,2,128,128]{3,2,1,0:T(8,128)(2,1)}, u32[]{:S(2)}, u32[]{:S(2)}) collective-permute-start(bf16[8,2,128,128]{3,2,1,0:T(8,128)(2,1)S(1)} %constant_dynamic-update-slice_fusion.refs_1_), channel_id=1, source_target_pairs={{0,8},{8,16},{16,24},{24,32},{32,40},{40,48},{48,56},{56,64},{64,7... | collective-permute-start | bytes 1572872 | tf_op jit(solution)/shard_map/ppermute | solution.py:322
  72.0 1.7 collective-permute-start.10
  73.7 1.8 collective-permute-start.15
  75.5 0.7 fusion.46
  76.2 0.7 fusion.33.entries_ref
  77.0 0.8 copy-done.2
  77.7 1.1 copy.31
  78.9 0.9 collective-permute-done.13.refs_9_
  79.8 2.0 %collective-permute-done.16.refs_11_ = bf16[128,2048]{1,0:T(8,128)(2,1)} collective-permute-done((bf16[128,2048]{1,0:T(8,128)(2,1)}, bf16[128,2048]{1,0:T(8,128)(2,1)}, u32[]{:S(2)}, u32[]{:S(2)}) %collective-permute-start.16) | collective-permute-done | bytes 524320 | tf_op jit(solution)/shard_map/ppermute | solution.py:296
  81.8 5.5 %collective-permute-done.7.refs_0_ = bf16[8,2,128,128]{3,2,1,0:T(8,128)(2,1)} collective-permute-done((bf16[8,2,128,128]{3,2,1,0:T(8,128)(2,1)S(1)}, bf16[8,2,128,128]{3,2,1,0:T(8,128)(2,1)}, u32[]{:S(2)}, u32[]{:S(2)}) %collective-permute-start.7) | collective-permute-done | bytes 524320 | tf_op jit(solution)/shard_map/ppermute | solution.py:322
  87.3 2.8 %collective-permute-done.10.refs_6_ = bf16[128,2048]{1,0:T(8,128)(2,1)} collective-permute-done((bf16[128,2048]{1,0:T(8,128)(2,1)}, bf16[128,2048]{1,0:T(8,128)(2,1)}, u32[]{:S(2)}, u32[]{:S(2)}) %collective-permute-start.10) | collective-permute-done | bytes 524320 | tf_op jit(solution)/shard_map/ppermute | solution.py:296
  90.1 2.9 %collective-permute-done.15.refs_10_ = bf16[128,2048]{1,0:T(8,128)(2,1)} collective-permute-done((bf16[128,2048]{1,0:T(8,128)(2,1)}, bf16[128,2048]{1,0:T(8,128)(2,1)}, u32[]{:S(2)}, u32[]{:S(2)}) %collective-permute-start.15) | collective-permute-done | bytes 524320 | tf_op jit(solution)/shard_map/ppermute | solution.py:296
  93.0 27.6 %attend.2 = bf16[8,128,1024]{2,1,0:T(8,128)(2,1)} custom-call(s32[8]{0:T(128)S(1)} %get-tuple-element.40.filled_ref, s32[8,12]{1,0:T(8,128)S(1)} %fusion.33.entries_ref, s32[8]{0:T(128)S(1)} %stack.85.order_ref, bf16[8,2,128,128]{3,2,1,0:T(8,128)(2,1)} %collective-permute-done.7.refs_0_, ...), custom_call_target="tpu_custom_call" | custom-call | flops 4294967296 | bytes 6291456 | tf_op jit(solution)/shard_map/attend/pallas_call | solution.py:239
  120.7 5.3 %all-to-all-start.3 = ((bf16[8,128,1024]{2,1,0:T(8,128)(2,1)}), bf16[8,128,1024]{2,1,0:T(8,128)(2,1)}, u32[]{:S(2)}, u32[]{:S(2)}) async-start(bf16[8,128,1024]{2,1,0:T(8,128)(2,1)} %attend.2), calls=%async_computation.3 | async-start | bytes 4194304 | tf_op jit(solution)/shard_map/all_to_all | solution.py:277
  126.0 27.6 %attend.3 = bf16[8,128,1024]{2,1,0:T(8,128)(2,1)} custom-call(s32[8]{0:T(128)S(1)} %get-tuple-element.40.filled_ref, s32[8,12]{1,0:T(8,128)S(1)} %fusion.33.entries_ref, s32[8]{0:T(128)S(1)} %stack.85.order_ref, bf16[8,2,128,128]{3,2,1,0:T(8,128)(2,1)} %collective-permute-done.7.refs_0_, ...), custom_call_target="tpu_custom_call" | custom-call | flops 4294967296 | bytes 6291456 | tf_op jit(solution)/shard_map/attend/pallas_call | solution.py:239
  153.6 31.1 %all_to_all.25.refs_1_ = bf16[8,128,1024]{2,1,0:T(8,128)(2,1)} all-to-all(bf16[8,128,1024]{2,1,0:T(8,128)(2,1)} %attend.3), channel_id=1, replica_groups=mesh['x'=4,'z'=8,'c'=2,'t'=4] {'c','t'}, dimensions={0} | all-to-all | bytes 4194304 | tf_op jit(solution)/shard_map/all_to_all | solution.py:277
  184.7 6.5 %unpack.1 = bf16[128,16384]{1,0:T(8,128)(2,1)} custom-call(bf16[8,128,1024]{2,1,0:T(8,128)(2,1)} %all-to-all-done.3.refs_0_, bf16[8,128,1024]{2,1,0:T(8,128)(2,1)} %all_to_all.25.refs_1_), custom_call_target="tpu_custom_call" | custom-call | bytes 8388608 | tf_op jit(solution)/shard_map/unpack/pallas_call | solution.py:224
  (75 shorter events, 3.5 us)
Async XLA Ops:
  0.0 1.0 copy-start
  2.1 39.3 %collective-permute-start.5 = (bf16[32,8,128]{2,1,0:T(8,128)(2,1)S(1)}, bf16[32,8,128]{2,1,0:T(8,128)(2,1)S(1)}, u32[]{:S(2)}, u32[]{:S(2)}) collective-permute-start(bf16[32,8,128]{2,1,0:T(8,128)(2,1)S(1)} %get-tuple-element.50), channel_id=1, source_target_pairs={{0,6},{1,7},{2,4},{3,5},{4,2},{5,3},{6,0},{7,1},{8,14},{9,15},{10,... | collective-permute-start | bytes 196616 | tf_op jit(solution)/shard_map/ppermute | solution.py:296
  5.6 36.4 %collective-permute-start.4 = (bf16[32,8,128]{2,1,0:T(8,128)(2,1)S(1)}, bf16[32,8,128]{2,1,0:T(8,128)(2,1)S(1)}, u32[]{:S(2)}, u32[]{:S(2)}) collective-permute-start(bf16[32,8,128]{2,1,0:T(8,128)(2,1)S(1)} %get-tuple-element.51), channel_id=1, source_target_pairs={{0,5},{1,6},{2,7},{3,4},{4,1},{5,2},{6,3},{7,0},{8,13},{9,14},{10,... | collective-permute-start | bytes 196616 | tf_op jit(solution)/shard_map/ppermute | solution.py:296
  5.8 20.0 %copy-start.9 = (s32[48]{0:T(128)S(1)}, s32[48]{0:T(128)}, u32[]{:S(2)}) copy-start(s32[48]{0:T(128)} %param.12) | copy-start | bytes 580
  5.8 20.5 %copy-start.11 = (s32[48]{0:T(128)S(1)}, s32[48]{0:T(128)}, u32[]{:S(2)}) copy-start(s32[48]{0:T(128)} %param.11) | copy-start | bytes 580
  5.8 22.0 %copy-start.10 = (s32[48]{0:T(128)S(1)}, s32[48]{0:T(128)}, u32[]{:S(2)}) copy-start(s32[48]{0:T(128)} %param.13) | copy-start | bytes 580
  6.8 40.3 %all-to-all-start.1 = ((bf16[256,8,128]{2,1,0:T(8,128)(2,1)}), bf16[256,8,128]{2,1,0:T(8,128)(2,1)S(1)}, u32[]{:S(2)}, u32[]{:S(2)}) async-start(bf16[256,8,128]{2,1,0:T(8,128)(2,1)} %bitcast.32), calls=%async_computation.1 | async-start | bytes 1048576 | tf_op jit(solution)/shard_map/all_to_all | solution.py:280
  21.2 22.3 %collective-permute-start.6 = (bf16[32,8,128]{2,1,0:T(8,128)(2,1)S(1)}, bf16[32,8,128]{2,1,0:T(8,128)(2,1)S(1)}, u32[]{:S(2)}, u32[]{:S(2)}) collective-permute-start(bf16[32,8,128]{2,1,0:T(8,128)(2,1)S(1)} %get-tuple-element.44), channel_id=1, source_target_pairs={{0,7},{1,4},{2,5},{3,6},{4,3},{5,0},{6,1},{7,2},{8,15},{9,12},{10,... | collective-permute-start | bytes 196616 | tf_op jit(solution)/shard_map/ppermute | solution.py:296
  24.1 15.2 %collective-permute-start = (bf16[32,8,128]{2,1,0:T(8,128)(2,1)S(1)}, bf16[32,8,128]{2,1,0:T(8,128)(2,1)S(1)}, u32[]{:S(2)}, u32[]{:S(2)}) collective-permute-start(bf16[32,8,128]{2,1,0:T(8,128)(2,1)S(1)} %get-tuple-element.46), channel_id=1, source_target_pairs={{0,1},{1,2},{2,3},{3,0},{4,5},{5,6},{6,7},{7,4},{8,9},{9,10},{10,1... | collective-permute-start | bytes 196616 | tf_op jit(solution)/shard_map/ppermute | solution.py:296
  24.1 16.3 %collective-permute-start.1 = (bf16[32,8,128]{2,1,0:T(8,128)(2,1)S(1)}, bf16[32,8,128]{2,1,0:T(8,128)(2,1)S(1)}, u32[]{:S(2)}, u32[]{:S(2)}) collective-permute-start(bf16[32,8,128]{2,1,0:T(8,128)(2,1)S(1)} %get-tuple-element.47), channel_id=1, source_target_pairs={{0,2},{1,3},{2,0},{3,1},{4,6},{5,7},{6,4},{7,5},{8,10},{9,11},{10,... | collective-permute-start | bytes 196616 | tf_op jit(solution)/shard_map/ppermute | solution.py:296
  26.7 1.0 copy-start.8
  27.5 9.9 %copy-start.5 = (s32[8]{0:T(128)}, s32[8]{0:T(128)S(1)}, u32[]{:S(2)}) copy-start(s32[8]{0:T(128)S(1)} %get-tuple-element.38) | copy-start | bytes 100
  27.6 9.8 %copy-start.7 = (s32[8]{0:T(128)}, s32[8]{0:T(128)S(1)}, u32[]{:S(2)}) copy-start(s32[8]{0:T(128)S(1)} %select_reduce_fusion.12) | copy-start | bytes 100
  39.3 6.0 %collective-permute-start.2 = (bf16[32,8,128]{2,1,0:T(8,128)(2,1)S(1)}, bf16[32,8,128]{2,1,0:T(8,128)(2,1)S(1)}, u32[]{:S(2)}, u32[]{:S(2)}) collective-permute-start(bf16[32,8,128]{2,1,0:T(8,128)(2,1)S(1)} %get-tuple-element.48), channel_id=1, source_target_pairs={{0,3},{1,0},{2,1},{3,2},{4,7},{5,4},{6,5},{7,6},{8,11},{9,8},{10,9... | collective-permute-start | bytes 196616 | tf_op jit(solution)/shard_map/ppermute | solution.py:296
  40.4 5.8 %collective-permute-start.3 = (bf16[32,8,128]{2,1,0:T(8,128)(2,1)S(1)}, bf16[32,8,128]{2,1,0:T(8,128)(2,1)S(1)}, u32[]{:S(2)}, u32[]{:S(2)}) collective-permute-start(bf16[32,8,128]{2,1,0:T(8,128)(2,1)S(1)} %get-tuple-element.49), channel_id=1, source_target_pairs={{0,4},{1,5},{2,6},{3,7},{4,0},{5,1},{6,2},{7,3},{8,12},{9,13},{10,... | collective-permute-start | bytes 196616 | tf_op jit(solution)/shard_map/ppermute | solution.py:296
  41.3 21.0 %collective-permute-start.8 = (bf16[128,2048]{1,0:T(8,128)(2,1)}, bf16[128,2048]{1,0:T(8,128)(2,1)S(1)}, u32[]{:S(2)}, u32[]{:S(2)}) collective-permute-start(bf16[128,2048]{1,0:T(8,128)(2,1)} %get-tuple-element.23), channel_id=1, source_target_pairs={{0,1},{1,2},{2,3},{3,0},{4,5},{5,6},{6,7},{7,4},{8,9},{9,10},{10,1... | collective-permute-start | bytes 1572872 | tf_op jit(solution)/shard_map/ppermute | solution.py:296
  42.0 25.6 %collective-permute-start.9 = (bf16[128,2048]{1,0:T(8,128)(2,1)}, bf16[128,2048]{1,0:T(8,128)(2,1)}, u32[]{:S(2)}, u32[]{:S(2)}) collective-permute-start(bf16[128,2048]{1,0:T(8,128)(2,1)} %get-tuple-element.24), channel_id=1, source_target_pairs={{0,1},{1,2},{2,3},{3,0},{4,5},{5,6},{6,7},{7,4},{8,9},{9,10},{10,1... | collective-permute-start | bytes 1572872 | tf_op jit(solution)/shard_map/ppermute | solution.py:296
  43.6 0.6 copy-start.3
  44.2 24.5 %collective-permute-start.11 = (bf16[128,2048]{1,0:T(8,128)(2,1)}, bf16[128,2048]{1,0:T(8,128)(2,1)S(1)}, u32[]{:S(2)}, u32[]{:S(2)}) collective-permute-start(bf16[128,2048]{1,0:T(8,128)(2,1)} %get-tuple-element.25), channel_id=1, source_target_pairs={{0,3},{1,0},{2,1},{3,2},{4,7},{5,4},{6,5},{7,6},{8,11},{9,8},{10,9... | collective-permute-start | bytes 1572872 | tf_op jit(solution)/shard_map/ppermute | solution.py:296
  45.3 26.7 %collective-permute-start.12 = (bf16[128,2048]{1,0:T(8,128)(2,1)}, bf16[128,2048]{1,0:T(8,128)(2,1)S(1)}, u32[]{:S(2)}, u32[]{:S(2)}) collective-permute-start(bf16[128,2048]{1,0:T(8,128)(2,1)} %get-tuple-element.26), channel_id=1, source_target_pairs={{0,4},{1,5},{2,6},{3,7},{4,0},{5,1},{6,2},{7,3},{8,12},{9,13},{10,... | collective-permute-start | bytes 1572872 | tf_op jit(solution)/shard_map/ppermute | solution.py:296
  46.2 0.9 copy-start.4
  46.2 27.6 %collective-permute-start.14 = (bf16[128,2048]{1,0:T(8,128)(2,1)}, bf16[128,2048]{1,0:T(8,128)(2,1)}, u32[]{:S(2)}, u32[]{:S(2)}) collective-permute-start(bf16[128,2048]{1,0:T(8,128)(2,1)} %get-tuple-element.28), channel_id=1, source_target_pairs={{0,3},{1,0},{2,1},{3,2},{4,7},{5,4},{6,5},{7,6},{8,11},{9,8},{10,9... | collective-permute-start | bytes 1572872 | tf_op jit(solution)/shard_map/ppermute | solution.py:296
  48.7 26.8 %copy-start.12 = (s32[8]{0:T(128)S(1)}, s32[8]{0:T(128)}, u32[]{:S(2)}) copy-start(s32[8]{0:T(128)} %get-tuple-element.37) | copy-start | bytes 100
  48.7 26.8 %copy-start.6 = (s32[8]{0:T(128)S(1)}, s32[8]{0:T(128)}, u32[]{:S(2)}) copy-start(s32[8]{0:T(128)} %copy-done.5) | copy-start | bytes 100
  48.7 44.3 %copy-start.1 = (bf16[128,2048]{1,0:T(8,128)(2,1)S(1)}, bf16[128,2048]{1,0:T(8,128)(2,1)}, u32[]{:S(2)}) copy-start(bf16[128,2048]{1,0:T(8,128)(2,1)} %get-tuple-element.22.refs_4_) | copy-start | bytes 1572868
  50.3 26.6 %all-to-all-start.2 = ((bf16[32,8,8,128]{3,2,1,0:T(8,128)(2,1)}), bf16[32,8,8,128]{3,2,1,0:T(8,128)(2,1)S(1)}, u32[]{:S(2)}, u32[]{:S(2)}) async-start(bf16[32,8,8,128]{3,2,1,0:T(8,128)(2,1)} %bitcast.59), calls=%async_computation.2 | async-start | bytes 1048576 | tf_op jit(solution)/shard_map/all_to_all | solution.py:327
  62.3 17.5 %collective-permute-start.13 = (bf16[128,2048]{1,0:T(8,128)(2,1)}, bf16[128,2048]{1,0:T(8,128)(2,1)}, u32[]{:S(2)}, u32[]{:S(2)}) collective-permute-start(bf16[128,2048]{1,0:T(8,128)(2,1)} %get-tuple-element.27), channel_id=1, source_target_pairs={{0,5},{1,6},{2,7},{3,4},{4,1},{5,2},{6,3},{7,0},{8,13},{9,14},{10,... | collective-permute-start | bytes 1572872 | tf_op jit(solution)/shard_map/ppermute | solution.py:296
  67.6 14.2 %collective-permute-start.16 = (bf16[128,2048]{1,0:T(8,128)(2,1)}, bf16[128,2048]{1,0:T(8,128)(2,1)}, u32[]{:S(2)}, u32[]{:S(2)}) collective-permute-start(bf16[128,2048]{1,0:T(8,128)(2,1)} %get-tuple-element.29), channel_id=1, source_target_pairs={{0,7},{1,4},{2,5},{3,6},{4,3},{5,0},{6,1},{7,2},{8,15},{9,12},{10,... | collective-permute-start | bytes 1572872 | tf_op jit(solution)/shard_map/ppermute | solution.py:296
  68.7 18.6 %collective-permute-start.7 = (bf16[8,2,128,128]{3,2,1,0:T(8,128)(2,1)S(1)}, bf16[8,2,128,128]{3,2,1,0:T(8,128)(2,1)}, u32[]{:S(2)}, u32[]{:S(2)}) collective-permute-start(bf16[8,2,128,128]{3,2,1,0:T(8,128)(2,1)S(1)} %constant_dynamic-update-slice_fusion.refs_1_), channel_id=1, source_target_pairs={{0,8},{8,16},{16,24},{24,32},{32,40},{40,48},{48,56},{56,64},{64,7... | collective-permute-start | bytes 1572872 | tf_op jit(solution)/shard_map/ppermute | solution.py:322
  72.0 18.1 %collective-permute-start.10 = (bf16[128,2048]{1,0:T(8,128)(2,1)}, bf16[128,2048]{1,0:T(8,128)(2,1)}, u32[]{:S(2)}, u32[]{:S(2)}) collective-permute-start(bf16[128,2048]{1,0:T(8,128)(2,1)} %collective-permute-done.9), channel_id=1, source_target_pairs={{0,1},{1,2},{2,3},{3,0},{4,5},{5,6},{6,7},{7,4},{8,9},{9,10},{10,1... | collective-permute-start | bytes 1572872 | tf_op jit(solution)/shard_map/ppermute | solution.py:296
  73.7 19.3 %collective-permute-start.15 = (bf16[128,2048]{1,0:T(8,128)(2,1)}, bf16[128,2048]{1,0:T(8,128)(2,1)}, u32[]{:S(2)}, u32[]{:S(2)}) collective-permute-start(bf16[128,2048]{1,0:T(8,128)(2,1)} %collective-permute-done.14), channel_id=1, source_target_pairs={{0,7},{1,4},{2,5},{3,6},{4,3},{5,0},{6,1},{7,2},{8,15},{9,12},{10,... | collective-permute-start | bytes 1572872 | tf_op jit(solution)/shard_map/ppermute | solution.py:296
  76.9 0.8 copy-start.2
  120.7 32.9 %all-to-all-start.3 = ((bf16[8,128,1024]{2,1,0:T(8,128)(2,1)}), bf16[8,128,1024]{2,1,0:T(8,128)(2,1)}, u32[]{:S(2)}, u32[]{:S(2)}) async-start(bf16[8,128,1024]{2,1,0:T(8,128)(2,1)} %attend.2), calls=%async_computation.3 | async-start | bytes 4194304 | tf_op jit(solution)/shard_map/all_to_all | solution.py:277

commit v3 on v2

--- a/solution.py
+++ b/solution.py
@@ -20,7 +20,7 @@
 FAST_SLOTS = 8
 REST_SLOTS = SLOTS - FAST_SLOTS
 CHUNKS = 2
-PACK_STEPS = 4
+STACK = 8
 LIST = WINDOW + (DEPTH - 1) * HDR
 NEG = -1e30
 VMEM_LIMIT = 48 * 1024 * 1024
@@ -120,27 +120,31 @@
     def tile(which, a, b):
         return jnp.concatenate([pool[a, which], pool[b, which]], axis=0)
 
-    def queries(h):
-        return asked[step, :, h * HEAD:(h + 1) * HEAD]
+    def queries(g):
+        return jnp.concatenate(
+            [asked[step, :, h * HEAD:(h + 1) * HEAD] for h in range(g * STACK, (g + 1) * STACK)], axis=0
+        )
 
     def score(q, keys):
         return lax.dot_general(q, keys, (((1,), (1,)), ((), ())), preferred_element_type=jnp.float32)
 
-    row = lax.broadcasted_iota(jnp.int32, (BLK, 2 * BLK), 0)
-    col = lax.broadcasted_iota(jnp.int32, (BLK, 2 * BLK), 1)
+    tall = STACK * BLK
+    groups = heads // STACK
+    row = lax.broadcasted_iota(jnp.int32, (tall, 2 * BLK), 0) % BLK
+    col = lax.broadcasted_iota(jnp.int32, (tall, 2 * BLK), 1)
     usable = (col <= row) | ((col >= BLK) & (odd == 1))
     keys = tile(0, diagonal, last)
-    for h in range(heads):
-        s = jnp.where(usable, score(queries(h), keys), NEG)
-        r = slice(h * BLK, (h + 1) * BLK)
+    for g in range(groups):
+        s = jnp.where(usable, score(queries(g), keys), NEG)
+        r = slice(g * tall, (g + 1) * tall)
         scores[0, r, :] = s
         top[r, :] = jnp.maximum(s[:, :BLK], s[:, BLK:])
 
     def first_pass(p, carry):
         keys = tile(0, entries_ref[step, 2 * p], entries_ref[step, 2 * p + 1])
-        for h in range(heads):
-            s = score(queries(h), keys)
-            r = slice(h * BLK, (h + 1) * BLK)
+        for g in range(groups):
+            s = score(queries(g), keys)
+            r = slice(g * tall, (g + 1) * tall)
             scores[p + 1, r, :] = s
             top[r, :] = jnp.maximum(top[r, :], jnp.maximum(s[:, :BLK], s[:, BLK:]))
         return carry
@@ -149,8 +153,8 @@
 
     def weigh(p, a, b, fresh):
         vals = tile(1, a, b)
-        for h in range(heads):
-            r = slice(h * BLK, (h + 1) * BLK)
+        for g in range(groups):
+            r = slice(g * tall, (g + 1) * tall)
             t = top[r, :]
             s = scores[p, r, :]
             w0 = jnp.exp2((s[:, :BLK] - t) * EXP_SCALE)
@@ -182,23 +186,24 @@
         out_ref[0, :, h * HEAD:(h + 1) * HEAD] = (acc[r, :] / total).astype(out_ref.dtype)
 
 
-def copy_kernel(*refs):
-    *sources, out_ref = refs
-    at = 0
-    for ref in sources:
-        piece = ref[...].reshape(BLK, -1)
-        width = piece.shape[1]
-        if out_ref.ndim == 3:
-            out_ref[0, :, at:at + width] = piece
-        else:
-            out_ref[:, at:at + width] = piece
-        at += width
-
-
-def pack_kernel(target_ref, query_ref, *out_refs):
-    width = out_refs[0].shape[1]
-    for n, out_ref in enumerate(out_refs):
-        out_ref[...] = query_ref[:, pl.ds(pl.multiple_of(target_ref[n] * width, width), width)]
+def pack_kernel(target_ref, query_ref, *refs):
+    out_refs, (held, in_sems, out_sems) = refs[:GROUP], refs[GROUP:]
+    width = held.shape[2]
+
+    def fetch(n):
+        at = pl.multiple_of(target_ref[n] * width, width)
+        return pltpu.make_async_copy(query_ref.at[:, pl.ds(at, width)], held.at[n], in_sems.at[n])
+
+    def put(n):
+        return pltpu.make_async_copy(held.at[n], out_refs[n], out_sems.at[n])
+
+    for n in range(GROUP):
+        fetch(n).start()
+    for n in range(GROUP):
+        fetch(n).wait()
+        put(n).start()
+    for n in range(GROUP):
+        put(n).wait()
 
 
 def pack(targets, queries):
@@ -207,29 +212,57 @@
     return pl.pallas_call(
         pack_kernel,
         out_shape=[jax.ShapeDtypeStruct((BLK, width), queries.dtype)] * GROUP,
-        grid_spec=pltpu.PrefetchScalarGridSpec(
-            num_scalar_prefetch=1,
-            grid=(PACK_STEPS,),
-            in_specs=[pl.BlockSpec((BLK // PACK_STEPS, total), lambda i, *_: (i, 0))],
-            out_specs=[pl.BlockSpec((BLK // PACK_STEPS, width), lambda i, *_: (i, 0))] * GROUP,
-        ),
+        in_specs=[pl.BlockSpec(memory_space=pltpu.SMEM), pl.BlockSpec(memory_space=pl.ANY)],
+        out_specs=[pl.BlockSpec(memory_space=pl.ANY)] * GROUP,
+        scratch_shapes=[
+            pltpu.VMEM((GROUP, BLK, width), queries.dtype),
+            pltpu.SemaphoreType.DMA((GROUP,)),
+            pltpu.SemaphoreType.DMA((GROUP,)),
+        ],
         cost_estimate=pl.CostEstimate(flops=0, bytes_accessed=4 * BLK * total, transcendentals=0),
         name="pack",
     )(targets, queries)
 
 
-def unpack(parts):
-    width = parts[0].shape[2]
-    total = GROUP * CHUNKS * width
+def unpack_kernel(chunk, part_ref, *refs):
+    out_ref, held, in_sems, out_sems = refs[-4:]
+    width = held.shape[2]
+
+    def fetch(n):
+        return pltpu.make_async_copy(part_ref.at[n], held.at[n], in_sems.at[n])
+
+    def put(n):
+        at = (n * CHUNKS + chunk) * width
+        return pltpu.make_async_copy(held.at[n], out_ref.at[:, pl.ds(at, width)], out_sems.at[n])
+
+    for n in range(GROUP):
+        fetch(n).start()
+    for n in range(GROUP):
+        fetch(n).wait()
+        put(n).start()
+    for n in range(GROUP):
+        put(n).wait()
+
+
+def unpack(part, chunk, whole):
+    width = part.shape[2]
+    held = () if whole is None else (whole,)
     return pl.pallas_call(
-        copy_kernel,
-        out_shape=jax.ShapeDtypeStruct((BLK, total), parts[0].dtype),
-        grid=(GROUP,),
-        in_specs=[pl.BlockSpec((1, BLK, width), lambda i: (i, 0, 0))] * CHUNKS,
-        out_specs=pl.BlockSpec((BLK, CHUNKS * width), lambda i: (0, i)),
-        cost_estimate=pl.CostEstimate(flops=0, bytes_accessed=4 * BLK * total, transcendentals=0),
+        functools.partial(unpack_kernel, chunk),
+        out_shape=jax.ShapeDtypeStruct((BLK, GROUP * CHUNKS * width), part.dtype),
+        in_specs=[pl.BlockSpec(memory_space=pl.ANY)] * (1 + len(held)),
+        out_specs=pl.BlockSpec(memory_space=pl.ANY),
+        scratch_shapes=[
+            pltpu.VMEM((GROUP, BLK, width), part.dtype),
+            pltpu.SemaphoreType.DMA((GROUP,)),
+            pltpu.SemaphoreType.DMA((GROUP,)),
+        ],
+        input_output_aliases={1: 0} if held else {},
+        cost_estimate=pl.CostEstimate(
+            flops=0, bytes_accessed=4 * BLK * GROUP * width, transcendentals=0
+        ),
         name="unpack",
-    )(*parts)
+    )(part, *held)
 
 
 def attend(filled, entries, order, before, own, fast, rest, query, chunk):
@@ -277,15 +310,17 @@
         return lax.all_to_all(a, inside, split_axis=0, concat_axis=0, tiled=True)
 
     sent = jnp.concatenate([tiles(keys), tiles(values)], axis=0)
-    everyone = lax.all_to_all(sent.reshape(-1, pieces, HEAD), across + inside, split_axis=0, concat_axis=0, tiled=True)
+    everyone = lax.all_to_all(
+        sent.reshape(-1, pieces, HEAD), across + inside, split_axis=0, concat_axis=0, tiled=True
+    )
     core = lax.axis_index("c")
     ring = lax.axis_index("t")
     ring_size = lax.axis_size("t")
     core_size = lax.axis_size("c")
-    moves = [(dc, dt) for dc in range(core_size) for dt in range(ring_size)]
+    moves = [(dc, dt) for dt in range(ring_size) for dc in range(core_size)]
 
     def place(r):
-        return (core ^ (r // ring_size)) * ring_size + (ring - r % ring_size) % ring_size
+        return (ring - r % ring_size) % ring_size * core_size + (core ^ (r // ring_size))
 
     def move(piece, dc, dt):
         pairs = [
@@ -304,20 +339,24 @@
     mine = []
     for n, (dc, dt) in enumerate(moves):
         piece = packed[n]
+        hop = 1 - 2 * dc
         if dt == 2:
-            hop = 1 - 2 * dc
             piece = move(piece, 0, hop)
-            piece = move(piece, dc, hop)
         elif dc or dt:
             piece = move(piece, dc, dt)
+        if dt == 2:
+            piece = move(piece, dc, hop)
         mine.append(piece)
 
     slot_block, most, entries, filled = tree_tables(lengths, parents, headers, group_id, groups, order, place)
     blocks = (-1, 2, BLK, HEAD)
     own = []
-    for n, (dc, dt) in enumerate(moves):
-        piece = lax.dynamic_index_in_dim(sent, targets[n], 1, keepdims=False)
-        own.append(move(piece, dc, dt) if dc or dt else piece)
+    kept = lax.dynamic_slice_in_dim(sent, core * ring_size, ring_size, 1)
+    given = lax.dynamic_slice_in_dim(sent, (1 - core) * ring_size, ring_size, 1)
+    both = jnp.stack([kept, move(given, 1, 0)])
+    for dt in range(ring_size):
+        piece = lax.dynamic_index_in_dim(both, (ring + dt) % ring_size, 2, keepdims=False)
+        own.append(move(piece, 0, dt) if dt else piece)
     own = jnp.stack(own).reshape(blocks)
     before = lax.ppermute(own, across, [(j, j + 1) for j in range(groups - 1)])
 
@@ -334,13 +373,16 @@
         lambda: jnp.zeros((REST_SLOTS,) + own.shape[1:], own.dtype),
     )
 
-    parts = []
+    whole = None
     for chunk in range(CHUNKS):
-        parts.append(exchange(attend(filled, entries, order, before, own, fast, rest, mine, chunk)))
-    return unpack(parts)
+        part = exchange(attend(filled, entries, order, before, own, fast, rest, mine, chunk))
+        whole = unpack(part, chunk, whole)
+    return whole
 
 
 def solution(mesh):
     inner = Mesh(mesh.devices.reshape(4, 8, 2, 4), ("x", "z", "c", "t"))
     rows = P(("x", "z", "c", "t"), None)
-    return jax.shard_map(body, mesh=inner, in_specs=(rows, rows, rows, P(), P(), P()), out_specs=rows, check_vma=False)
+    return jax.shard_map(
+        body, mesh=inner, in_specs=(rows, rows, rows, P(), P(), P()), out_specs=rows, check_vma=False
+    )

time: 192 us -> 193 us (level)
  waiting for transfers between devices: 17.8 us -> 64 us
  blocking collectives: 31.1 us -> 0 us
  starting transfers between devices: 54.7 us -> 48.9 us
  local copies, waits for them, and re-layouts: 11.4 us -> 6.64 us
  Pallas kernels: 67.2 us -> 64.4 us
    all_to_all x1 -> x0, blocking collectives: 31.1 us -> none  [exchange(): return lax.all_to_all(a, inside, split_axis=0, concat_axis=0, tiled=True)]
    ppermute x16 -> x13, waiting for transfers between devices: 12.3 us -> 40.4 us  [move(): return lax.ppermute(piece, inside, pairs)]
    all_to_all x1 -> x2, waiting for transfers between devices: 0.01 us -> 23.6 us  [exchange(): return lax.all_to_all(a, inside, split_axis=0, concat_axis=0, tiled=True)]
    ppermute x16 -> x13, starting transfers between devices: 21.5 us -> 14.9 us  [move(): return lax.ppermute(piece, inside, pairs)]
    ppermute x1, waiting for transfers between devices: 5.5 us -> 0.01 us  [body(): before = lax.ppermute(own, across, [(j, j + 1) for j in range(groups - 1)])]
    concatenate x1 -> x2, other arithmetic: 0.05 us -> 3.01 us  [body(): sent = jnp.concatenate([tiles(keys), tiles(values)], axis=0)]
    all_to_all x1 -> x2, starting transfers between devices: 5.31 us -> 7.89 us  [exchange(): return lax.all_to_all(a, inside, split_axis=0, concat_axis=0, tiled=True)]
    unnamed x33 -> x10, local copies, waits for them, and re-layouts: 3.33 us -> 1.37 us
  transfers between devices with their start and end apart: 20 -> 18, of which waited for: 6 -> 6; matrix products, arithmetic and copies ran while one was open for 8% -> 6% of each run, Pallas kernels for 17% -> 18%
where the time goes in v3:
time: 193 us
  Pallas kernels  64.4 us (33%)
  waiting for transfers between devices  64 us (33%)
  starting transfers between devices  48.9 us (25%)
  other arithmetic  7.42 us (4%)
  local copies, waits for them, and re-layouts  6.64 us (3%)
    pallas_call x2, Pallas kernels, attend(): pl.pallas_call(functools.partial(attend_kernel, chunk), out_shape=jax.Sha...  55.1 us
    ppermute x13, waiting for transfers between devices, move(): return lax.ppermute(piece, inside, pairs)  40.4 us
    all_to_all x2, waiting for transfers between devices, exchange(): return lax.all_to_all(a, inside, split_axis=0, concat_axis=0, tiled=True)  23.6 us
    ppermute x13, starting transfers between devices, move(): return lax.ppermute(piece, inside, pairs)  14.9 us
    all_to_all x1, starting transfers between devices, body(): lax.all_to_all(sent.reshape(-1, pieces, HEAD), across + inside, split_axi...  14.4 us
    all_to_all x1, starting transfers between devices, fetch(): lax.all_to_all(picked, across, split_axis=0, concat_axis=0, tiled=True)  8.65 us
    all_to_all x2, starting transfers between devices, exchange(): return lax.all_to_all(a, inside, split_axis=0, concat_axis=0, tiled=True)  7.89 us
    pallas_call x2, Pallas kernels, unpack(): pl.pallas_call(functools.partial(unpack_kernel, chunk), out_shape=jax.Sha...  4.79 us
  transfers between devices with their start and end apart: 18, of which 6 were waited for; matrix products, arithmetic and copies ran while one was open for 6% of the time, Pallas kernels for 18%

profile of v3, /device:TPU:3, one launch (start us, length us, event | category | flops | bytes accessed | tf_op | source)
XLA Modules:
  0.0 192.5 jit_solution(7625682405748216990)
XLA Ops:
  0.0 1.1 fusion.5
  1.1 0.8 collective-permute-start
  1.9 1.9 pad_maximum_fusion
  3.8 14.4 %all-to-all-start.1 = ((bf16[256,8,128]{2,1,0:T(8,128)(2,1)}), bf16[256,8,128]{2,1,0:T(8,128)(2,1)S(1)}, u32[]{:S(2)}, u32[]{:S(2)}) async-start(bf16[256,8,128]{2,1,0:T(8,128)(2,1)} %bitcast.27), calls=%async_computation.1 | async-start | bytes 1048576 | tf_op jit(solution)/shard_map/all_to_all | solution.py:313
  18.3 0.7 stack.97.target_ref
  18.9 4.4 %pack.1 = (bf16[128,2048]{1,0:T(8,128)(2,1)}, bf16[128,2048]{1,0:T(8,128)(2,1)}, bf16[128,2048]{1,0:T(8,128)(2,1)}, bf16[128,2048]{1,0:T(8,128)(2,1)}, bf16[128,...) custom-call(s32[8]{0:T(128)} %stack.97.target_ref, ...), custom_call_target="tpu_custom_call" | custom-call | bytes 8388608 | tf_op jit(solution)/shard_map/pack/pallas_call | solution.py:212
  23.4 0.5 collective-permute-start.5
  23.9 1.2 collective-permute-start.6
  25.1 0.1 select_reduce_fusion.4
  25.2 0.2 select_reduce_fusion.3
  25.4 0.2 select_reduce_fusion.2
  25.6 0.1 select_reduce_fusion.5
  25.8 0.2 convert_reduce_fusion
  26.2 0.3 and_reduce_fusion
  26.5 0.1 fusion.19
  26.6 0.6 select_reduce_fusion
  27.3 0.7 select_reduce_fusion.1
  28.1 0.2 select_reduce_fusion.14
  28.3 0.2 select_reduce_fusion.12
  28.5 0.2 select_reduce_fusion.10
  28.8 1.3 collective-permute-start.1
  30.1 1.5 collective-permute-start.2
  31.5 1.9 collective-permute-start.3
  33.4 0.6 reduce_max.9
  34.7 0.2 select_reduce_fusion.8
  34.9 10.1 %collective-permute-done.1 = bf16[2,32,8,128]{3,2,1,0:T(8,128)(2,1)S(1)} collective-permute-done((bf16[2,32,8,128]{3,2,1,0:T(8,128)(2,1)S(1)}, bf16[2,32,8,128]{3,2,1,0:T(8,128)(2,1)S(1)}, u32[]{:S(2)}, u32[]{:S(2)}) %collective-permute-start.1) | collective-permute-done | bytes 131104 | tf_op jit(solution)/shard_map/ppermute | solution.py:331
  45.0 0.2 collective-permute-start.7
  45.2 3.1 %collective-permute-done.2 = bf16[2,32,8,128]{3,2,1,0:T(8,128)(2,1)S(1)} collective-permute-done((bf16[2,32,8,128]{3,2,1,0:T(8,128)(2,1)S(1)}, bf16[2,32,8,128]{3,2,1,0:T(8,128)(2,1)S(1)}, u32[]{:S(2)}, u32[]{:S(2)}) %collective-permute-start.2) | collective-permute-done | bytes 131104 | tf_op jit(solution)/shard_map/ppermute | solution.py:331
  48.3 2.7 %collective-permute-start.10 = (bf16[128,2048]{1,0:T(8,128)(2,1)}, bf16[128,2048]{1,0:T(8,128)(2,1)}, u32[]{:S(2)}, u32[]{:S(2)}) collective-permute-start(bf16[128,2048]{1,0:T(8,128)(2,1)} %get-tuple-element.27), channel_id=1, source_target_pairs={{0,3},{1,0},{2,1},{3,2},{4,7},{5,4},{6,5},{7,6},{8,11},{9,8},{10,9... | collective-permute-start | bytes 1572872 | tf_op jit(solution)/shard_map/ppermute | solution.py:331
  51.0 1.6 conditional.1
  51.0 1.6 broadcast.268
  52.6 1.6 gather_fusion.1
  54.2 8.7 %all-to-all-start.2 = ((bf16[32,8,8,128]{3,2,1,0:T(8,128)(2,1)}), bf16[32,8,8,128]{3,2,1,0:T(8,128)(2,1)}, u32[]{:S(2)}, u32[]{:S(2)}) async-start(bf16[32,8,8,128]{3,2,1,0:T(8,128)(2,1)} %bitcast.28), calls=%async_computation.2 | async-start | bytes 1048576 | tf_op jit(solution)/shard_map/all_to_all | solution.py:366
  63.1 1.6 collective-permute-start.13
  64.7 3.1 %collective-permute-start.4 = (bf16[8,2,128,128]{3,2,1,0:T(8,128)(2,1)S(1)}, bf16[8,2,128,128]{3,2,1,0:T(8,128)(2,1)}, u32[]{:S(2)}, u32[]{:S(2)}) collective-permute-start(bf16[8,2,128,128]{3,2,1,0:T(8,128)(2,1)S(1)} %bitcast.45), channel_id=1, source_target_pairs={{0,8},{8,16},{16,24},{24,32},{32,40},{40,48},{48,56},{56,64},{64,7... | collective-permute-start | bytes 1572872 | tf_op jit(solution)/shard_map/ppermute | solution.py:361
  67.8 4.5 %collective-permute-done.8 = bf16[128,2048]{1,0:T(8,128)(2,1)} collective-permute-done((bf16[128,2048]{1,0:T(8,128)(2,1)}, bf16[128,2048]{1,0:T(8,128)(2,1)}, u32[]{:S(2)}, u32[]{:S(2)}) %collective-permute-start.8) | collective-permute-done | bytes 524320 | tf_op jit(solution)/shard_map/ppermute | solution.py:331
  72.3 3.2 %collective-permute-start.11 = (bf16[128,2048]{1,0:T(8,128)(2,1)}, bf16[128,2048]{1,0:T(8,128)(2,1)}, u32[]{:S(2)}, u32[]{:S(2)}) collective-permute-start(bf16[128,2048]{1,0:T(8,128)(2,1)} %collective-permute-done.10), channel_id=1, source_target_pairs={{0,7},{1,4},{2,5},{3,6},{4,3},{5,0},{6,1},{7,2},{8,15},{9,12},{10,... | collective-permute-start | bytes 1572872 | tf_op jit(solution)/shard_map/ppermute | solution.py:331
  75.6 1.1 copy.17
  76.8 14.1 %collective-permute-done.13.refs_11_ = bf16[128,2048]{1,0:T(8,128)(2,1)} collective-permute-done((bf16[128,2048]{1,0:T(8,128)(2,1)}, bf16[128,2048]{1,0:T(8,128)(2,1)}, u32[]{:S(2)}, u32[]{:S(2)}) %collective-permute-start.13) | collective-permute-done | bytes 524320 | tf_op jit(solution)/shard_map/ppermute | solution.py:331
  90.9 8.6 %collective-permute-done.11.refs_9_ = bf16[128,2048]{1,0:T(8,128)(2,1)} collective-permute-done((bf16[128,2048]{1,0:T(8,128)(2,1)}, bf16[128,2048]{1,0:T(8,128)(2,1)}, u32[]{:S(2)}, u32[]{:S(2)}) %collective-permute-start.11) | collective-permute-done | bytes 524320 | tf_op jit(solution)/shard_map/ppermute | solution.py:331
  99.5 27.6 %attend.3 = bf16[8,128,1024]{2,1,0:T(8,128)(2,1)} custom-call(s32[8]{0:T(128)S(1)} %get-tuple-element.40.filled_ref, s32[8,12]{1,0:T(8,128)S(1)} %fusion.30.entries_ref, s32[8]{0:T(128)S(1)} %stack.82.order_ref, bf16[8,2,128,128]{3,2,1,0:T(8,128)(2,1)} %collective-permute-done.4.refs_0_, bf16[8,2,128,128]{3,2,1,0:T(8,128)(2,1)S(1)} %bitcast.46, ...), custom_call_target="tpu_custom_call" | custom-call | flops 4294967296 | bytes 6291456 | tf_op jit(solution)/shard_map/attend/pallas_call | solution.py:272
  127.1 4.3 %all-to-all-start.4 = ((bf16[8,128,1024]{2,1,0:T(8,128)(2,1)}), bf16[8,128,1024]{2,1,0:T(8,128)(2,1)}, u32[]{:S(2)}, u32[]{:S(2)}) async-start(bf16[8,128,1024]{2,1,0:T(8,128)(2,1)} %attend.3), calls=%async_computation.4 | async-start | bytes 4194304 | tf_op jit(solution)/shard_map/all_to_all | solution.py:310
  131.4 27.6 %attend.2 = bf16[8,128,1024]{2,1,0:T(8,128)(2,1)} custom-call(s32[8]{0:T(128)S(1)} %get-tuple-element.40.filled_ref, s32[8,12]{1,0:T(8,128)S(1)} %fusion.30.entries_ref, s32[8]{0:T(128)S(1)} %stack.82.order_ref, bf16[8,2,128,128]{3,2,1,0:T(8,128)(2,1)} %collective-permute-done.4.refs_0_, bf16[8,2,128,128]{3,2,1,0:T(8,128)(2,1)S(1)} %bitcast.47, ...), custom_call_target="tpu_custom_call" | custom-call | flops 4294967296 | bytes 6291456 | tf_op jit(solution)/shard_map/attend/pallas_call | solution.py:272
  159.0 3.6 %all-to-all-start.3 = ((bf16[8,128,1024]{2,1,0:T(8,128)(2,1)}), bf16[8,128,1024]{2,1,0:T(8,128)(2,1)S(1)}, u32[]{:S(2)}, u32[]{:S(2)}) async-start(bf16[8,128,1024]{2,1,0:T(8,128)(2,1)} %attend.2), calls=%async_computation.3 | async-start | bytes 4194304 | tf_op jit(solution)/shard_map/all_to_all | solution.py:310
  162.6 2.4 %unpack.2.refs_0_ = bf16[128,16384]{1,0:T(8,128)(2,1)} custom-call(bf16[8,128,1024]{2,1,0:T(8,128)(2,1)} %all-to-all-done.4.part_ref), custom_call_target="tpu_custom_call" | custom-call | bytes 4194304 | tf_op jit(solution)/shard_map/unpack/pallas_call | solution.py:250
  165.0 23.6 %all-to-all-done.3.part_ref = bf16[8,128,1024]{2,1,0:T(8,128)(2,1)S(1)} async-done(((bf16[8,128,1024]{2,1,0:T(8,128)(2,1)}), bf16[8,128,1024]{2,1,0:T(8,128)(2,1)S(1)}, u32[]{:S(2)}, u32[]{:S(2)}) %all-to-all-start.3) | async-done | bytes 2097184 | tf_op jit(solution)/shard_map/all_to_all | solution.py:310
  188.6 1.3 copy-done.1
  190.0 2.4 %unpack.3 = bf16[128,16384]{1,0:T(8,128)(2,1)} custom-call(bf16[8,128,1024]{2,1,0:T(8,128)(2,1)} %copy-done.1, bf16[128,16384]{1,0:T(8,128)(2,1)} %unpack.2.refs_0_), custom_call_target="tpu_custom_call", output_to_operand_aliasing={{}: (1, {})} | custom-call | bytes 4194304 | tf_op jit(solution)/shard_map/unpack/pallas_call | solution.py:250
  (46 shorter events, 0.9 us)
Async XLA Ops:
  1.1 27.5 %collective-permute-start = (bf16[32,4,8,128]{3,2,1,0:T(8,128)(2,1)S(1)}, bf16[32,4,8,128]{3,2,1,0:T(8,128)(2,1)S(1)}, u32[]{:S(2)}, u32[]{:S(2)}) collective-permute-start(bf16[32,4,8,128]{3,2,1,0:T(8,128)(2,1)S(1)} %get-tuple-element.48), channel_id=1, source_target_pairs={{0,4},{1,5},{2,6},{3,7},{4,0},{5,1},{6,2},{7,3},{8,12},{9,13},{10,... | collective-permute-start | bytes 786440 | tf_op jit(solution)/shard_map/ppermute | solution.py:331
  3.8 47.2 %all-to-all-start.1 = ((bf16[256,8,128]{2,1,0:T(8,128)(2,1)}), bf16[256,8,128]{2,1,0:T(8,128)(2,1)S(1)}, u32[]{:S(2)}, u32[]{:S(2)}) async-start(bf16[256,8,128]{2,1,0:T(8,128)(2,1)} %bitcast.27), calls=%async_computation.1 | async-start | bytes 1048576 | tf_op jit(solution)/shard_map/all_to_all | solution.py:313
  18.9 6.1 %copy-start.4 = (s32[48]{0:T(128)S(1)}, s32[48]{0:T(128)}, u32[]{:S(2)}) copy-start(s32[48]{0:T(128)} %param.12) | copy-start | bytes 580
  18.9 6.6 %copy-start.3 = (s32[48]{0:T(128)S(1)}, s32[48]{0:T(128)}, u32[]{:S(2)}) copy-start(s32[48]{0:T(128)} %param.11) | copy-start | bytes 580
  18.9 7.1 %copy-start.2 = (s32[48]{0:T(128)S(1)}, s32[48]{0:T(128)}, u32[]{:S(2)}) copy-start(s32[48]{0:T(128)} %param.13) | copy-start | bytes 580
  23.4 39.6 %collective-permute-start.5 = (bf16[128,2048]{1,0:T(8,128)(2,1)}, bf16[128,2048]{1,0:T(8,128)(2,1)S(1)}, u32[]{:S(2)}, u32[]{:S(2)}) collective-permute-start(bf16[128,2048]{1,0:T(8,128)(2,1)} %get-tuple-element.23), channel_id=1, source_target_pairs={{0,4},{1,5},{2,6},{3,7},{4,0},{5,1},{6,2},{7,3},{8,12},{9,13},{10,... | collective-permute-start | bytes 1572872 | tf_op jit(solution)/shard_map/ppermute | solution.py:331
  23.9 39.2 %collective-permute-start.6 = (bf16[128,2048]{1,0:T(8,128)(2,1)}, bf16[128,2048]{1,0:T(8,128)(2,1)S(1)}, u32[]{:S(2)}, u32[]{:S(2)}) collective-permute-start(bf16[128,2048]{1,0:T(8,128)(2,1)} %get-tuple-element.24), channel_id=1, source_target_pairs={{0,1},{1,2},{2,3},{3,0},{4,5},{5,6},{6,7},{7,4},{8,9},{9,10},{10,1... | collective-permute-start | bytes 1572872 | tf_op jit(solution)/shard_map/ppermute | solution.py:331
  28.8 16.2 %collective-permute-start.1 = (bf16[2,32,8,128]{3,2,1,0:T(8,128)(2,1)S(1)}, bf16[2,32,8,128]{3,2,1,0:T(8,128)(2,1)S(1)}, u32[]{:S(2)}, u32[]{:S(2)}) collective-permute-start(bf16[2,32,8,128]{3,2,1,0:T(8,128)(2,1)S(1)} %get-tuple-element.45), channel_id=1, source_target_pairs={{0,1},{1,2},{2,3},{3,0},{4,5},{5,6},{6,7},{7,4},{8,9},{9,10},{10,1... | collective-permute-start | bytes 393224 | tf_op jit(solution)/shard_map/ppermute | solution.py:331
  30.1 18.3 %collective-permute-start.2 = (bf16[2,32,8,128]{3,2,1,0:T(8,128)(2,1)S(1)}, bf16[2,32,8,128]{3,2,1,0:T(8,128)(2,1)S(1)}, u32[]{:S(2)}, u32[]{:S(2)}) collective-permute-start(bf16[2,32,8,128]{3,2,1,0:T(8,128)(2,1)S(1)} %get-tuple-element.46), channel_id=1, source_target_pairs={{0,2},{1,3},{2,0},{3,1},{4,6},{5,7},{6,4},{7,5},{8,10},{9,11},{10,... | collective-permute-start | bytes 393224 | tf_op jit(solution)/shard_map/ppermute | solution.py:331
  31.5 16.8 %collective-permute-start.3 = (bf16[2,32,8,128]{3,2,1,0:T(8,128)(2,1)S(1)}, bf16[2,32,8,128]{3,2,1,0:T(8,128)(2,1)S(1)}, u32[]{:S(2)}, u32[]{:S(2)}) collective-permute-start(bf16[2,32,8,128]{3,2,1,0:T(8,128)(2,1)S(1)} %get-tuple-element.47), channel_id=1, source_target_pairs={{0,3},{1,0},{2,1},{3,2},{4,7},{5,4},{6,5},{7,6},{8,11},{9,8},{10,9... | collective-permute-start | bytes 393224 | tf_op jit(solution)/shard_map/ppermute | solution.py:331
  45.0 19.7 %collective-permute-start.7 = (bf16[128,2048]{1,0:T(8,128)(2,1)}, bf16[128,2048]{1,0:T(8,128)(2,1)S(1)}, u32[]{:S(2)}, u32[]{:S(2)}) collective-permute-start(bf16[128,2048]{1,0:T(8,128)(2,1)} %get-tuple-element.25), channel_id=1, source_target_pairs={{0,5},{1,6},{2,7},{3,4},{4,1},{5,2},{6,3},{7,0},{8,13},{9,14},{10,... | collective-permute-start | bytes 1572872 | tf_op jit(solution)/shard_map/ppermute | solution.py:331
  48.3 23.9 %collective-permute-start.8 = (bf16[128,2048]{1,0:T(8,128)(2,1)}, bf16[128,2048]{1,0:T(8,128)(2,1)}, u32[]{:S(2)}, u32[]{:S(2)}) collective-permute-start(bf16[128,2048]{1,0:T(8,128)(2,1)} %get-tuple-element.26), channel_id=1, source_target_pairs={{0,1},{1,2},{2,3},{3,0},{4,5},{5,6},{6,7},{7,4},{8,9},{9,10},{10,1... | collective-permute-start | bytes 1572872 | tf_op jit(solution)/shard_map/ppermute | solution.py:331
  48.3 23.9 %collective-permute-start.10 = (bf16[128,2048]{1,0:T(8,128)(2,1)}, bf16[128,2048]{1,0:T(8,128)(2,1)}, u32[]{:S(2)}, u32[]{:S(2)}) collective-permute-start(bf16[128,2048]{1,0:T(8,128)(2,1)} %get-tuple-element.27), channel_id=1, source_target_pairs={{0,3},{1,0},{2,1},{3,2},{4,7},{5,4},{6,5},{7,6},{8,11},{9,8},{10,9... | collective-permute-start | bytes 1572872 | tf_op jit(solution)/shard_map/ppermute | solution.py:331
  54.2 45.3 %copy-start = (bf16[128,2048]{1,0:T(8,128)(2,1)S(1)}, bf16[128,2048]{1,0:T(8,128)(2,1)}, u32[]{:S(2)}) copy-start(bf16[128,2048]{1,0:T(8,128)(2,1)} %get-tuple-element.22.refs_4_) | copy-start | bytes 1572868
  54.2 21.4 %all-to-all-start.2 = ((bf16[32,8,8,128]{3,2,1,0:T(8,128)(2,1)}), bf16[32,8,8,128]{3,2,1,0:T(8,128)(2,1)}, u32[]{:S(2)}, u32[]{:S(2)}) async-start(bf16[32,8,8,128]{3,2,1,0:T(8,128)(2,1)} %bitcast.28), calls=%async_computation.2 | async-start | bytes 1048576 | tf_op jit(solution)/shard_map/all_to_all | solution.py:366
  63.0 13.8 %collective-permute-start.12 = (bf16[128,2048]{1,0:T(8,128)(2,1)}, bf16[128,2048]{1,0:T(8,128)(2,1)}, u32[]{:S(2)}, u32[]{:S(2)}) collective-permute-start(bf16[128,2048]{1,0:T(8,128)(2,1)} %get-tuple-element.28), channel_id=1, source_target_pairs={{0,3},{1,0},{2,1},{3,2},{4,7},{5,4},{6,5},{7,6},{8,11},{9,8},{10,9... | collective-permute-start | bytes 1572872 | tf_op jit(solution)/shard_map/ppermute | solution.py:331
  63.1 27.8 %collective-permute-start.13 = (bf16[128,2048]{1,0:T(8,128)(2,1)}, bf16[128,2048]{1,0:T(8,128)(2,1)}, u32[]{:S(2)}, u32[]{:S(2)}) collective-permute-start(bf16[128,2048]{1,0:T(8,128)(2,1)} %get-tuple-element.29), channel_id=1, source_target_pairs={{0,7},{1,4},{2,5},{3,6},{4,3},{5,0},{6,1},{7,2},{8,15},{9,12},{10,... | collective-permute-start | bytes 1572872 | tf_op jit(solution)/shard_map/ppermute | solution.py:331
  64.7 26.2 %collective-permute-start.4 = (bf16[8,2,128,128]{3,2,1,0:T(8,128)(2,1)S(1)}, bf16[8,2,128,128]{3,2,1,0:T(8,128)(2,1)}, u32[]{:S(2)}, u32[]{:S(2)}) collective-permute-start(bf16[8,2,128,128]{3,2,1,0:T(8,128)(2,1)S(1)} %bitcast.45), channel_id=1, source_target_pairs={{0,8},{8,16},{16,24},{24,32},{32,40},{40,48},{48,56},{56,64},{64,7... | collective-permute-start | bytes 1572872 | tf_op jit(solution)/shard_map/ppermute | solution.py:361
  72.3 18.6 %collective-permute-start.9 = (bf16[128,2048]{1,0:T(8,128)(2,1)}, bf16[128,2048]{1,0:T(8,128)(2,1)}, u32[]{:S(2)}, u32[]{:S(2)}) collective-permute-start(bf16[128,2048]{1,0:T(8,128)(2,1)} %collective-permute-done.8), channel_id=1, source_target_pairs={{0,1},{1,2},{2,3},{3,0},{4,5},{5,6},{6,7},{7,4},{8,9},{9,10},{10,1... | collective-permute-start | bytes 1572872 | tf_op jit(solution)/shard_map/ppermute | solution.py:331
  72.3 27.2 %collective-permute-start.11 = (bf16[128,2048]{1,0:T(8,128)(2,1)}, bf16[128,2048]{1,0:T(8,128)(2,1)}, u32[]{:S(2)}, u32[]{:S(2)}) collective-permute-start(bf16[128,2048]{1,0:T(8,128)(2,1)} %collective-permute-done.10), channel_id=1, source_target_pairs={{0,7},{1,4},{2,5},{3,6},{4,3},{5,0},{6,1},{7,2},{8,15},{9,12},{10,... | collective-permute-start | bytes 1572872 | tf_op jit(solution)/shard_map/ppermute | solution.py:331
  127.1 31.9 %all-to-all-start.4 = ((bf16[8,128,1024]{2,1,0:T(8,128)(2,1)}), bf16[8,128,1024]{2,1,0:T(8,128)(2,1)}, u32[]{:S(2)}, u32[]{:S(2)}) async-start(bf16[8,128,1024]{2,1,0:T(8,128)(2,1)} %attend.3), calls=%async_computation.4 | async-start | bytes 4194304 | tf_op jit(solution)/shard_map/all_to_all | solution.py:310
  159.0 29.6 %all-to-all-start.3 = ((bf16[8,128,1024]{2,1,0:T(8,128)(2,1)}), bf16[8,128,1024]{2,1,0:T(8,128)(2,1)S(1)}, u32[]{:S(2)}, u32[]{:S(2)}) async-start(bf16[8,128,1024]{2,1,0:T(8,128)(2,1)} %attend.2), calls=%async_computation.3 | async-start | bytes 4194304 | tf_op jit(solution)/shard_map/all_to_all | solution.py:310
  188.6 1.4 copy-start.1

commit v4 on v3

--- a/solution.py
+++ b/solution.py
@@ -20,7 +20,7 @@
 FAST_SLOTS = 8
 REST_SLOTS = SLOTS - FAST_SLOTS
 CHUNKS = 2
-STACK = 8
+STACK = 1
 LIST = WINDOW + (DEPTH - 1) * HDR
 NEG = -1e30
 VMEM_LIMIT = 48 * 1024 * 1024
@@ -309,10 +309,6 @@
     def exchange(a):
         return lax.all_to_all(a, inside, split_axis=0, concat_axis=0, tiled=True)
 
-    sent = jnp.concatenate([tiles(keys), tiles(values)], axis=0)
-    everyone = lax.all_to_all(
-        sent.reshape(-1, pieces, HEAD), across + inside, split_axis=0, concat_axis=0, tiled=True
-    )
     core = lax.axis_index("c")
     ring = lax.axis_index("t")
     ring_size = lax.axis_size("t")
@@ -335,6 +331,31 @@
 
     targets = indices(1)
     order = indices(-1)
+    blocks = (-1, 2, BLK, HEAD)
+
+    def split(pieces_of):
+        kept = lax.dynamic_slice_in_dim(pieces_of, core * ring_size, ring_size, 1)
+        given = lax.dynamic_slice_in_dim(pieces_of, (1 - core) * ring_size, ring_size, 1)
+        taken = move(given, 1, 0)
+        both = jnp.stack([kept, taken])
+        got = []
+        for dt in range(ring_size):
+            piece = lax.dynamic_index_in_dim(both, (ring + dt) % ring_size, 2, keepdims=False)
+            if dt:
+                piece = move(piece, 0, dt)
+            got.append(piece)
+        return jnp.concatenate(got, axis=0)
+
+    sent = jnp.concatenate([tiles(keys), tiles(values)], axis=0)
+    shifted = lax.ppermute(sent, across, [(j, j + 1) for j in range(groups - 1)])
+    near = split(sent)
+    own = near.reshape(blocks)
+    everyone = lax.all_to_all(
+        jnp.transpose(near, (1, 0, 2, 3)), across, split_axis=0, concat_axis=0, tiled=True
+    )
+    everyone = everyone.reshape(-1, pieces, HEAD)
+    before = split(shifted).reshape(blocks)
+
     packed = pack(targets, queries)
     mine = []
     for n, (dc, dt) in enumerate(moves):
@@ -349,19 +370,10 @@
         mine.append(piece)
 
     slot_block, most, entries, filled = tree_tables(lengths, parents, headers, group_id, groups, order, place)
-    blocks = (-1, 2, BLK, HEAD)
-    own = []
-    kept = lax.dynamic_slice_in_dim(sent, core * ring_size, ring_size, 1)
-    given = lax.dynamic_slice_in_dim(sent, (1 - core) * ring_size, ring_size, 1)
-    both = jnp.stack([kept, move(given, 1, 0)])
-    for dt in range(ring_size):
-        piece = lax.dynamic_index_in_dim(both, (ring + dt) % ring_size, 2, keepdims=False)
-        own.append(move(piece, 0, dt) if dt else piece)
-    own = jnp.stack(own).reshape(blocks)
-    before = lax.ppermute(own, across, [(j, j + 1) for j in range(groups - 1)])
 
     def fetch(first, count):
         wanted = slot_block[:, first:first + count].reshape(-1)
+        wanted = wanted // GROUP * GROUP + place(wanted % GROUP)
         picked = jnp.take(everyone, wanted, axis=0, mode="clip").reshape(groups, count, pieces, HEAD)
         got = lax.all_to_all(picked, across, split_axis=0, concat_axis=0, tiled=True)
         return jnp.transpose(got, (1, 0, 2, 3)).reshape(blocks)

time: 193 us -> 205 us (1.062)
  starting transfers between devices: 48.9 us -> 55.3 us
  local copies, waits for them, and re-layouts: 6.64 us -> 12.2 us
  waiting for transfers between devices: 64 us -> 60.7 us
  other arithmetic: 7.42 us -> 10.3 us
    ppermute x13 -> x17, waiting for transfers between devices: 40.4 us -> 31.7 us  [move(): return lax.ppermute(piece, inside, pairs)]
    ppermute x13 -> x17, starting transfers between devices: 14.9 us -> 22.8 us  [move(): return lax.ppermute(piece, inside, pairs)]
    all_to_all x1, waiting for transfers between devices: 0.01 us -> 5.16 us  [body(): lax.all_to_all(jnp.transpose(near, (1, 0, 2, 3)), across, split_axis=0, c...]
    all_to_all x1, starting transfers between devices: 14.4 us -> 10.2 us  [body(): lax.all_to_all(jnp.transpose(near, (1, 0, 2, 3)), across, split_axis=0, c...]
    unnamed x10 -> x28, local copies, waits for them, and re-layouts: 1.37 us -> 4.32 us
    concatenate x2, other arithmetic: 3.01 us -> 0.1 us  [body(): sent = jnp.concatenate([tiles(keys), tiles(values)], axis=0)]
  transfers between devices with their start and end apart: 18 -> 22, of which waited for: 6 -> 9; matrix products, arithmetic and copies ran while one was open for 6% -> 8% of each run, Pallas kernels for 18% -> 17%
where the time goes in v4:
time: 205 us; the launch traced here: 204 us
  Pallas kernels  64.2 us (31%)
  waiting for transfers between devices  60.7 us (30%)
  starting transfers between devices  55.3 us (27%)
  local copies, waits for them, and re-layouts  12.2 us (6%)
  other arithmetic  10.3 us (5%)
    pallas_call x2, Pallas kernels, attend(): pl.pallas_call(functools.partial(attend_kernel, chunk), out_shape=jax.Sha...  55 us
    ppermute x17, waiting for transfers between devices, move(): return lax.ppermute(piece, inside, pairs)  31.7 us
    all_to_all x2, waiting for transfers between devices, exchange(): return lax.all_to_all(a, inside, split_axis=0, concat_axis=0, tiled=True)  23.8 us
    ppermute x17, starting transfers between devices, move(): return lax.ppermute(piece, inside, pairs)  22.8 us
    all_to_all x1, starting transfers between devices, body(): lax.all_to_all(jnp.transpose(near, (1, 0, 2, 3)), across, split_axis=0, c...  10.2 us
    all_to_all x2, starting transfers between devices, exchange(): return lax.all_to_all(a, inside, split_axis=0, concat_axis=0, tiled=True)  9.92 us
    all_to_all x1, starting transfers between devices, fetch(): lax.all_to_all(picked, across, split_axis=0, concat_axis=0, tiled=True)  8.87 us
    all_to_all x1, waiting for transfers between devices, body(): lax.all_to_all(jnp.transpose(near, (1, 0, 2, 3)), across, split_axis=0, c...  5.16 us
  transfers between devices with their start and end apart: 22, of which 9 were waited for; matrix products, arithmetic and copies ran while one was open for 8% of the time, Pallas kernels for 17%

profile of v4, /device:TPU:3, one launch (start us, length us, event | category | flops | bytes accessed | tf_op | source)
XLA Modules:
  0.0 203.9 jit_solution(14839950094974412306)
XLA Ops:
  0.0 0.9 copy-done
  1.0 1.1 copy_bitcast_fusion
  2.1 0.8 collective-permute-start.5
  2.9 3.5 %collective-permute-start = (bf16[32,8,8,128]{3,2,0,1:T(8,128)(2,1)S(1)}, bf16[32,8,8,128]{3,2,0,1:T(8,128)(2,1)S(1)}, u32[]{:S(2)}, u32[]{:S(2)}) collective-permute-start(bf16[32,8,8,128]{3,2,0,1:T(8,128)(2,1)S(1)} %pad_maximum_fusion), channel_id=1, source_target_pairs={{0,8},{8,16},{16,24},{24,32},{32,40},{40,48},{48,56},{56,64},{64,7... | collective-permute-start | bytes 1572872 | tf_op jit(solution)/shard_map/ppermute | solution.py:350
  7.1 4.4 %pack.1 = (bf16[128,2048]{1,0:T(8,128)(2,1)}, bf16[128,2048]{1,0:T(8,128)(2,1)}, bf16[128,2048]{1,0:T(8,128)(2,1)}, bf16[128,2048]{1,0:T(8,128)(2,1)}, bf16[128,...) custom-call(s32[8]{0:T(128)} %stack.89.target_ref, ...), custom_call_target="tpu_custom_call" | custom-call | bytes 8388608 | tf_op jit(solution)/shard_map/pack/pallas_call | solution.py:212
  14.5 0.7 select_reduce_fusion.1
  15.4 2.8 %collective-permute-start.8 = (bf16[2,32,8,128]{3,2,0,1:T(8,128)(2,1)S(1)}, bf16[2,32,8,128]{3,2,0,1:T(8,128)(2,1)S(1)}, u32[]{:S(2)}, u32[]{:S(2)}) collective-permute-start(bf16[2,32,8,128]{3,2,0,1:T(8,128)(2,1)S(1)} %bitcast.86), channel_id=1, source_target_pairs={{0,3},{1,0},{2,1},{3,2},{4,7},{5,4},{6,5},{7,6},{8,11},{9,8},{10,9... | collective-permute-start | bytes 393224 | tf_op jit(solution)/shard_map/ppermute | solution.py:327
  18.5 0.7 collective-permute-start.6
  19.6 3.9 %collective-permute-done.8 = bf16[2,32,8,128]{3,2,0,1:T(8,128)(2,1)S(1)} collective-permute-done((bf16[2,32,8,128]{3,2,0,1:T(8,128)(2,1)S(1)}, bf16[2,32,8,128]{3,2,0,1:T(8,128)(2,1)S(1)}, u32[]{:S(2)}, u32[]{:S(2)}) %collective-permute-start.8) | collective-permute-done | bytes 131104 | tf_op jit(solution)/shard_map/ppermute | solution.py:327
  23.5 0.8 collective-permute-done.7
  24.3 1.1 collective-permute-start.12
  25.4 2.5 %collective-permute-done.6 = bf16[2,32,8,128]{3,2,0,1:T(8,128)(2,1)S(1)} collective-permute-done((bf16[2,32,8,128]{3,2,0,1:T(8,128)(2,1)S(1)}, bf16[2,32,8,128]{3,2,0,1:T(8,128)(2,1)S(1)}, u32[]{:S(2)}, u32[]{:S(2)}) %collective-permute-start.6) | collective-permute-done | bytes 131104 | tf_op jit(solution)/shard_map/ppermute | solution.py:327
  27.9 0.9 maximum_bitcast_fusion
  28.8 10.2 %all-to-all-start.1 = ((bf16[32,8,8,128]{3,2,1,0:T(8,128)(2,1)}), bf16[32,8,8,128]{3,2,1,0:T(8,128)(2,1)S(1)}, u32[]{:S(2)}, u32[]{:S(2)}) async-start(bf16[32,8,8,128]{3,2,1,0:T(8,128)(2,1)} %maximum_bitcast_fusion), calls=%async_computation.1 | async-start | bytes 1048576 | tf_op jit(solution)/shard_map/all_to_all | solution.py:353
  39.0 0.8 select_reduce_fusion.8
  40.4 0.8 constant_dynamic-slice_fusion
  41.3 2.5 %collective-permute-start.1 = (bf16[32,4,8,128]{3,2,0,1:T(8,128)(2,1)}, bf16[32,4,8,128]{3,2,0,1:T(8,128)(2,1)}, u32[]{:S(2)}, u32[]{:S(2)}) collective-permute-start(bf16[32,4,8,128]{3,2,0,1:T(8,128)(2,1)} %get-tuple-element.62), channel_id=1, source_target_pairs={{0,4},{1,5},{2,6},{3,7},{4,0},{5,1},{6,2},{7,3},{8,12},{9,13},{10,... | collective-permute-start | bytes 786440 | tf_op jit(solution)/shard_map/ppermute | solution.py:327
  43.7 0.7 reduce_max.9
  45.6 5.2 %all-to-all-done.1 = bf16[32,8,8,128]{3,2,1,0:T(8,128)(2,1)S(1)} async-done(((bf16[32,8,8,128]{3,2,1,0:T(8,128)(2,1)}), bf16[32,8,8,128]{3,2,1,0:T(8,128)(2,1)S(1)}, u32[]{:S(2)}, u32[]{:S(2)}) %all-to-all-start.1) | async-done | bytes 524320 | tf_op jit(solution)/shard_map/all_to_all | solution.py:353
  50.7 1.6 gather_fusion.1
  52.7 1.2 copy-done.4
  53.9 8.9 %all-to-all-start.2 = ((bf16[32,8,8,128]{3,2,1,0:T(8,128)(2,1)}), bf16[32,8,8,128]{3,2,1,0:T(8,128)(2,1)S(1)}, u32[]{:S(2)}, u32[]{:S(2)}) async-start(bf16[32,8,8,128]{3,2,1,0:T(8,128)(2,1)} %bitcast.74), calls=%async_computation.2 | async-start | bytes 1048576 | tf_op jit(solution)/shard_map/all_to_all | solution.py:378
  62.8 1.2 fusion.18
  64.0 2.9 %collective-permute-start.2 = (bf16[2,32,8,128]{3,2,1,0:T(8,128)(2,1)S(1)}, bf16[2,32,8,128]{3,2,1,0:T(8,128)(2,1)S(1)}, u32[]{:S(2)}, u32[]{:S(2)}) collective-permute-start(bf16[2,32,8,128]{3,2,1,0:T(8,128)(2,1)S(1)} %get-tuple-element.59), channel_id=1, source_target_pairs={{0,1},{1,2},{2,3},{3,0},{4,5},{5,6},{6,7},{7,4},{8,9},{9,10},{10,1... | collective-permute-start | bytes 393224 | tf_op jit(solution)/shard_map/ppermute | solution.py:327
  67.0 2.4 %collective-permute-start.4 = (bf16[2,32,8,128]{3,2,1,0:T(8,128)(2,1)S(1)}, bf16[2,32,8,128]{3,2,1,0:T(8,128)(2,1)S(1)}, u32[]{:S(2)}, u32[]{:S(2)}) collective-permute-start(bf16[2,32,8,128]{3,2,1,0:T(8,128)(2,1)S(1)} %get-tuple-element.61), channel_id=1, source_target_pairs={{0,3},{1,0},{2,1},{3,2},{4,7},{5,4},{6,5},{7,6},{8,11},{9,8},{10,9... | collective-permute-start | bytes 393224 | tf_op jit(solution)/shard_map/ppermute | solution.py:327
  69.4 0.7 broadcast_add_fusion.1
  70.1 2.0 collective-permute-start.11
  72.1 3.2 %collective-permute-start.16 = (bf16[128,2048]{1,0:T(8,128)(2,1)}, bf16[128,2048]{1,0:T(8,128)(2,1)}, u32[]{:S(2)}, u32[]{:S(2)}) collective-permute-start(bf16[128,2048]{1,0:T(8,128)(2,1)} %get-tuple-element.34), channel_id=1, source_target_pairs={{0,3},{1,0},{2,1},{3,2},{4,7},{5,4},{6,5},{7,6},{8,11},{9,8},{10,9... | collective-permute-start | bytes 1572872 | tf_op jit(solution)/shard_map/ppermute | solution.py:327
  75.3 2.1 %collective-permute-start.13 = (bf16[128,2048]{1,0:T(8,128)(2,1)}, bf16[128,2048]{1,0:T(8,128)(2,1)}, u32[]{:S(2)}, u32[]{:S(2)}) collective-permute-start(bf16[128,2048]{1,0:T(8,128)(2,1)} %collective-permute-done.12), channel_id=1, source_target_pairs={{0,1},{1,2},{2,3},{3,0},{4,5},{5,6},{6,7},{7,4},{8,9},{9,10},{10,1... | collective-permute-start | bytes 1572872 | tf_op jit(solution)/shard_map/ppermute | solution.py:327
  77.4 1.5 collective-permute-start.15
  78.9 0.7 broadcast_add_fusion
  79.5 0.8 fusion.39.entries_ref
  80.3 0.9 copy.47
  81.2 0.9 copy.45
  82.4 0.8 copy-done.3
  83.2 1.1 copy.50
  84.3 1.5 collective-permute-done.11.refs_7_
  85.8 1.5 collective-permute-done.16.refs_10_
  87.3 11.4 %collective-permute-done.17.refs_11_ = bf16[128,2048]{1,0:T(8,128)(2,1)} collective-permute-done((bf16[128,2048]{1,0:T(8,128)(2,1)}, bf16[128,2048]{1,0:T(8,128)(2,1)}, u32[]{:S(2)}, u32[]{:S(2)}) %collective-permute-start.17) | collective-permute-done | bytes 524320 | tf_op jit(solution)/shard_map/ppermute | solution.py:327
  98.8 10.1 %collective-permute-done.15.refs_9_ = bf16[128,2048]{1,0:T(8,128)(2,1)} collective-permute-done((bf16[128,2048]{1,0:T(8,128)(2,1)}, bf16[128,2048]{1,0:T(8,128)(2,1)}, u32[]{:S(2)}, u32[]{:S(2)}) %collective-permute-start.15) | collective-permute-done | bytes 524320 | tf_op jit(solution)/shard_map/ppermute | solution.py:327
  108.9 27.5 %attend.3 = bf16[8,128,1024]{2,1,0:T(8,128)(2,1)} custom-call(s32[8]{0:T(128)S(1)} %get-tuple-element.48.filled_ref, s32[8,12]{1,0:T(8,128)S(1)} %fusion.39.entries_ref, s32[8]{0:T(128)S(1)} %stack.76.order_ref, bf16[8,2,128,128]{3,2,1,0:T(8,128)(2,1)S(1)} %pad_maximum_fusion.1.refs_0_, bf16[8,2,128,128]{3,2,1,0:T(8,128)(2,1)S(1)} %pad_maximum_fusion.2.refs_1_, ...), custom_call_target="tpu_custom_call" | custom-call | flops 4294967296 | bytes 6291456 | tf_op jit(solution)/shard_map/attend/pallas_call | solution.py:272
  136.4 5.1 %all-to-all-start.4 = ((bf16[8,128,1024]{2,1,0:T(8,128)(2,1)}), bf16[8,128,1024]{2,1,0:T(8,128)(2,1)}, u32[]{:S(2)}, u32[]{:S(2)}) async-start(bf16[8,128,1024]{2,1,0:T(8,128)(2,1)} %attend.3), calls=%async_computation.4 | async-start | bytes 4194304 | tf_op jit(solution)/shard_map/all_to_all | solution.py:310
  141.5 27.5 %attend.2 = bf16[8,128,1024]{2,1,0:T(8,128)(2,1)} custom-call(s32[8]{0:T(128)S(1)} %get-tuple-element.48.filled_ref, s32[8,12]{1,0:T(8,128)S(1)} %fusion.39.entries_ref, s32[8]{0:T(128)S(1)} %stack.76.order_ref, bf16[8,2,128,128]{3,2,1,0:T(8,128)(2,1)S(1)} %pad_maximum_fusion.1.refs_0_, bf16[8,2,128,128]{3,2,1,0:T(8,128)(2,1)S(1)} %pad_maximum_fusion.2.refs_1_, ...), custom_call_target="tpu_custom_call" | custom-call | flops 4294967296 | bytes 6291456 | tf_op jit(solution)/shard_map/attend/pallas_call | solution.py:272
  169.0 4.8 %all-to-all-start.3 = ((bf16[8,128,1024]{2,1,0:T(8,128)(2,1)}), bf16[8,128,1024]{2,1,0:T(8,128)(2,1)S(1)}, u32[]{:S(2)}, u32[]{:S(2)}) async-start(bf16[8,128,1024]{2,1,0:T(8,128)(2,1)} %attend.2), calls=%async_computation.3 | async-start | bytes 4194304 | tf_op jit(solution)/shard_map/all_to_all | solution.py:310
  173.8 2.4 %unpack.2.refs_0_ = bf16[128,16384]{1,0:T(8,128)(2,1)} custom-call(bf16[8,128,1024]{2,1,0:T(8,128)(2,1)} %all-to-all-done.4.part_ref), custom_call_target="tpu_custom_call" | custom-call | bytes 4194304 | tf_op jit(solution)/shard_map/unpack/pallas_call | solution.py:250
  176.2 23.8 %all-to-all-done.3.part_ref = bf16[8,128,1024]{2,1,0:T(8,128)(2,1)S(1)} async-done(((bf16[8,128,1024]{2,1,0:T(8,128)(2,1)}), bf16[8,128,1024]{2,1,0:T(8,128)(2,1)S(1)}, u32[]{:S(2)}, u32[]{:S(2)}) %all-to-all-start.3) | async-done | bytes 2097184 | tf_op jit(solution)/shard_map/all_to_all | solution.py:310
  200.0 1.3 copy-done.2
  201.3 2.4 %unpack.3 = bf16[128,16384]{1,0:T(8,128)(2,1)} custom-call(bf16[8,128,1024]{2,1,0:T(8,128)(2,1)} %copy-done.2, bf16[128,16384]{1,0:T(8,128)(2,1)} %unpack.2.refs_0_), custom_call_target="tpu_custom_call", output_to_operand_aliasing={{}: (1, {})} | custom-call | bytes 4194304 | tf_op jit(solution)/shard_map/unpack/pallas_call | solution.py:250
  (85 shorter events, 6.7 us)
Async XLA Ops:
  0.0 1.0 copy-start
  2.1 13.1 %collective-permute-start.5 = (bf16[32,4,8,128]{3,2,0,1:T(8,128)(2,1)S(1)}, bf16[32,4,8,128]{3,2,0,1:T(8,128)(2,1)S(1)}, u32[]{:S(2)}, u32[]{:S(2)}) collective-permute-start(bf16[32,4,8,128]{3,2,0,1:T(8,128)(2,1)S(1)} %get-tuple-element.56), channel_id=1, source_target_pairs={{0,4},{1,5},{2,6},{3,7},{4,0},{5,1},{6,2},{7,3},{8,12},{9,13},{10,... | collective-permute-start | bytes 786440 | tf_op jit(solution)/shard_map/ppermute | solution.py:327
  2.9 37.5 %collective-permute-start = (bf16[32,8,8,128]{3,2,0,1:T(8,128)(2,1)S(1)}, bf16[32,8,8,128]{3,2,0,1:T(8,128)(2,1)S(1)}, u32[]{:S(2)}, u32[]{:S(2)}) collective-permute-start(bf16[32,8,8,128]{3,2,0,1:T(8,128)(2,1)S(1)} %pad_maximum_fusion), channel_id=1, source_target_pairs={{0,8},{8,16},{16,24},{24,32},{32,40},{40,48},{48,56},{56,64},{64,7... | collective-permute-start | bytes 1572872 | tf_op jit(solution)/shard_map/ppermute | solution.py:350
  7.1 4.8 %copy-start.13 = (s32[48]{0:T(128)S(1)}, s32[48]{0:T(128)}, u32[]{:S(2)}) copy-start(s32[48]{0:T(128)} %param.12) | copy-start | bytes 580
  7.1 5.3 %copy-start.12 = (s32[48]{0:T(128)S(1)}, s32[48]{0:T(128)}, u32[]{:S(2)}) copy-start(s32[48]{0:T(128)} %param.11) | copy-start | bytes 580
  7.1 6.1 %copy-start.11 = (s32[48]{0:T(128)S(1)}, s32[48]{0:T(128)}, u32[]{:S(2)}) copy-start(s32[48]{0:T(128)} %param.13) | copy-start | bytes 580
  11.5 55.4 %collective-permute-start.9 = (bf16[128,2048]{1,0:T(8,128)(2,1)}, bf16[128,2048]{1,0:T(8,128)(2,1)S(1)}, u32[]{:S(2)}, u32[]{:S(2)}) collective-permute-start(bf16[128,2048]{1,0:T(8,128)(2,1)} %get-tuple-element.29), channel_id=1, source_target_pairs={{0,4},{1,5},{2,6},{3,7},{4,0},{5,1},{6,2},{7,3},{8,12},{9,13},{10,... | collective-permute-start | bytes 1572872 | tf_op jit(solution)/shard_map/ppermute | solution.py:327
  15.3 8.2 %copy-start.5 = (bf16[2,32,1,8,128]{4,3,1,0,2:T(8,128)(2,1)}, bf16[2,32,1,8,128]{4,3,1,0,2:T(8,128)(2,1)S(1)}, u32[]{:S(2)}) copy-start(bf16[2,32,1,8,128]{4,3,1,0,2:T(8,128)(2,1)S(1)} %get-tuple-element.52) | copy-start | bytes 393220
  15.4 8.1 %collective-permute-start.8 = (bf16[2,32,8,128]{3,2,0,1:T(8,128)(2,1)S(1)}, bf16[2,32,8,128]{3,2,0,1:T(8,128)(2,1)S(1)}, u32[]{:S(2)}, u32[]{:S(2)}) collective-permute-start(bf16[2,32,8,128]{3,2,0,1:T(8,128)(2,1)S(1)} %bitcast.86), channel_id=1, source_target_pairs={{0,3},{1,0},{2,1},{3,2},{4,7},{5,4},{6,5},{7,6},{8,11},{9,8},{10,9... | collective-permute-start | bytes 393224 | tf_op jit(solution)/shard_map/ppermute | solution.py:327
  18.2 6.1 %collective-permute-start.7 = (bf16[2,32,8,128]{3,2,0,1:T(8,128)(2,1)S(1)}, bf16[2,32,8,128]{3,2,0,1:T(8,128)(2,1)S(1)}, u32[]{:S(2)}, u32[]{:S(2)}) collective-permute-start(bf16[2,32,8,128]{3,2,0,1:T(8,128)(2,1)S(1)} %bitcast.85), channel_id=1, source_target_pairs={{0,2},{1,3},{2,0},{3,1},{4,6},{5,7},{6,4},{7,5},{8,10},{9,11},{10,... | collective-permute-start | bytes 393224 | tf_op jit(solution)/shard_map/ppermute | solution.py:327
  18.5 9.4 %collective-permute-start.6 = (bf16[2,32,8,128]{3,2,0,1:T(8,128)(2,1)S(1)}, bf16[2,32,8,128]{3,2,0,1:T(8,128)(2,1)S(1)}, u32[]{:S(2)}, u32[]{:S(2)}) collective-permute-start(bf16[2,32,8,128]{3,2,0,1:T(8,128)(2,1)S(1)} %bitcast.84), channel_id=1, source_target_pairs={{0,1},{1,2},{2,3},{3,0},{4,5},{5,6},{6,7},{7,4},{8,9},{9,10},{10,1... | collective-permute-start | bytes 393224 | tf_op jit(solution)/shard_map/ppermute | solution.py:327
  23.5 5.3 %copy-start.7 = (bf16[2,32,8,128]{3,2,0,1:T(8,128)(2,1)}, bf16[2,32,8,128]{3,2,0,1:T(8,128)(2,1)S(1)}, u32[]{:S(2)}) copy-start(bf16[2,32,8,128]{3,2,0,1:T(8,128)(2,1)S(1)} %collective-permute-done.8) | copy-start | bytes 393220
  23.5 43.5 %collective-permute-start.10 = (bf16[128,2048]{1,0:T(8,128)(2,1)}, bf16[128,2048]{1,0:T(8,128)(2,1)S(1)}, u32[]{:S(2)}, u32[]{:S(2)}) collective-permute-start(bf16[128,2048]{1,0:T(8,128)(2,1)} %get-tuple-element.30), channel_id=1, source_target_pairs={{0,1},{1,2},{2,3},{3,0},{4,5},{5,6},{6,7},{7,4},{8,9},{9,10},{10,1... | collective-permute-start | bytes 1572872 | tf_op jit(solution)/shard_map/ppermute | solution.py:327
  24.3 4.5 %copy-start.8 = (bf16[2,32,8,128]{3,2,0,1:T(8,128)(2,1)}, bf16[2,32,8,128]{3,2,0,1:T(8,128)(2,1)S(1)}, u32[]{:S(2)}) copy-start(bf16[2,32,8,128]{3,2,0,1:T(8,128)(2,1)S(1)} %collective-permute-done.7) | copy-start | bytes 393220
  24.3 45.8 %collective-permute-start.12 = (bf16[128,2048]{1,0:T(8,128)(2,1)}, bf16[128,2048]{1,0:T(8,128)(2,1)}, u32[]{:S(2)}, u32[]{:S(2)}) collective-permute-start(bf16[128,2048]{1,0:T(8,128)(2,1)} %get-tuple-element.32), channel_id=1, source_target_pairs={{0,1},{1,2},{2,3},{3,0},{4,5},{5,6},{6,7},{7,4},{8,9},{9,10},{10,1... | collective-permute-start | bytes 1572872 | tf_op jit(solution)/shard_map/ppermute | solution.py:327
  27.9 0.9 copy-start.9
  27.9 44.2 %collective-permute-start.14 = (bf16[128,2048]{1,0:T(8,128)(2,1)}, bf16[128,2048]{1,0:T(8,128)(2,1)}, u32[]{:S(2)}, u32[]{:S(2)}) collective-permute-start(bf16[128,2048]{1,0:T(8,128)(2,1)} %get-tuple-element.33), channel_id=1, source_target_pairs={{0,3},{1,0},{2,1},{3,2},{4,7},{5,4},{6,5},{7,6},{8,11},{9,8},{10,9... | collective-permute-start | bytes 1572872 | tf_op jit(solution)/shard_map/ppermute | solution.py:327
  28.8 21.9 %all-to-all-start.1 = ((bf16[32,8,8,128]{3,2,1,0:T(8,128)(2,1)}), bf16[32,8,8,128]{3,2,1,0:T(8,128)(2,1)S(1)}, u32[]{:S(2)}, u32[]{:S(2)}) async-start(bf16[32,8,8,128]{3,2,1,0:T(8,128)(2,1)} %maximum_bitcast_fusion), calls=%async_computation.1 | async-start | bytes 1048576 | tf_op jit(solution)/shard_map/all_to_all | solution.py:353
  41.3 21.6 %collective-permute-start.1 = (bf16[32,4,8,128]{3,2,0,1:T(8,128)(2,1)}, bf16[32,4,8,128]{3,2,0,1:T(8,128)(2,1)}, u32[]{:S(2)}, u32[]{:S(2)}) collective-permute-start(bf16[32,4,8,128]{3,2,0,1:T(8,128)(2,1)} %get-tuple-element.62), channel_id=1, source_target_pairs={{0,4},{1,5},{2,6},{3,7},{4,0},{5,1},{6,2},{7,3},{8,12},{9,13},{10,... | collective-permute-start | bytes 786440 | tf_op jit(solution)/shard_map/ppermute | solution.py:327
  52.7 1.2 copy-start.4
  52.7 29.5 %copy-start.6 = (bf16[2,32,1,8,128]{4,3,1,0,2:T(8,128)(2,1)S(1)}, bf16[2,32,1,8,128]{4,3,1,0,2:T(8,128)(2,1)}, u32[]{:S(2)}) copy-start(bf16[2,32,1,8,128]{4,3,1,0,2:T(8,128)(2,1)} %copy-done.5) | copy-start | bytes 393220
  53.9 28.5 %all-to-all-start.2 = ((bf16[32,8,8,128]{3,2,1,0:T(8,128)(2,1)}), bf16[32,8,8,128]{3,2,1,0:T(8,128)(2,1)S(1)}, u32[]{:S(2)}, u32[]{:S(2)}) async-start(bf16[32,8,8,128]{3,2,1,0:T(8,128)(2,1)} %bitcast.74), calls=%async_computation.2 | async-start | bytes 1048576 | tf_op jit(solution)/shard_map/all_to_all | solution.py:378
  62.8 19.4 %copy-start.10 = (bf16[2,32,8,128]{3,2,0,1:T(8,128)(2,1)S(1)}, bf16[2,32,8,128]{3,2,0,1:T(8,128)(2,1)}, u32[]{:S(2)}) copy-start(bf16[2,32,8,128]{3,2,0,1:T(8,128)(2,1)} %copy-done.9) | copy-start | bytes 393220
  64.0 11.3 %collective-permute-start.2 = (bf16[2,32,8,128]{3,2,1,0:T(8,128)(2,1)S(1)}, bf16[2,32,8,128]{3,2,1,0:T(8,128)(2,1)S(1)}, u32[]{:S(2)}, u32[]{:S(2)}) collective-permute-start(bf16[2,32,8,128]{3,2,1,0:T(8,128)(2,1)S(1)} %get-tuple-element.59), channel_id=1, source_target_pairs={{0,1},{1,2},{2,3},{3,0},{4,5},{5,6},{6,7},{7,4},{8,9},{9,10},{10,1... | collective-permute-start | bytes 393224 | tf_op jit(solution)/shard_map/ppermute | solution.py:327
  66.9 8.4 %collective-permute-start.3 = (bf16[2,32,8,128]{3,2,1,0:T(8,128)(2,1)S(1)}, bf16[2,32,8,128]{3,2,1,0:T(8,128)(2,1)S(1)}, u32[]{:S(2)}, u32[]{:S(2)}) collective-permute-start(bf16[2,32,8,128]{3,2,1,0:T(8,128)(2,1)S(1)} %get-tuple-element.60), channel_id=1, source_target_pairs={{0,2},{1,3},{2,0},{3,1},{4,6},{5,7},{6,4},{7,5},{8,10},{9,11},{10,... | collective-permute-start | bytes 393224 | tf_op jit(solution)/shard_map/ppermute | solution.py:327
  67.0 10.4 %collective-permute-start.4 = (bf16[2,32,8,128]{3,2,1,0:T(8,128)(2,1)S(1)}, bf16[2,32,8,128]{3,2,1,0:T(8,128)(2,1)S(1)}, u32[]{:S(2)}, u32[]{:S(2)}) collective-permute-start(bf16[2,32,8,128]{3,2,1,0:T(8,128)(2,1)S(1)} %get-tuple-element.61), channel_id=1, source_target_pairs={{0,3},{1,0},{2,1},{3,2},{4,7},{5,4},{6,5},{7,6},{8,11},{9,8},{10,9... | collective-permute-start | bytes 393224 | tf_op jit(solution)/shard_map/ppermute | solution.py:327
  70.1 15.8 %collective-permute-start.11 = (bf16[128,2048]{1,0:T(8,128)(2,1)}, bf16[128,2048]{1,0:T(8,128)(2,1)}, u32[]{:S(2)}, u32[]{:S(2)}) collective-permute-start(bf16[128,2048]{1,0:T(8,128)(2,1)} %get-tuple-element.31), channel_id=1, source_target_pairs={{0,5},{1,6},{2,7},{3,4},{4,1},{5,2},{6,3},{7,0},{8,13},{9,14},{10,... | collective-permute-start | bytes 1572872 | tf_op jit(solution)/shard_map/ppermute | solution.py:327
  72.1 15.2 %collective-permute-start.16 = (bf16[128,2048]{1,0:T(8,128)(2,1)}, bf16[128,2048]{1,0:T(8,128)(2,1)}, u32[]{:S(2)}, u32[]{:S(2)}) collective-permute-start(bf16[128,2048]{1,0:T(8,128)(2,1)} %get-tuple-element.34), channel_id=1, source_target_pairs={{0,3},{1,0},{2,1},{3,2},{4,7},{5,4},{6,5},{7,6},{8,11},{9,8},{10,9... | collective-permute-start | bytes 1572872 | tf_op jit(solution)/shard_map/ppermute | solution.py:327
  75.3 23.5 %collective-permute-start.17 = (bf16[128,2048]{1,0:T(8,128)(2,1)}, bf16[128,2048]{1,0:T(8,128)(2,1)}, u32[]{:S(2)}, u32[]{:S(2)}) collective-permute-start(bf16[128,2048]{1,0:T(8,128)(2,1)} %get-tuple-element.35), channel_id=1, source_target_pairs={{0,7},{1,4},{2,5},{3,6},{4,3},{5,0},{6,1},{7,2},{8,15},{9,12},{10,... | collective-permute-start | bytes 1572872 | tf_op jit(solution)/shard_map/ppermute | solution.py:327
  75.3 23.5 %collective-permute-start.13 = (bf16[128,2048]{1,0:T(8,128)(2,1)}, bf16[128,2048]{1,0:T(8,128)(2,1)}, u32[]{:S(2)}, u32[]{:S(2)}) collective-permute-start(bf16[128,2048]{1,0:T(8,128)(2,1)} %collective-permute-done.12), channel_id=1, source_target_pairs={{0,1},{1,2},{2,3},{3,0},{4,5},{5,6},{6,7},{7,4},{8,9},{9,10},{10,1... | collective-permute-start | bytes 1572872 | tf_op jit(solution)/shard_map/ppermute | solution.py:327
  77.4 31.5 %collective-permute-start.15 = (bf16[128,2048]{1,0:T(8,128)(2,1)}, bf16[128,2048]{1,0:T(8,128)(2,1)}, u32[]{:S(2)}, u32[]{:S(2)}) collective-permute-start(bf16[128,2048]{1,0:T(8,128)(2,1)} %collective-permute-done.14), channel_id=1, source_target_pairs={{0,7},{1,4},{2,5},{3,6},{4,3},{5,0},{6,1},{7,2},{8,15},{9,12},{10,... | collective-permute-start | bytes 1572872 | tf_op jit(solution)/shard_map/ppermute | solution.py:327
  82.2 26.7 %copy-start.1 = (bf16[128,2048]{1,0:T(8,128)(2,1)S(1)}, bf16[128,2048]{1,0:T(8,128)(2,1)}, u32[]{:S(2)}) copy-start(bf16[128,2048]{1,0:T(8,128)(2,1)} %get-tuple-element.28.refs_4_) | copy-start | bytes 1572868
  82.4 0.8 copy-start.3
  136.4 32.6 %all-to-all-start.4 = ((bf16[8,128,1024]{2,1,0:T(8,128)(2,1)}), bf16[8,128,1024]{2,1,0:T(8,128)(2,1)}, u32[]{:S(2)}, u32[]{:S(2)}) async-start(bf16[8,128,1024]{2,1,0:T(8,128)(2,1)} %attend.3), calls=%async_computation.4 | async-start | bytes 4194304 | tf_op jit(solution)/shard_map/all_to_all | solution.py:310
  169.0 31.0 %all-to-all-start.3 = ((bf16[8,128,1024]{2,1,0:T(8,128)(2,1)}), bf16[8,128,1024]{2,1,0:T(8,128)(2,1)S(1)}, u32[]{:S(2)}, u32[]{:S(2)}) async-start(bf16[8,128,1024]{2,1,0:T(8,128)(2,1)} %attend.2), calls=%async_computation.3 | async-start | bytes 4194304 | tf_op jit(solution)/shard_map/all_to_all | solution.py:310
  200.0 1.4 copy-start.2

commit v5 on v4

--- a/solution.py
+++ b/solution.py
@@ -19,8 +19,8 @@
 SLOTS = GROUP * (DEPTH - 2) * HDR + HDR
 FAST_SLOTS = 8
 REST_SLOTS = SLOTS - FAST_SLOTS
-CHUNKS = 2
-STACK = 1
+CHUNK_HEADS = (4, 6, 6)
+STACK = 2
 LIST = WINDOW + (DEPTH - 1) * HDR
 NEG = -1e30
 VMEM_LIMIT = 48 * 1024 * 1024
@@ -78,7 +78,7 @@
     return slot_block, most, entries, filled
 
 
-def attend_kernel(chunk, filled_ref, entries_ref, order_ref, *refs):
+def attend_kernel(first_head, filled_ref, entries_ref, order_ref, *refs):
     near_and_far, query_refs, refs = refs[:4], refs[4:4 + GROUP], refs[4 + GROUP:]
     out_ref, pool, asked, sems, query_sems, scores, top, acc, den = refs
     step = pl.program_id(0)
@@ -88,7 +88,7 @@
 
     def query_copy(n):
         return pltpu.make_async_copy(
-            query_refs[n].at[:, pl.ds(chunk * width, width)], asked.at[n], query_sems.at[n]
+            query_refs[n].at[:, pl.ds(first_head * HEAD, width)], asked.at[n], query_sems.at[n]
         )
 
     @pl.when(step == 0)
@@ -120,31 +120,36 @@
     def tile(which, a, b):
         return jnp.concatenate([pool[a, which], pool[b, which]], axis=0)
 
-    def queries(g):
-        return jnp.concatenate(
-            [asked[step, :, h * HEAD:(h + 1) * HEAD] for h in range(g * STACK, (g + 1) * STACK)], axis=0
+    tall = STACK * BLK
+    stacks = heads // STACK
+
+    def rows_of(g):
+        return pl.ds(g * tall, tall)
+
+    def score(g, keys):
+        q = jnp.concatenate(
+            [asked[step, :, pl.ds(h * HEAD, HEAD)] for h in range(g * STACK, (g + 1) * STACK)], axis=0
         )
-
-    def score(q, keys):
         return lax.dot_general(q, keys, (((1,), (1,)), ((), ())), preferred_element_type=jnp.float32)
 
-    tall = STACK * BLK
-    groups = heads // STACK
-    row = lax.broadcasted_iota(jnp.int32, (tall, 2 * BLK), 0) % BLK
-    col = lax.broadcasted_iota(jnp.int32, (tall, 2 * BLK), 1)
+    row = lax.broadcasted_iota(jnp.int32, (BLK, 2 * BLK), 0)
+    col = lax.broadcasted_iota(jnp.int32, (BLK, 2 * BLK), 1)
     usable = (col <= row) | ((col >= BLK) & (odd == 1))
+
     keys = tile(0, diagonal, last)
-    for g in range(groups):
-        s = jnp.where(usable, score(queries(g), keys), NEG)
-        r = slice(g * tall, (g + 1) * tall)
-        scores[0, r, :] = s
-        top[r, :] = jnp.maximum(s[:, :BLK], s[:, BLK:])
+    for g in range(stacks):
+        s = score(g, keys)
+        s = jnp.concatenate(
+            [jnp.where(usable, s[n * BLK:(n + 1) * BLK], NEG) for n in range(STACK)], axis=0
+        )
+        scores[0, rows_of(g), :] = s
+        top[rows_of(g), :] = jnp.maximum(s[:, :BLK], s[:, BLK:])
 
     def first_pass(p, carry):
         keys = tile(0, entries_ref[step, 2 * p], entries_ref[step, 2 * p + 1])
-        for g in range(groups):
-            s = score(queries(g), keys)
-            r = slice(g * tall, (g + 1) * tall)
+        for g in range(stacks):
+            r = rows_of(g)
+            s = score(g, keys)
             scores[p + 1, r, :] = s
             top[r, :] = jnp.maximum(top[r, :], jnp.maximum(s[:, :BLK], s[:, BLK:]))
         return carry
@@ -153,8 +158,8 @@
 
     def weigh(p, a, b, fresh):
         vals = tile(1, a, b)
-        for g in range(groups):
-            r = slice(g * tall, (g + 1) * tall)
+        for g in range(stacks):
+            r = rows_of(g)
             t = top[r, :]
             s = scores[p, r, :]
             w0 = jnp.exp2((s[:, :BLK] - t) * EXP_SCALE)
@@ -170,9 +175,9 @@
                 den[r, :] += w0 + w1
                 acc[r, :] += mixed
 
-    for h in range(heads):
-        r = slice(h * BLK, (h + 1) * BLK)
-        top[r, :] = jnp.broadcast_to(jnp.max(top[r, :], axis=1, keepdims=True), (BLK, BLK))
+    for g in range(stacks):
+        r = rows_of(g)
+        top[r, :] = jnp.broadcast_to(jnp.max(top[r, :], axis=1, keepdims=True), (tall, BLK))
     weigh(0, diagonal, last, True)
 
     def second_pass(p, carry):
@@ -224,7 +229,7 @@
     )(targets, queries)
 
 
-def unpack_kernel(chunk, part_ref, *refs):
+def unpack_kernel(first_head, stride, part_ref, *refs):
     out_ref, held, in_sems, out_sems = refs[-4:]
     width = held.shape[2]
 
@@ -232,7 +237,7 @@
         return pltpu.make_async_copy(part_ref.at[n], held.at[n], in_sems.at[n])
 
     def put(n):
-        at = (n * CHUNKS + chunk) * width
+        at = n * stride + first_head * HEAD
         return pltpu.make_async_copy(held.at[n], out_ref.at[:, pl.ds(at, width)], out_sems.at[n])
 
     for n in range(GROUP):
@@ -244,12 +249,12 @@
         put(n).wait()
 
 
-def unpack(part, chunk, whole):
+def unpack(part, first_head, stride, whole):
     width = part.shape[2]
     held = () if whole is None else (whole,)
     return pl.pallas_call(
-        functools.partial(unpack_kernel, chunk),
-        out_shape=jax.ShapeDtypeStruct((BLK, GROUP * CHUNKS * width), part.dtype),
+        functools.partial(unpack_kernel, first_head, stride),
+        out_shape=jax.ShapeDtypeStruct((BLK, GROUP * stride), part.dtype),
         in_specs=[pl.BlockSpec(memory_space=pl.ANY)] * (1 + len(held)),
         out_specs=pl.BlockSpec(memory_space=pl.ANY),
         scratch_shapes=[
@@ -265,12 +270,11 @@
     )(part, *held)
 
 
-def attend(filled, entries, order, before, own, fast, rest, query, chunk):
-    width = query[0].shape[1] // CHUNKS
+def attend(filled, entries, order, before, own, fast, rest, query, first_head, heads):
+    width = heads * HEAD
     rows = width // HEAD * BLK
-    longest = 1 + LIST // 2
     return pl.pallas_call(
-        functools.partial(attend_kernel, chunk),
+        functools.partial(attend_kernel, first_head),
         out_shape=jax.ShapeDtypeStruct((GROUP, BLK, width), query[0].dtype),
         grid_spec=pltpu.PrefetchScalarGridSpec(
             num_scalar_prefetch=3,
@@ -282,7 +286,7 @@
                 pltpu.VMEM((GROUP, BLK, width), jnp.bfloat16),
                 pltpu.SemaphoreType.DMA((4,)),
                 pltpu.SemaphoreType.DMA((GROUP,)),
-                pltpu.VMEM((longest, rows, 2 * BLK), jnp.float32),
+                pltpu.VMEM((1 + LIST // 2, rows, 2 * BLK), jnp.float32),
                 pltpu.VMEM((rows, BLK), jnp.float32),
                 pltpu.VMEM((rows, HEAD), jnp.float32),
                 pltpu.VMEM((rows, BLK), jnp.float32),
@@ -333,10 +337,11 @@
     order = indices(-1)
     blocks = (-1, 2, BLK, HEAD)
 
-    def split(pieces_of):
+    def split(pieces_of, late=()):
         kept = lax.dynamic_slice_in_dim(pieces_of, core * ring_size, ring_size, 1)
         given = lax.dynamic_slice_in_dim(pieces_of, (1 - core) * ring_size, ring_size, 1)
         taken = move(given, 1, 0)
+        taken, *late = lax.optimization_barrier((taken, *late))
         both = jnp.stack([kept, taken])
         got = []
         for dt in range(ring_size):
@@ -344,17 +349,18 @@
             if dt:
                 piece = move(piece, 0, dt)
             got.append(piece)
-        return jnp.concatenate(got, axis=0)
+        return jnp.concatenate(got, axis=0), late
 
     sent = jnp.concatenate([tiles(keys), tiles(values)], axis=0)
     shifted = lax.ppermute(sent, across, [(j, j + 1) for j in range(groups - 1)])
-    near = split(sent)
+    near, _ = split(sent)
     own = near.reshape(blocks)
     everyone = lax.all_to_all(
         jnp.transpose(near, (1, 0, 2, 3)), across, split_axis=0, concat_axis=0, tiled=True
     )
     everyone = everyone.reshape(-1, pieces, HEAD)
-    before = split(shifted).reshape(blocks)
+    before, (lengths, parents, headers) = split(shifted, (lengths, parents, headers))
+    before = before.reshape(blocks)
 
     packed = pack(targets, queries)
     mine = []
@@ -386,9 +392,12 @@
     )
 
     whole = None
-    for chunk in range(CHUNKS):
-        part = exchange(attend(filled, entries, order, before, own, fast, rest, mine, chunk))
-        whole = unpack(part, chunk, whole)
+    first_head = 0
+    for heads in CHUNK_HEADS:
+        part = attend(filled, entries, order, before, own, fast, rest, mine, first_head, heads)
+        part = exchange(part)
+        whole = unpack(part, first_head, mine[0].shape[1], whole)
+        first_head += heads
     return whole
 
 

time: 205 us -> 215 us (1.049)
  Pallas kernels: 64.2 us -> 81 us
  waiting for transfers between devices: 60.7 us -> 50.1 us
  starting transfers between devices: 55.3 us -> 60.9 us
  local copies, waits for them, and re-layouts: 12.2 us -> 10 us
    pallas_call x4 -> x6, Pallas kernels: 59.8 us -> 76.7 us  [the longest x3 70 us: attend(): pl.pallas_call(functools.partial(attend_kernel, first_head), out_shape=ja...]
    all_to_all x2 -> x3, waiting for transfers between devices: 23.8 us -> 16.2 us  [exchange(): return lax.all_to_all(a, inside, split_axis=0, concat_axis=0, tiled=True)]
    all_to_all x2 -> x3, starting transfers between devices: 9.92 us -> 15 us  [exchange(): return lax.all_to_all(a, inside, split_axis=0, concat_axis=0, tiled=True)]
    ppermute x1, waiting for transfers between devices: 0.01 us -> 4.9 us  [body(): lax.ppermute(sent, across, [(j, j + 1) for j in range(groups - 1)])]
    ppermute x17, waiting for transfers between devices: 31.7 us -> 27 us  [move(): return lax.ppermute(piece, inside, pairs)]
    all_to_all x1, waiting for transfers between devices: 5.16 us -> 2.03 us  [body(): lax.all_to_all(jnp.transpose(near, (1, 0, 2, 3)), across, split_axis=0, c...]
    ppermute x17, starting transfers between devices: 22.8 us -> 24.9 us  [move(): return lax.ppermute(piece, inside, pairs)]
    unnamed x28 -> x26, local copies, waits for them, and re-layouts: 4.32 us -> 2.94 us
  transfers between devices with their start and end apart: 22 -> 23, of which waited for: 9 -> 7; matrix products, arithmetic and copies ran while one was open for 8% -> 8% of each run, Pallas kernels for 17% -> 27%
where the time goes in v5:
time: 215 us; the launch traced here: 214 us
  Pallas kernels  81 us (38%)
  starting transfers between devices  60.9 us (28%)
  waiting for transfers between devices  50.1 us (23%)
  other arithmetic  11 us (5%)
  local copies, waits for them, and re-layouts  10 us (5%)
    pallas_call x3, Pallas kernels, attend(): pl.pallas_call(functools.partial(attend_kernel, first_head), out_shape=ja...  70 us
    ppermute x17, waiting for transfers between devices, move(): return lax.ppermute(piece, inside, pairs)  27 us
    ppermute x17, starting transfers between devices, move(): return lax.ppermute(piece, inside, pairs)  24.9 us
    all_to_all x3, waiting for transfers between devices, exchange(): return lax.all_to_all(a, inside, split_axis=0, concat_axis=0, tiled=True)  16.2 us
    all_to_all x3, starting transfers between devices, exchange(): return lax.all_to_all(a, inside, split_axis=0, concat_axis=0, tiled=True)  15 us
    all_to_all x1, starting transfers between devices, fetch(): lax.all_to_all(picked, across, split_axis=0, concat_axis=0, tiled=True)  8.83 us
    all_to_all x1, starting transfers between devices, body(): lax.all_to_all(jnp.transpose(near, (1, 0, 2, 3)), across, split_axis=0, c...  8.65 us
    pallas_call x3, Pallas kernels, unpack(): pl.pallas_call(functools.partial(unpack_kernel, first_head, stride), out_...  6.67 us
  transfers between devices with their start and end apart: 23, of which 7 were waited for; matrix products, arithmetic and copies ran while one was open for 8% of the time, Pallas kernels for 27%

profile of v5, /device:TPU:3, one launch (start us, length us, event | category | flops | bytes accessed | tf_op | source)
XLA Modules:
  0.0 214.3 jit_solution(15380054024010952117)
XLA Ops:
  0.0 0.9 copy-done
  1.0 1.1 copy_bitcast_fusion
  2.1 0.8 collective-permute-start.5
  2.9 3.5 %collective-permute-start = (bf16[32,8,8,128]{3,2,0,1:T(8,128)(2,1)S(1)}, bf16[32,8,8,128]{3,2,0,1:T(8,128)(2,1)S(1)}, u32[]{:S(2)}, u32[]{:S(2)}) collective-permute-start(bf16[32,8,8,128]{3,2,0,1:T(8,128)(2,1)S(1)} %pad_maximum_fusion), channel_id=1, source_target_pairs={{0,8},{8,16},{16,24},{24,32},{32,40},{40,48},{48,56},{56,64},{64,7... | collective-permute-start | bytes 1572872 | tf_op jit(solution)/shard_map/ppermute | solution.py:355
  7.1 4.3 %pack.1 = (bf16[128,2048]{1,0:T(8,128)(2,1)}, bf16[128,2048]{1,0:T(8,128)(2,1)}, bf16[128,2048]{1,0:T(8,128)(2,1)}, bf16[128,2048]{1,0:T(8,128)(2,1)}, bf16[128,...) custom-call(s32[8]{0:T(128)} %stack.89.target_ref, ...), custom_call_target="tpu_custom_call" | custom-call | bytes 8388608 | tf_op jit(solution)/shard_map/pack/pallas_call | solution.py:217
  13.2 0.7 copy.61
  13.9 2.8 %collective-permute-start.8 = (bf16[2,32,8,128]{3,2,0,1:T(8,128)(2,1)S(1)}, bf16[2,32,8,128]{3,2,0,1:T(8,128)(2,1)S(1)}, u32[]{:S(2)}, u32[]{:S(2)}) collective-permute-start(bf16[2,32,8,128]{3,2,0,1:T(8,128)(2,1)S(1)} %bitcast.84), channel_id=1, source_target_pairs={{0,3},{1,0},{2,1},{3,2},{4,7},{5,4},{6,5},{7,6},{8,11},{9,8},{10,9... | collective-permute-start | bytes 393224 | tf_op jit(solution)/shard_map/ppermute | solution.py:331
  17.0 0.7 collective-permute-start.6
  17.7 4.9 %collective-permute-done = bf16[32,8,8,128]{3,2,0,1:T(8,128)(2,1)S(1)} collective-permute-done((bf16[32,8,8,128]{3,2,0,1:T(8,128)(2,1)S(1)}, bf16[32,8,8,128]{3,2,0,1:T(8,128)(2,1)S(1)}, u32[]{:S(2)}, u32[]{:S(2)}) %collective-permute-start) | collective-permute-done | bytes 524320 | tf_op jit(solution)/shard_map/ppermute | solution.py:355
  22.7 0.7 collective-permute-start.1
  23.9 1.4 collective-permute-start.10
  25.3 1.3 collective-permute-start.12
  26.6 1.4 collective-permute-start.14
  28.0 0.9 maximum_bitcast_fusion
  28.9 8.6 %all-to-all-start.1 = ((bf16[32,8,8,128]{3,2,1,0:T(8,128)(2,1)}), bf16[32,8,8,128]{3,2,1,0:T(8,128)(2,1)S(1)}, u32[]{:S(2)}, u32[]{:S(2)}) async-start(bf16[32,8,8,128]{3,2,1,0:T(8,128)(2,1)} %maximum_bitcast_fusion), calls=%async_computation.1 | async-start | bytes 1048576 | tf_op jit(solution)/shard_map/all_to_all | solution.py:358
  41.1 0.7 select_reduce_fusion.1
  42.0 1.7 fusion.18
  43.7 1.5 collective-permute-start.2
  45.2 0.8 select_reduce_fusion.12
  46.0 0.8 select_reduce_fusion.10
  47.1 2.0 all-to-all-done.1
  49.2 1.6 gather_fusion.1
  50.8 1.6 conditional.1
  50.8 1.6 broadcast.698
  52.4 8.8 %all-to-all-start.2 = ((bf16[32,8,8,128]{3,2,1,0:T(8,128)(2,1)}), bf16[32,8,8,128]{3,2,1,0:T(8,128)(2,1)S(1)}, u32[]{:S(2)}, u32[]{:S(2)}) async-start(bf16[32,8,8,128]{3,2,1,0:T(8,128)(2,1)} %bitcast.39), calls=%async_computation.2 | async-start | bytes 1048576 | tf_op jit(solution)/shard_map/all_to_all | solution.py:384
  61.2 2.3 %collective-permute-start.3 = (bf16[2,32,8,128]{3,2,1,0:T(8,128)(2,1)S(1)}, bf16[2,32,8,128]{3,2,1,0:T(8,128)(2,1)S(1)}, u32[]{:S(2)}, u32[]{:S(2)}) collective-permute-start(bf16[2,32,8,128]{3,2,1,0:T(8,128)(2,1)S(1)} %copy-done.5), channel_id=1, source_target_pairs={{0,2},{1,3},{2,0},{3,1},{4,6},{5,7},{6,4},{7,5},{8,10},{9,11},{10,... | collective-permute-start | bytes 393224 | tf_op jit(solution)/shard_map/ppermute | solution.py:331
  63.5 3.1 %collective-permute-start.4 = (bf16[2,32,8,128]{3,2,1,0:T(8,128)(2,1)S(1)}, bf16[2,32,8,128]{3,2,1,0:T(8,128)(2,1)S(1)}, u32[]{:S(2)}, u32[]{:S(2)}) collective-permute-start(bf16[2,32,8,128]{3,2,1,0:T(8,128)(2,1)S(1)} %get-tuple-element.69), channel_id=1, source_target_pairs={{0,3},{1,0},{2,1},{3,2},{4,7},{5,4},{6,5},{7,6},{8,11},{9,8},{10,9... | collective-permute-start | bytes 393224 | tf_op jit(solution)/shard_map/ppermute | solution.py:331
  66.7 1.9 collective-permute-start.11
  68.5 3.2 %collective-permute-start.16 = (bf16[128,2048]{1,0:T(8,128)(2,1)}, bf16[128,2048]{1,0:T(8,128)(2,1)}, u32[]{:S(2)}, u32[]{:S(2)}) collective-permute-start(bf16[128,2048]{1,0:T(8,128)(2,1)} %get-tuple-element.42), channel_id=1, source_target_pairs={{0,3},{1,0},{2,1},{3,2},{4,7},{5,4},{6,5},{7,6},{8,11},{9,8},{10,9... | collective-permute-start | bytes 1572872 | tf_op jit(solution)/shard_map/ppermute | solution.py:331
  71.8 3.2 %collective-permute-start.15 = (bf16[128,2048]{1,0:T(8,128)(2,1)}, bf16[128,2048]{1,0:T(8,128)(2,1)}, u32[]{:S(2)}, u32[]{:S(2)}) collective-permute-start(bf16[128,2048]{1,0:T(8,128)(2,1)} %collective-permute-done.14), channel_id=1, source_target_pairs={{0,7},{1,4},{2,5},{3,6},{4,3},{5,0},{6,1},{7,2},{8,15},{9,12},{10,... | collective-permute-start | bytes 1572872 | tf_op jit(solution)/shard_map/ppermute | solution.py:331
  75.2 1.0 pad_maximum_fusion.1.refs_0_
  76.1 0.8 copy-done.3
  76.9 1.1 copy.51
  78.1 2.8 %collective-permute-done.11.refs_7_ = bf16[128,2048]{1,0:T(8,128)(2,1)} collective-permute-done((bf16[128,2048]{1,0:T(8,128)(2,1)}, bf16[128,2048]{1,0:T(8,128)(2,1)}, u32[]{:S(2)}, u32[]{:S(2)}) %collective-permute-start.11) | collective-permute-done | bytes 524320 | tf_op jit(solution)/shard_map/ppermute | solution.py:331
  80.9 2.8 %collective-permute-done.16.refs_10_ = bf16[128,2048]{1,0:T(8,128)(2,1)} collective-permute-done((bf16[128,2048]{1,0:T(8,128)(2,1)}, bf16[128,2048]{1,0:T(8,128)(2,1)}, u32[]{:S(2)}, u32[]{:S(2)}) %collective-permute-start.16) | collective-permute-done | bytes 524320 | tf_op jit(solution)/shard_map/ppermute | solution.py:331
  83.8 11.4 %collective-permute-done.17.refs_11_ = bf16[128,2048]{1,0:T(8,128)(2,1)} collective-permute-done((bf16[128,2048]{1,0:T(8,128)(2,1)}, bf16[128,2048]{1,0:T(8,128)(2,1)}, u32[]{:S(2)}, u32[]{:S(2)}) %collective-permute-start.17) | collective-permute-done | bytes 524320 | tf_op jit(solution)/shard_map/ppermute | solution.py:331
  95.2 9.9 %collective-permute-done.15.refs_9_ = bf16[128,2048]{1,0:T(8,128)(2,1)} collective-permute-done((bf16[128,2048]{1,0:T(8,128)(2,1)}, bf16[128,2048]{1,0:T(8,128)(2,1)}, u32[]{:S(2)}, u32[]{:S(2)}) %collective-permute-start.15) | collective-permute-done | bytes 524320 | tf_op jit(solution)/shard_map/ppermute | solution.py:331
  105.0 21.3 %attend.5 = bf16[8,128,512]{2,1,0:T(8,128)(2,1)} custom-call(s32[8]{0:T(128)S(1)} %get-tuple-element.56.filled_ref, s32[8,12]{1,0:T(8,128)S(1)} %fusion.39.entries_ref, s32[8]{0:T(128)S(1)} %stack.76.order_ref, bf16[8,2,128,128]{3,2,1,0:T(8,128)(2,1)S(1)} %pad_maximum_fusion.1.refs_0_, bf16[8,2,128,128]{3,2,1,0:T(8,128)(2,1)S(1)} %pad_maximum_fusion.2.refs_1_, ...), custom_call_target="tpu_custom_call" | custom-call | flops 2147483648 | bytes 6291456 | tf_op jit(solution)/shard_map/attend/pallas_call | solution.py:276
  126.3 5.4 %all-to-all-start.5 = ((bf16[8,128,512]{2,1,0:T(8,128)(2,1)}), bf16[8,128,512]{2,1,0:T(8,128)(2,1)}, u32[]{:S(2)}, u32[]{:S(2)}) async-start(bf16[8,128,512]{2,1,0:T(8,128)(2,1)} %attend.5), calls=%async_computation.5 | async-start | bytes 2097152 | tf_op jit(solution)/shard_map/all_to_all | solution.py:314
  131.7 24.4 %attend.4 = bf16[8,128,768]{2,1,0:T(8,128)(2,1)} custom-call(s32[8]{0:T(128)S(1)} %get-tuple-element.56.filled_ref, s32[8,12]{1,0:T(8,128)S(1)} %fusion.39.entries_ref, s32[8]{0:T(128)S(1)} %stack.76.order_ref, bf16[8,2,128,128]{3,2,1,0:T(8,128)(2,1)S(1)} %pad_maximum_fusion.1.refs_0_, bf16[8,2,128,128]{3,2,1,0:T(8,128)(2,1)S(1)} %pad_maximum_fusion.2.refs_1_, ...), custom_call_target="tpu_custom_call" | custom-call | flops 3221225472 | bytes 6291456 | tf_op jit(solution)/shard_map/attend/pallas_call | solution.py:276
  156.1 4.8 %all-to-all-start.4 = ((bf16[8,128,768]{2,1,0:T(8,128)(2,1)}), bf16[8,128,768]{2,1,0:T(8,128)(2,1)}, u32[]{:S(2)}, u32[]{:S(2)}) async-start(bf16[8,128,768]{2,1,0:T(8,128)(2,1)} %attend.4), calls=%async_computation.4 | async-start | bytes 3145728 | tf_op jit(solution)/shard_map/all_to_all | solution.py:314
  160.9 24.4 %attend.3 = bf16[8,128,768]{2,1,0:T(8,128)(2,1)} custom-call(s32[8]{0:T(128)S(1)} %get-tuple-element.56.filled_ref, s32[8,12]{1,0:T(8,128)S(1)} %fusion.39.entries_ref, s32[8]{0:T(128)S(1)} %stack.76.order_ref, bf16[8,2,128,128]{3,2,1,0:T(8,128)(2,1)S(1)} %pad_maximum_fusion.1.refs_0_, bf16[8,2,128,128]{3,2,1,0:T(8,128)(2,1)S(1)} %pad_maximum_fusion.2.refs_1_, ...), custom_call_target="tpu_custom_call" | custom-call | flops 3221225472 | bytes 6291456 | tf_op jit(solution)/shard_map/attend/pallas_call | solution.py:276
  185.3 4.8 %all-to-all-start.3 = ((bf16[8,128,768]{2,1,0:T(8,128)(2,1)}), bf16[8,128,768]{2,1,0:T(8,128)(2,1)S(1)}, u32[]{:S(2)}, u32[]{:S(2)}) async-start(bf16[8,128,768]{2,1,0:T(8,128)(2,1)} %attend.3), calls=%async_computation.3 | async-start | bytes 3145728 | tf_op jit(solution)/shard_map/all_to_all | solution.py:314
  190.1 2.1 unpack.3.refs_0_
  192.2 2.3 %unpack.4.refs_0_ = bf16[128,16384]{1,0:T(8,128)(2,1)} custom-call(bf16[8,128,768]{2,1,0:T(8,128)(2,1)} %all-to-all-done.4.part_ref, bf16[128,16384]{1,0:T(8,128)(2,1)} %unpack.3.refs_0_), custom_call_target="tpu_custom_call", output_to_operand_aliasing={{}: (1, {})} | custom-call | bytes 3145728 | tf_op jit(solution)/shard_map/unpack/pallas_call | solution.py:255
  194.5 16.2 %all-to-all-done.3.part_ref = bf16[8,128,768]{2,1,0:T(8,128)(2,1)S(1)} async-done(((bf16[8,128,768]{2,1,0:T(8,128)(2,1)}), bf16[8,128,768]{2,1,0:T(8,128)(2,1)S(1)}, u32[]{:S(2)}, u32[]{:S(2)}) %all-to-all-start.3) | async-done | bytes 1572896 | tf_op jit(solution)/shard_map/all_to_all | solution.py:314
  210.6 1.2 copy-done.2
  211.8 2.3 %unpack.5 = bf16[128,16384]{1,0:T(8,128)(2,1)} custom-call(bf16[8,128,768]{2,1,0:T(8,128)(2,1)} %copy-done.2, bf16[128,16384]{1,0:T(8,128)(2,1)} %unpack.4.refs_0_), custom_call_target="tpu_custom_call", output_to_operand_aliasing={{}: (1, {})} | custom-call | bytes 3145728 | tf_op jit(solution)/shard_map/unpack/pallas_call | solution.py:255
  (88 shorter events, 7.1 us)
Async XLA Ops:
  0.0 1.0 copy-start
  2.1 11.0 %collective-permute-start.5 = (bf16[32,4,8,128]{3,2,0,1:T(8,128)(2,1)S(1)}, bf16[32,4,8,128]{3,2,0,1:T(8,128)(2,1)S(1)}, u32[]{:S(2)}, u32[]{:S(2)}) collective-permute-start(bf16[32,4,8,128]{3,2,0,1:T(8,128)(2,1)S(1)} %get-tuple-element.64), channel_id=1, source_target_pairs={{0,4},{1,5},{2,6},{3,7},{4,0},{5,1},{6,2},{7,3},{8,12},{9,13},{10,... | collective-permute-start | bytes 786440 | tf_op jit(solution)/shard_map/ppermute | solution.py:331
  2.9 19.7 %collective-permute-start = (bf16[32,8,8,128]{3,2,0,1:T(8,128)(2,1)S(1)}, bf16[32,8,8,128]{3,2,0,1:T(8,128)(2,1)S(1)}, u32[]{:S(2)}, u32[]{:S(2)}) collective-permute-start(bf16[32,8,8,128]{3,2,0,1:T(8,128)(2,1)S(1)} %pad_maximum_fusion), channel_id=1, source_target_pairs={{0,8},{8,16},{16,24},{24,32},{32,40},{40,48},{48,56},{56,64},{64,7... | collective-permute-start | bytes 1572872 | tf_op jit(solution)/shard_map/ppermute | solution.py:355
  11.4 49.8 %collective-permute-start.9 = (bf16[128,2048]{1,0:T(8,128)(2,1)}, bf16[128,2048]{1,0:T(8,128)(2,1)S(1)}, u32[]{:S(2)}, u32[]{:S(2)}) collective-permute-start(bf16[128,2048]{1,0:T(8,128)(2,1)} %get-tuple-element.37), channel_id=1, source_target_pairs={{0,4},{1,5},{2,6},{3,7},{4,0},{5,1},{6,2},{7,3},{8,12},{9,13},{10,... | collective-permute-start | bytes 1572872 | tf_op jit(solution)/shard_map/ppermute | solution.py:331
  13.9 10.0 %collective-permute-start.8 = (bf16[2,32,8,128]{3,2,0,1:T(8,128)(2,1)S(1)}, bf16[2,32,8,128]{3,2,0,1:T(8,128)(2,1)S(1)}, u32[]{:S(2)}, u32[]{:S(2)}) collective-permute-start(bf16[2,32,8,128]{3,2,0,1:T(8,128)(2,1)S(1)} %bitcast.84), channel_id=1, source_target_pairs={{0,3},{1,0},{2,1},{3,2},{4,7},{5,4},{6,5},{7,6},{8,11},{9,8},{10,9... | collective-permute-start | bytes 393224 | tf_op jit(solution)/shard_map/ppermute | solution.py:331
  16.7 8.6 %collective-permute-start.7 = (bf16[2,32,8,128]{3,2,0,1:T(8,128)(2,1)}, bf16[2,32,8,128]{3,2,0,1:T(8,128)(2,1)S(1)}, u32[]{:S(2)}, u32[]{:S(2)}) collective-permute-start(bf16[2,32,8,128]{3,2,0,1:T(8,128)(2,1)} %bitcast.67), channel_id=1, source_target_pairs={{0,2},{1,3},{2,0},{3,1},{4,6},{5,7},{6,4},{7,5},{8,10},{9,11},{10,... | collective-permute-start | bytes 393224 | tf_op jit(solution)/shard_map/ppermute | solution.py:331
  17.0 9.6 %collective-permute-start.6 = (bf16[2,32,8,128]{3,2,0,1:T(8,128)(2,1)S(1)}, bf16[2,32,8,128]{3,2,0,1:T(8,128)(2,1)S(1)}, u32[]{:S(2)}, u32[]{:S(2)}) collective-permute-start(bf16[2,32,8,128]{3,2,0,1:T(8,128)(2,1)S(1)} %bitcast.83), channel_id=1, source_target_pairs={{0,1},{1,2},{2,3},{3,0},{4,5},{5,6},{6,7},{7,4},{8,9},{9,10},{10,1... | collective-permute-start | bytes 393224 | tf_op jit(solution)/shard_map/ppermute | solution.py:331
  22.7 15.0 %collective-permute-start.1 = (bf16[32,4,8,128]{3,2,0,1:T(8,128)(2,1)S(1)}, bf16[32,4,8,128]{3,2,0,1:T(8,128)(2,1)}, u32[]{:S(2)}, u32[]{:S(2)}) collective-permute-start(bf16[32,4,8,128]{3,2,0,1:T(8,128)(2,1)S(1)} %get-tuple-element.71), channel_id=1, source_target_pairs={{0,4},{1,5},{2,6},{3,7},{4,0},{5,1},{6,2},{7,3},{8,12},{9,13},{10,... | collective-permute-start | bytes 786440 | tf_op jit(solution)/shard_map/ppermute | solution.py:331
  23.9 39.6 %collective-permute-start.10 = (bf16[128,2048]{1,0:T(8,128)(2,1)}, bf16[128,2048]{1,0:T(8,128)(2,1)S(1)}, u32[]{:S(2)}, u32[]{:S(2)}) collective-permute-start(bf16[128,2048]{1,0:T(8,128)(2,1)} %get-tuple-element.38), channel_id=1, source_target_pairs={{0,1},{1,2},{2,3},{3,0},{4,5},{5,6},{6,7},{7,4},{8,9},{9,10},{10,1... | collective-permute-start | bytes 1572872 | tf_op jit(solution)/shard_map/ppermute | solution.py:331
  25.3 41.4 %collective-permute-start.12 = (bf16[128,2048]{1,0:T(8,128)(2,1)}, bf16[128,2048]{1,0:T(8,128)(2,1)}, u32[]{:S(2)}, u32[]{:S(2)}) collective-permute-start(bf16[128,2048]{1,0:T(8,128)(2,1)} %get-tuple-element.40), channel_id=1, source_target_pairs={{0,1},{1,2},{2,3},{3,0},{4,5},{5,6},{6,7},{7,4},{8,9},{9,10},{10,1... | collective-permute-start | bytes 1572872 | tf_op jit(solution)/shard_map/ppermute | solution.py:331
  26.6 41.9 %collective-permute-start.14 = (bf16[128,2048]{1,0:T(8,128)(2,1)}, bf16[128,2048]{1,0:T(8,128)(2,1)}, u32[]{:S(2)}, u32[]{:S(2)}) collective-permute-start(bf16[128,2048]{1,0:T(8,128)(2,1)} %get-tuple-element.41), channel_id=1, source_target_pairs={{0,3},{1,0},{2,1},{3,2},{4,7},{5,4},{6,5},{7,6},{8,11},{9,8},{10,9... | collective-permute-start | bytes 1572872 | tf_op jit(solution)/shard_map/ppermute | solution.py:331
  28.8 8.8 %copy-start.8 = (s32[48]{0:T(128)S(1)}, s32[48]{0:T(128)}, u32[]{:S(2)}) copy-start(s32[48]{0:T(128)} %param.12) | copy-start | bytes 580
  28.8 9.4 %copy-start.7 = (s32[48]{0:T(128)S(1)}, s32[48]{0:T(128)}, u32[]{:S(2)}) copy-start(s32[48]{0:T(128)} %param.11) | copy-start | bytes 580
  28.8 9.5 %copy-start.12 = (s32[8]{0:T(128)S(1)}, s32[8]{0:T(128)}, u32[]{:S(2)}) copy-start(s32[8]{0:T(128)} %broadcast_add_fusion.5) | copy-start | bytes 100
  28.9 9.9 %copy-start.6 = (s32[48]{0:T(128)S(1)}, s32[48]{0:T(128)}, u32[]{:S(2)}) copy-start(s32[48]{0:T(128)} %param.13) | copy-start | bytes 580
  28.9 9.9 %copy-start.9 = (s32[32]{0:T(128)S(1)}, s32[32]{0:T(128)}, u32[]{:S(2)}) copy-start(s32[32]{0:T(128)} %get-tuple-element.79) | copy-start | bytes 388
  28.9 9.9 %copy-start.10 = (s32[32]{0:T(128)S(1)}, s32[32]{0:T(128)}, u32[]{:S(2)}) copy-start(s32[32]{0:T(128)} %get-tuple-element.80) | copy-start | bytes 388
  28.9 9.9 %copy-start.11 = (pred[48]{0:T(512)(128)(4,1)S(1)}, pred[48]{0:T(512)(128)(4,1)}, u32[]{:S(2)}) copy-start(pred[48]{0:T(512)(128)(4,1)} %iota_compare_fusion.16) | copy-start | bytes 148
  28.9 20.3 %all-to-all-start.1 = ((bf16[32,8,8,128]{3,2,1,0:T(8,128)(2,1)}), bf16[32,8,8,128]{3,2,1,0:T(8,128)(2,1)S(1)}, u32[]{:S(2)}, u32[]{:S(2)}) async-start(bf16[32,8,8,128]{3,2,1,0:T(8,128)(2,1)} %maximum_bitcast_fusion), calls=%async_computation.1 | async-start | bytes 1048576 | tf_op jit(solution)/shard_map/all_to_all | solution.py:358
  43.7 28.0 %collective-permute-start.2 = (bf16[2,32,8,128]{3,2,1,0:T(8,128)(2,1)}, bf16[2,32,8,128]{3,2,1,0:T(8,128)(2,1)S(1)}, u32[]{:S(2)}, u32[]{:S(2)}) collective-permute-start(bf16[2,32,8,128]{3,2,1,0:T(8,128)(2,1)} %get-tuple-element.67), channel_id=1, source_target_pairs={{0,1},{1,2},{2,3},{3,0},{4,5},{5,6},{6,7},{7,4},{8,9},{9,10},{10,1... | collective-permute-start | bytes 393224 | tf_op jit(solution)/shard_map/ppermute | solution.py:331
  50.8 10.5 %copy-start.5 = (bf16[2,32,8,128]{3,2,1,0:T(8,128)(2,1)S(1)}, bf16[2,32,8,128]{3,2,1,0:T(8,128)(2,1)}, u32[]{:S(2)}) copy-start(bf16[2,32,8,128]{3,2,1,0:T(8,128)(2,1)} %get-tuple-element.68) | copy-start | bytes 393220
  52.4 52.7 %copy-start.1 = (bf16[128,2048]{1,0:T(8,128)(2,1)S(1)}, bf16[128,2048]{1,0:T(8,128)(2,1)}, u32[]{:S(2)}) copy-start(bf16[128,2048]{1,0:T(8,128)(2,1)} %get-tuple-element.36.refs_4_) | copy-start | bytes 1572868
  52.4 23.8 %all-to-all-start.2 = ((bf16[32,8,8,128]{3,2,1,0:T(8,128)(2,1)}), bf16[32,8,8,128]{3,2,1,0:T(8,128)(2,1)S(1)}, u32[]{:S(2)}, u32[]{:S(2)}) async-start(bf16[32,8,8,128]{3,2,1,0:T(8,128)(2,1)} %bitcast.39), calls=%async_computation.2 | async-start | bytes 1048576 | tf_op jit(solution)/shard_map/all_to_all | solution.py:384
  61.2 10.5 %collective-permute-start.3 = (bf16[2,32,8,128]{3,2,1,0:T(8,128)(2,1)S(1)}, bf16[2,32,8,128]{3,2,1,0:T(8,128)(2,1)S(1)}, u32[]{:S(2)}, u32[]{:S(2)}) collective-permute-start(bf16[2,32,8,128]{3,2,1,0:T(8,128)(2,1)S(1)} %copy-done.5), channel_id=1, source_target_pairs={{0,2},{1,3},{2,0},{3,1},{4,6},{5,7},{6,4},{7,5},{8,10},{9,11},{10,... | collective-permute-start | bytes 393224 | tf_op jit(solution)/shard_map/ppermute | solution.py:331
  63.5 8.3 %collective-permute-start.4 = (bf16[2,32,8,128]{3,2,1,0:T(8,128)(2,1)S(1)}, bf16[2,32,8,128]{3,2,1,0:T(8,128)(2,1)S(1)}, u32[]{:S(2)}, u32[]{:S(2)}) collective-permute-start(bf16[2,32,8,128]{3,2,1,0:T(8,128)(2,1)S(1)} %get-tuple-element.69), channel_id=1, source_target_pairs={{0,3},{1,0},{2,1},{3,2},{4,7},{5,4},{6,5},{7,6},{8,11},{9,8},{10,9... | collective-permute-start | bytes 393224 | tf_op jit(solution)/shard_map/ppermute | solution.py:331
  66.7 14.3 %collective-permute-start.11 = (bf16[128,2048]{1,0:T(8,128)(2,1)}, bf16[128,2048]{1,0:T(8,128)(2,1)}, u32[]{:S(2)}, u32[]{:S(2)}) collective-permute-start(bf16[128,2048]{1,0:T(8,128)(2,1)} %get-tuple-element.39), channel_id=1, source_target_pairs={{0,5},{1,6},{2,7},{3,4},{4,1},{5,2},{6,3},{7,0},{8,13},{9,14},{10,... | collective-permute-start | bytes 1572872 | tf_op jit(solution)/shard_map/ppermute | solution.py:331
  68.5 15.2 %collective-permute-start.16 = (bf16[128,2048]{1,0:T(8,128)(2,1)}, bf16[128,2048]{1,0:T(8,128)(2,1)}, u32[]{:S(2)}, u32[]{:S(2)}) collective-permute-start(bf16[128,2048]{1,0:T(8,128)(2,1)} %get-tuple-element.42), channel_id=1, source_target_pairs={{0,3},{1,0},{2,1},{3,2},{4,7},{5,4},{6,5},{7,6},{8,11},{9,8},{10,9... | collective-permute-start | bytes 1572872 | tf_op jit(solution)/shard_map/ppermute | solution.py:331
  71.7 3.4 %copy-start.4 = (bf16[2,32,8,128]{3,2,1,0:T(8,128)(2,1)}, bf16[2,32,8,128]{3,2,1,0:T(8,128)(2,1)S(1)}, u32[]{:S(2)}) copy-start(bf16[2,32,8,128]{3,2,1,0:T(8,128)(2,1)S(1)} %collective-permute-done.2) | copy-start | bytes 393220
  71.7 23.5 %collective-permute-start.17 = (bf16[128,2048]{1,0:T(8,128)(2,1)}, bf16[128,2048]{1,0:T(8,128)(2,1)}, u32[]{:S(2)}, u32[]{:S(2)}) collective-permute-start(bf16[128,2048]{1,0:T(8,128)(2,1)} %get-tuple-element.43), channel_id=1, source_target_pairs={{0,7},{1,4},{2,5},{3,6},{4,3},{5,0},{6,1},{7,2},{8,15},{9,12},{10,... | collective-permute-start | bytes 1572872 | tf_op jit(solution)/shard_map/ppermute | solution.py:331
  71.7 23.5 %collective-permute-start.13 = (bf16[128,2048]{1,0:T(8,128)(2,1)}, bf16[128,2048]{1,0:T(8,128)(2,1)}, u32[]{:S(2)}, u32[]{:S(2)}) collective-permute-start(bf16[128,2048]{1,0:T(8,128)(2,1)} %collective-permute-done.12), channel_id=1, source_target_pairs={{0,1},{1,2},{2,3},{3,0},{4,5},{5,6},{6,7},{7,4},{8,9},{9,10},{10,1... | collective-permute-start | bytes 1572872 | tf_op jit(solution)/shard_map/ppermute | solution.py:331
  71.8 33.2 %collective-permute-start.15 = (bf16[128,2048]{1,0:T(8,128)(2,1)}, bf16[128,2048]{1,0:T(8,128)(2,1)}, u32[]{:S(2)}, u32[]{:S(2)}) collective-permute-start(bf16[128,2048]{1,0:T(8,128)(2,1)} %collective-permute-done.14), channel_id=1, source_target_pairs={{0,7},{1,4},{2,5},{3,6},{4,3},{5,0},{6,1},{7,2},{8,15},{9,12},{10,... | collective-permute-start | bytes 1572872 | tf_op jit(solution)/shard_map/ppermute | solution.py:331
  76.1 0.8 copy-start.3
  126.3 29.8 %all-to-all-start.5 = ((bf16[8,128,512]{2,1,0:T(8,128)(2,1)}), bf16[8,128,512]{2,1,0:T(8,128)(2,1)}, u32[]{:S(2)}, u32[]{:S(2)}) async-start(bf16[8,128,512]{2,1,0:T(8,128)(2,1)} %attend.5), calls=%async_computation.5 | async-start | bytes 2097152 | tf_op jit(solution)/shard_map/all_to_all | solution.py:314
  156.1 29.2 %all-to-all-start.4 = ((bf16[8,128,768]{2,1,0:T(8,128)(2,1)}), bf16[8,128,768]{2,1,0:T(8,128)(2,1)}, u32[]{:S(2)}, u32[]{:S(2)}) async-start(bf16[8,128,768]{2,1,0:T(8,128)(2,1)} %attend.4), calls=%async_computation.4 | async-start | bytes 3145728 | tf_op jit(solution)/shard_map/all_to_all | solution.py:314
  185.3 25.4 %all-to-all-start.3 = ((bf16[8,128,768]{2,1,0:T(8,128)(2,1)}), bf16[8,128,768]{2,1,0:T(8,128)(2,1)S(1)}, u32[]{:S(2)}, u32[]{:S(2)}) async-start(bf16[8,128,768]{2,1,0:T(8,128)(2,1)} %attend.3), calls=%async_computation.3 | async-start | bytes 3145728 | tf_op jit(solution)/shard_map/all_to_all | solution.py:314
  210.6 1.2 copy-start.2

commit v6 on v5

--- a/solution.py
+++ b/solution.py
@@ -19,8 +19,8 @@
 SLOTS = GROUP * (DEPTH - 2) * HDR + HDR
 FAST_SLOTS = 8
 REST_SLOTS = SLOTS - FAST_SLOTS
-CHUNK_HEADS = (4, 6, 6)
-STACK = 2
+CHUNK_HEADS = (8, 8)
+STACK = 1
 LIST = WINDOW + (DEPTH - 1) * HDR
 NEG = -1e30
 VMEM_LIMIT = 48 * 1024 * 1024
@@ -78,7 +78,7 @@
     return slot_block, most, entries, filled
 
 
-def attend_kernel(first_head, filled_ref, entries_ref, order_ref, *refs):
+def attend_kernel(first_head, filled_ref, entries_ref, order_ref, more_ref, *refs):
     near_and_far, query_refs, refs = refs[:4], refs[4:4 + GROUP], refs[4 + GROUP:]
     out_ref, pool, asked, sems, query_sems, scores, top, acc, den = refs
     step = pl.program_id(0)
@@ -95,7 +95,7 @@
     def _():
         copies = []
         at = 0
-        for n, ref in enumerate(near_and_far):
+        for n, ref in enumerate(near_and_far[:3]):
             copies.append(pltpu.make_async_copy(ref, pool.at[pl.ds(at, ref.shape[0])], sems.at[n]))
             at += ref.shape[0]
         query_copy(0).start()
@@ -105,6 +105,13 @@
             query_copy(n).start()
         for c in copies:
             c.wait()
+
+        @pl.when(more_ref[0] > 0)
+        def _():
+            rest_ref = near_and_far[3]
+            rest_copy = pltpu.make_async_copy(rest_ref, pool.at[pl.ds(at, rest_ref.shape[0])], sems.at[3])
+            rest_copy.start()
+            rest_copy.wait()
 
     for n in range(GROUP):
         @pl.when(step == n)
@@ -270,17 +277,17 @@
     )(part, *held)
 
 
-def attend(filled, entries, order, before, own, fast, rest, query, first_head, heads):
+def attend(filled, entries, order, overflow, before, own, fast, rest, query, first_head, heads):
     width = heads * HEAD
     rows = width // HEAD * BLK
     return pl.pallas_call(
         functools.partial(attend_kernel, first_head),
         out_shape=jax.ShapeDtypeStruct((GROUP, BLK, width), query[0].dtype),
         grid_spec=pltpu.PrefetchScalarGridSpec(
-            num_scalar_prefetch=3,
+            num_scalar_prefetch=4,
             grid=(GROUP,),
             in_specs=[pl.BlockSpec(memory_space=pl.ANY)] * (4 + GROUP),
-            out_specs=pl.BlockSpec((1, BLK, width), lambda i, f, e, order_ref: (order_ref[i], 0, 0)),
+            out_specs=pl.BlockSpec((1, BLK, width), lambda i, f, e, order_ref, m: (order_ref[i], 0, 0)),
             scratch_shapes=[
                 pltpu.VMEM((NEAR + SLOTS, 2, BLK, HEAD), jnp.bfloat16),
                 pltpu.VMEM((GROUP, BLK, width), jnp.bfloat16),
@@ -297,7 +304,7 @@
             flops=GROUP * rows * 4 * 8 * BLK * HEAD, bytes_accessed=6 << 20, transcendentals=0
         ),
         name="attend",
-    )(filled, entries, order, before, own, fast, rest, *query)
+    )(filled, entries, order, overflow, before, own, fast, rest, *query)
 
 
 def body(queries, keys, values, lengths, parents, headers):
@@ -391,10 +398,11 @@
         lambda: jnp.zeros((REST_SLOTS,) + own.shape[1:], own.dtype),
     )
 
+    overflow = (most > FAST_SLOTS).astype(jnp.int32).reshape(1)
     whole = None
     first_head = 0
     for heads in CHUNK_HEADS:
-        part = attend(filled, entries, order, before, own, fast, rest, mine, first_head, heads)
+        part = attend(filled, entries, order, overflow, before, own, fast, rest, mine, first_head, heads)
         part = exchange(part)
         whole = unpack(part, first_head, mine[0].shape[1], whole)
         first_head += heads
@@ -404,6 +412,4 @@
 def solution(mesh):
     inner = Mesh(mesh.devices.reshape(4, 8, 2, 4), ("x", "z", "c", "t"))
     rows = P(("x", "z", "c", "t"), None)
-    return jax.shard_map(
-        body, mesh=inner, in_specs=(rows, rows, rows, P(), P(), P()), out_specs=rows, check_vma=False
-    )
+    return jax.shard_map(body, mesh=inner, in_specs=(rows, rows, rows, P(), P(), P()), out_specs=rows, check_vma=False)

time: 215 us -> 198 us (0.921)
  Pallas kernels: 81 us -> 61.3 us
  waiting for transfers between devices: 50.1 us -> 57.9 us
  starting transfers between devices: 60.9 us -> 55.9 us
    pallas_call x3 -> x2, Pallas kernels: 70 us -> 52.2 us  [attend(): pl.pallas_call(functools.partial(attend_kernel, first_head), out_shape=ja...]
    all_to_all x3 -> x2, waiting for transfers between devices: 16.2 us -> 24 us  [exchange(): return lax.all_to_all(a, inside, split_axis=0, concat_axis=0, tiled=True)]
    all_to_all x3 -> x2, starting transfers between devices: 15 us -> 9.98 us  [exchange(): return lax.all_to_all(a, inside, split_axis=0, concat_axis=0, tiled=True)]
    pallas_call x3 -> x2, Pallas kernels: 6.67 us -> 4.79 us  [unpack(): pl.pallas_call(functools.partial(unpack_kernel, first_head, stride), out_...]
  transfers between devices with their start and end apart: 23 -> 22, of which waited for: 7 -> 8; matrix products, arithmetic and copies ran while one was open for 8% -> 9% of each run, Pallas kernels for 27% -> 17%
where the time goes in v6:
time: 198 us; the launch traced here: 197 us
  Pallas kernels  61.3 us (31%)
  waiting for transfers between devices  57.9 us (29%)
  starting transfers between devices  55.9 us (28%)
  other arithmetic  11 us (6%)
  local copies, waits for them, and re-layouts  10.2 us (5%)
    pallas_call x2, Pallas kernels, attend(): pl.pallas_call(functools.partial(attend_kernel, first_head), out_shape=ja...  52.2 us
    ppermute x17, waiting for transfers between devices, move(): return lax.ppermute(piece, inside, pairs)  27 us
    ppermute x17, starting transfers between devices, move(): return lax.ppermute(piece, inside, pairs)  24.9 us
    all_to_all x2, waiting for transfers between devices, exchange(): return lax.all_to_all(a, inside, split_axis=0, concat_axis=0, tiled=True)  24 us
    all_to_all x2, starting transfers between devices, exchange(): return lax.all_to_all(a, inside, split_axis=0, concat_axis=0, tiled=True)  9.98 us
    all_to_all x1, starting transfers between devices, fetch(): lax.all_to_all(picked, across, split_axis=0, concat_axis=0, tiled=True)  8.83 us
    all_to_all x1, starting transfers between devices, body(): lax.all_to_all(jnp.transpose(near, (1, 0, 2, 3)), across, split_axis=0, c...  8.6 us
    ppermute x1, waiting for transfers between devices, body(): lax.ppermute(sent, across, [(j, j + 1) for j in range(groups - 1)])  4.92 us
  transfers between devices with their start and end apart: 22, of which 8 were waited for; matrix products, arithmetic and copies ran while one was open for 9% of the time, Pallas kernels for 17%

profile of v6, /device:TPU:3, one launch (start us, length us, event | category | flops | bytes accessed | tf_op | source)
XLA Modules:
  0.0 197.5 jit_solution(6310771736312575137)
XLA Ops:
  0.0 0.9 copy-done
  1.0 1.1 copy_bitcast_fusion
  2.1 0.8 collective-permute-start.5
  2.9 3.5 %collective-permute-start = (bf16[32,8,8,128]{3,2,0,1:T(8,128)(2,1)S(1)}, bf16[32,8,8,128]{3,2,0,1:T(8,128)(2,1)S(1)}, u32[]{:S(2)}, u32[]{:S(2)}) collective-permute-start(bf16[32,8,8,128]{3,2,0,1:T(8,128)(2,1)S(1)} %pad_maximum_fusion), channel_id=1, source_target_pairs={{0,8},{8,16},{16,24},{24,32},{32,40},{40,48},{48,56},{56,64},{64,7... | collective-permute-start | bytes 1572872 | tf_op jit(solution)/shard_map/ppermute | solution.py:362
  6.5 0.6 stack.89.target_ref
  7.1 4.3 %pack.1 = (bf16[128,2048]{1,0:T(8,128)(2,1)}, bf16[128,2048]{1,0:T(8,128)(2,1)}, bf16[128,2048]{1,0:T(8,128)(2,1)}, bf16[128,2048]{1,0:T(8,128)(2,1)}, bf16[128,...) custom-call(s32[8]{0:T(128)} %stack.89.target_ref, ...), custom_call_target="tpu_custom_call" | custom-call | bytes 8388608 | tf_op jit(solution)/shard_map/pack/pallas_call | solution.py:224
  13.2 0.7 copy.60
  13.9 2.8 %collective-permute-start.8 = (bf16[2,32,8,128]{3,2,0,1:T(8,128)(2,1)S(1)}, bf16[2,32,8,128]{3,2,0,1:T(8,128)(2,1)S(1)}, u32[]{:S(2)}, u32[]{:S(2)}) collective-permute-start(bf16[2,32,8,128]{3,2,0,1:T(8,128)(2,1)S(1)} %bitcast.84), channel_id=1, source_target_pairs={{0,3},{1,0},{2,1},{3,2},{4,7},{5,4},{6,5},{7,6},{8,11},{9,8},{10,9... | collective-permute-start | bytes 393224 | tf_op jit(solution)/shard_map/ppermute | solution.py:338
  17.0 0.7 collective-permute-start.6
  17.7 4.9 %collective-permute-done = bf16[32,8,8,128]{3,2,0,1:T(8,128)(2,1)S(1)} collective-permute-done((bf16[32,8,8,128]{3,2,0,1:T(8,128)(2,1)S(1)}, bf16[32,8,8,128]{3,2,0,1:T(8,128)(2,1)S(1)}, u32[]{:S(2)}, u32[]{:S(2)}) %collective-permute-start) | collective-permute-done | bytes 524320 | tf_op jit(solution)/shard_map/ppermute | solution.py:362
  22.7 0.7 collective-permute-start.1
  23.9 1.4 collective-permute-start.10
  25.3 1.3 collective-permute-start.12
  26.6 1.4 collective-permute-start.14
  28.0 0.9 maximum_bitcast_fusion
  28.9 8.6 %all-to-all-start.1 = ((bf16[32,8,8,128]{3,2,1,0:T(8,128)(2,1)}), bf16[32,8,8,128]{3,2,1,0:T(8,128)(2,1)S(1)}, u32[]{:S(2)}, u32[]{:S(2)}) async-start(bf16[32,8,8,128]{3,2,1,0:T(8,128)(2,1)} %maximum_bitcast_fusion), calls=%async_computation.1 | async-start | bytes 1048576 | tf_op jit(solution)/shard_map/all_to_all | solution.py:365
  39.3 0.7 reduce_max.9
  40.6 0.6 select_reduce_fusion
  41.2 0.7 select_reduce_fusion.1
  42.0 1.7 fusion.18
  43.7 1.5 collective-permute-start.2
  45.2 0.8 select_reduce_fusion.12
  46.0 0.8 select_reduce_fusion.10
  47.2 2.0 all-to-all-done.1
  49.2 1.6 gather_fusion.1
  50.7 1.6 conditional.1
  50.7 1.6 broadcast.698
  52.3 8.8 %all-to-all-start.2 = ((bf16[32,8,8,128]{3,2,1,0:T(8,128)(2,1)}), bf16[32,8,8,128]{3,2,1,0:T(8,128)(2,1)S(1)}, u32[]{:S(2)}, u32[]{:S(2)}) async-start(bf16[32,8,8,128]{3,2,1,0:T(8,128)(2,1)} %bitcast.40), calls=%async_computation.2 | async-start | bytes 1048576 | tf_op jit(solution)/shard_map/all_to_all | solution.py:391
  61.2 2.3 %collective-permute-start.3 = (bf16[2,32,8,128]{3,2,1,0:T(8,128)(2,1)S(1)}, bf16[2,32,8,128]{3,2,1,0:T(8,128)(2,1)S(1)}, u32[]{:S(2)}, u32[]{:S(2)}) collective-permute-start(bf16[2,32,8,128]{3,2,1,0:T(8,128)(2,1)S(1)} %copy-done.5), channel_id=1, source_target_pairs={{0,2},{1,3},{2,0},{3,1},{4,6},{5,7},{6,4},{7,5},{8,10},{9,11},{10,... | collective-permute-start | bytes 393224 | tf_op jit(solution)/shard_map/ppermute | solution.py:338
  63.5 3.1 %collective-permute-start.4 = (bf16[2,32,8,128]{3,2,1,0:T(8,128)(2,1)S(1)}, bf16[2,32,8,128]{3,2,1,0:T(8,128)(2,1)S(1)}, u32[]{:S(2)}, u32[]{:S(2)}) collective-permute-start(bf16[2,32,8,128]{3,2,1,0:T(8,128)(2,1)S(1)} %get-tuple-element.69), channel_id=1, source_target_pairs={{0,3},{1,0},{2,1},{3,2},{4,7},{5,4},{6,5},{7,6},{8,11},{9,8},{10,9... | collective-permute-start | bytes 393224 | tf_op jit(solution)/shard_map/ppermute | solution.py:338
  66.6 1.9 collective-permute-start.11
  68.5 3.2 %collective-permute-start.16 = (bf16[128,2048]{1,0:T(8,128)(2,1)}, bf16[128,2048]{1,0:T(8,128)(2,1)}, u32[]{:S(2)}, u32[]{:S(2)}) collective-permute-start(bf16[128,2048]{1,0:T(8,128)(2,1)} %get-tuple-element.42), channel_id=1, source_target_pairs={{0,3},{1,0},{2,1},{3,2},{4,7},{5,4},{6,5},{7,6},{8,11},{9,8},{10,9... | collective-permute-start | bytes 1572872 | tf_op jit(solution)/shard_map/ppermute | solution.py:338
  71.8 3.2 %collective-permute-start.15 = (bf16[128,2048]{1,0:T(8,128)(2,1)}, bf16[128,2048]{1,0:T(8,128)(2,1)}, u32[]{:S(2)}, u32[]{:S(2)}) collective-permute-start(bf16[128,2048]{1,0:T(8,128)(2,1)} %collective-permute-done.14), channel_id=1, source_target_pairs={{0,7},{1,4},{2,5},{3,6},{4,3},{5,0},{6,1},{7,2},{8,15},{9,12},{10,... | collective-permute-start | bytes 1572872 | tf_op jit(solution)/shard_map/ppermute | solution.py:338
  75.1 1.0 pad_maximum_fusion.1.refs_0_
  76.1 0.8 copy-done.3
  76.9 1.1 copy.50
  78.0 2.8 %collective-permute-done.11.refs_7_ = bf16[128,2048]{1,0:T(8,128)(2,1)} collective-permute-done((bf16[128,2048]{1,0:T(8,128)(2,1)}, bf16[128,2048]{1,0:T(8,128)(2,1)}, u32[]{:S(2)}, u32[]{:S(2)}) %collective-permute-start.11) | collective-permute-done | bytes 524320 | tf_op jit(solution)/shard_map/ppermute | solution.py:338
  80.9 2.8 %collective-permute-done.16.refs_10_ = bf16[128,2048]{1,0:T(8,128)(2,1)} collective-permute-done((bf16[128,2048]{1,0:T(8,128)(2,1)}, bf16[128,2048]{1,0:T(8,128)(2,1)}, u32[]{:S(2)}, u32[]{:S(2)}) %collective-permute-start.16) | collective-permute-done | bytes 524320 | tf_op jit(solution)/shard_map/ppermute | solution.py:338
  83.7 11.4 %collective-permute-done.17.refs_11_ = bf16[128,2048]{1,0:T(8,128)(2,1)} collective-permute-done((bf16[128,2048]{1,0:T(8,128)(2,1)}, bf16[128,2048]{1,0:T(8,128)(2,1)}, u32[]{:S(2)}, u32[]{:S(2)}) %collective-permute-start.17) | collective-permute-done | bytes 524320 | tf_op jit(solution)/shard_map/ppermute | solution.py:338
  95.1 9.9 %collective-permute-done.15.refs_9_ = bf16[128,2048]{1,0:T(8,128)(2,1)} collective-permute-done((bf16[128,2048]{1,0:T(8,128)(2,1)}, bf16[128,2048]{1,0:T(8,128)(2,1)}, u32[]{:S(2)}, u32[]{:S(2)}) %collective-permute-start.15) | collective-permute-done | bytes 524320 | tf_op jit(solution)/shard_map/ppermute | solution.py:338
  105.0 26.1 %attend.3 = bf16[8,128,1024]{2,1,0:T(8,128)(2,1)} custom-call(s32[8]{0:T(128)S(1)} %get-tuple-element.56.filled_ref, s32[8,12]{1,0:T(8,128)S(1)} %fusion.39.entries_ref, s32[8]{0:T(128)S(1)} %stack.76.order_ref, s32[1]{0:T(128)} %bitcast.17.more_ref, bf16[8,2,128,128]{3,2,1,0:T(8,128)(2,1)S(1)} %pad_maximum_fusion.1.refs_0_, ...), custom_call_target="tpu_custom_call" | custom-call | flops 4294967296 | bytes 6291456 | tf_op jit(solution)/shard_map/attend/pallas_call | solution.py:283
  131.1 5.3 %all-to-all-start.4 = ((bf16[8,128,1024]{2,1,0:T(8,128)(2,1)}), bf16[8,128,1024]{2,1,0:T(8,128)(2,1)}, u32[]{:S(2)}, u32[]{:S(2)}) async-start(bf16[8,128,1024]{2,1,0:T(8,128)(2,1)} %attend.3), calls=%async_computation.4 | async-start | bytes 4194304 | tf_op jit(solution)/shard_map/all_to_all | solution.py:321
  136.5 26.1 %attend.2 = bf16[8,128,1024]{2,1,0:T(8,128)(2,1)} custom-call(s32[8]{0:T(128)S(1)} %get-tuple-element.56.filled_ref, s32[8,12]{1,0:T(8,128)S(1)} %fusion.39.entries_ref, s32[8]{0:T(128)S(1)} %stack.76.order_ref, s32[1]{0:T(128)} %bitcast.17.more_ref, bf16[8,2,128,128]{3,2,1,0:T(8,128)(2,1)S(1)} %pad_maximum_fusion.1.refs_0_, ...), custom_call_target="tpu_custom_call" | custom-call | flops 4294967296 | bytes 6291456 | tf_op jit(solution)/shard_map/attend/pallas_call | solution.py:283
  162.8 4.6 %all-to-all-start.3 = ((bf16[8,128,1024]{2,1,0:T(8,128)(2,1)}), bf16[8,128,1024]{2,1,0:T(8,128)(2,1)S(1)}, u32[]{:S(2)}, u32[]{:S(2)}) async-start(bf16[8,128,1024]{2,1,0:T(8,128)(2,1)} %attend.2), calls=%async_computation.3 | async-start | bytes 4194304 | tf_op jit(solution)/shard_map/all_to_all | solution.py:321
  167.4 2.4 %unpack.2.refs_0_ = bf16[128,16384]{1,0:T(8,128)(2,1)} custom-call(bf16[8,128,1024]{2,1,0:T(8,128)(2,1)} %all-to-all-done.4.part_ref), custom_call_target="tpu_custom_call" | custom-call | bytes 4194304 | tf_op jit(solution)/shard_map/unpack/pallas_call | solution.py:262
  169.8 23.8 %all-to-all-done.3.part_ref = bf16[8,128,1024]{2,1,0:T(8,128)(2,1)S(1)} async-done(((bf16[8,128,1024]{2,1,0:T(8,128)(2,1)}), bf16[8,128,1024]{2,1,0:T(8,128)(2,1)S(1)}, u32[]{:S(2)}, u32[]{:S(2)}) %all-to-all-start.3) | async-done | bytes 2097184 | tf_op jit(solution)/shard_map/all_to_all | solution.py:321
  193.6 1.3 copy-done.2
  194.9 2.4 %unpack.3 = bf16[128,16384]{1,0:T(8,128)(2,1)} custom-call(bf16[8,128,1024]{2,1,0:T(8,128)(2,1)} %copy-done.2, bf16[128,16384]{1,0:T(8,128)(2,1)} %unpack.2.refs_0_), custom_call_target="tpu_custom_call", output_to_operand_aliasing={{}: (1, {})} | custom-call | bytes 4194304 | tf_op jit(solution)/shard_map/unpack/pallas_call | solution.py:262
  (84 shorter events, 5.4 us)
Async XLA Ops:
  0.0 1.0 copy-start
  2.1 11.0 %collective-permute-start.5 = (bf16[32,4,8,128]{3,2,0,1:T(8,128)(2,1)S(1)}, bf16[32,4,8,128]{3,2,0,1:T(8,128)(2,1)S(1)}, u32[]{:S(2)}, u32[]{:S(2)}) collective-permute-start(bf16[32,4,8,128]{3,2,0,1:T(8,128)(2,1)S(1)} %get-tuple-element.64), channel_id=1, source_target_pairs={{0,4},{1,5},{2,6},{3,7},{4,0},{5,1},{6,2},{7,3},{8,12},{9,13},{10,... | collective-permute-start | bytes 786440 | tf_op jit(solution)/shard_map/ppermute | solution.py:338
  2.9 19.7 %collective-permute-start = (bf16[32,8,8,128]{3,2,0,1:T(8,128)(2,1)S(1)}, bf16[32,8,8,128]{3,2,0,1:T(8,128)(2,1)S(1)}, u32[]{:S(2)}, u32[]{:S(2)}) collective-permute-start(bf16[32,8,8,128]{3,2,0,1:T(8,128)(2,1)S(1)} %pad_maximum_fusion), channel_id=1, source_target_pairs={{0,8},{8,16},{16,24},{24,32},{32,40},{40,48},{48,56},{56,64},{64,7... | collective-permute-start | bytes 1572872 | tf_op jit(solution)/shard_map/ppermute | solution.py:362
  11.4 49.7 %collective-permute-start.9 = (bf16[128,2048]{1,0:T(8,128)(2,1)}, bf16[128,2048]{1,0:T(8,128)(2,1)S(1)}, u32[]{:S(2)}, u32[]{:S(2)}) collective-permute-start(bf16[128,2048]{1,0:T(8,128)(2,1)} %get-tuple-element.37), channel_id=1, source_target_pairs={{0,4},{1,5},{2,6},{3,7},{4,0},{5,1},{6,2},{7,3},{8,12},{9,13},{10,... | collective-permute-start | bytes 1572872 | tf_op jit(solution)/shard_map/ppermute | solution.py:338
  13.9 10.1 %collective-permute-start.8 = (bf16[2,32,8,128]{3,2,0,1:T(8,128)(2,1)S(1)}, bf16[2,32,8,128]{3,2,0,1:T(8,128)(2,1)S(1)}, u32[]{:S(2)}, u32[]{:S(2)}) collective-permute-start(bf16[2,32,8,128]{3,2,0,1:T(8,128)(2,1)S(1)} %bitcast.84), channel_id=1, source_target_pairs={{0,3},{1,0},{2,1},{3,2},{4,7},{5,4},{6,5},{7,6},{8,11},{9,8},{10,9... | collective-permute-start | bytes 393224 | tf_op jit(solution)/shard_map/ppermute | solution.py:338
  16.7 8.7 %collective-permute-start.7 = (bf16[2,32,8,128]{3,2,0,1:T(8,128)(2,1)}, bf16[2,32,8,128]{3,2,0,1:T(8,128)(2,1)S(1)}, u32[]{:S(2)}, u32[]{:S(2)}) collective-permute-start(bf16[2,32,8,128]{3,2,0,1:T(8,128)(2,1)} %bitcast.68), channel_id=1, source_target_pairs={{0,2},{1,3},{2,0},{3,1},{4,6},{5,7},{6,4},{7,5},{8,10},{9,11},{10,... | collective-permute-start | bytes 393224 | tf_op jit(solution)/shard_map/ppermute | solution.py:338
  17.0 9.6 %collective-permute-start.6 = (bf16[2,32,8,128]{3,2,0,1:T(8,128)(2,1)S(1)}, bf16[2,32,8,128]{3,2,0,1:T(8,128)(2,1)S(1)}, u32[]{:S(2)}, u32[]{:S(2)}) collective-permute-start(bf16[2,32,8,128]{3,2,0,1:T(8,128)(2,1)S(1)} %bitcast.83), channel_id=1, source_target_pairs={{0,1},{1,2},{2,3},{3,0},{4,5},{5,6},{6,7},{7,4},{8,9},{9,10},{10,1... | collective-permute-start | bytes 393224 | tf_op jit(solution)/shard_map/ppermute | solution.py:338
  22.7 15.0 %collective-permute-start.1 = (bf16[32,4,8,128]{3,2,0,1:T(8,128)(2,1)S(1)}, bf16[32,4,8,128]{3,2,0,1:T(8,128)(2,1)}, u32[]{:S(2)}, u32[]{:S(2)}) collective-permute-start(bf16[32,4,8,128]{3,2,0,1:T(8,128)(2,1)S(1)} %get-tuple-element.71), channel_id=1, source_target_pairs={{0,4},{1,5},{2,6},{3,7},{4,0},{5,1},{6,2},{7,3},{8,12},{9,13},{10,... | collective-permute-start | bytes 786440 | tf_op jit(solution)/shard_map/ppermute | solution.py:338
  23.9 39.5 %collective-permute-start.10 = (bf16[128,2048]{1,0:T(8,128)(2,1)}, bf16[128,2048]{1,0:T(8,128)(2,1)S(1)}, u32[]{:S(2)}, u32[]{:S(2)}) collective-permute-start(bf16[128,2048]{1,0:T(8,128)(2,1)} %get-tuple-element.38), channel_id=1, source_target_pairs={{0,1},{1,2},{2,3},{3,0},{4,5},{5,6},{6,7},{7,4},{8,9},{9,10},{10,1... | collective-permute-start | bytes 1572872 | tf_op jit(solution)/shard_map/ppermute | solution.py:338
  25.3 41.3 %collective-permute-start.12 = (bf16[128,2048]{1,0:T(8,128)(2,1)}, bf16[128,2048]{1,0:T(8,128)(2,1)}, u32[]{:S(2)}, u32[]{:S(2)}) collective-permute-start(bf16[128,2048]{1,0:T(8,128)(2,1)} %get-tuple-element.40), channel_id=1, source_target_pairs={{0,1},{1,2},{2,3},{3,0},{4,5},{5,6},{6,7},{7,4},{8,9},{9,10},{10,1... | collective-permute-start | bytes 1572872 | tf_op jit(solution)/shard_map/ppermute | solution.py:338
  26.6 41.9 %collective-permute-start.14 = (bf16[128,2048]{1,0:T(8,128)(2,1)}, bf16[128,2048]{1,0:T(8,128)(2,1)}, u32[]{:S(2)}, u32[]{:S(2)}) collective-permute-start(bf16[128,2048]{1,0:T(8,128)(2,1)} %get-tuple-element.41), channel_id=1, source_target_pairs={{0,3},{1,0},{2,1},{3,2},{4,7},{5,4},{6,5},{7,6},{8,11},{9,8},{10,9... | collective-permute-start | bytes 1572872 | tf_op jit(solution)/shard_map/ppermute | solution.py:338
  28.9 8.8 %copy-start.8 = (s32[48]{0:T(128)S(1)}, s32[48]{0:T(128)}, u32[]{:S(2)}) copy-start(s32[48]{0:T(128)} %param.12) | copy-start | bytes 580
  28.9 9.3 %copy-start.7 = (s32[48]{0:T(128)S(1)}, s32[48]{0:T(128)}, u32[]{:S(2)}) copy-start(s32[48]{0:T(128)} %param.11) | copy-start | bytes 580
  28.9 9.4 %copy-start.12 = (s32[8]{0:T(128)S(1)}, s32[8]{0:T(128)}, u32[]{:S(2)}) copy-start(s32[8]{0:T(128)} %broadcast_add_fusion.5) | copy-start | bytes 100
  28.9 9.8 %copy-start.6 = (s32[48]{0:T(128)S(1)}, s32[48]{0:T(128)}, u32[]{:S(2)}) copy-start(s32[48]{0:T(128)} %param.13) | copy-start | bytes 580
  28.9 9.8 %copy-start.9 = (s32[32]{0:T(128)S(1)}, s32[32]{0:T(128)}, u32[]{:S(2)}) copy-start(s32[32]{0:T(128)} %get-tuple-element.79) | copy-start | bytes 388
  28.9 9.8 %copy-start.10 = (s32[32]{0:T(128)S(1)}, s32[32]{0:T(128)}, u32[]{:S(2)}) copy-start(s32[32]{0:T(128)} %get-tuple-element.80) | copy-start | bytes 388
  28.9 9.9 %copy-start.11 = (pred[48]{0:T(512)(128)(4,1)S(1)}, pred[48]{0:T(512)(128)(4,1)}, u32[]{:S(2)}) copy-start(pred[48]{0:T(512)(128)(4,1)} %iota_compare_fusion.16) | copy-start | bytes 148
  28.9 20.2 %all-to-all-start.1 = ((bf16[32,8,8,128]{3,2,1,0:T(8,128)(2,1)}), bf16[32,8,8,128]{3,2,1,0:T(8,128)(2,1)S(1)}, u32[]{:S(2)}, u32[]{:S(2)}) async-start(bf16[32,8,8,128]{3,2,1,0:T(8,128)(2,1)} %maximum_bitcast_fusion), calls=%async_computation.1 | async-start | bytes 1048576 | tf_op jit(solution)/shard_map/all_to_all | solution.py:365
  43.7 27.9 %collective-permute-start.2 = (bf16[2,32,8,128]{3,2,1,0:T(8,128)(2,1)}, bf16[2,32,8,128]{3,2,1,0:T(8,128)(2,1)S(1)}, u32[]{:S(2)}, u32[]{:S(2)}) collective-permute-start(bf16[2,32,8,128]{3,2,1,0:T(8,128)(2,1)} %get-tuple-element.67), channel_id=1, source_target_pairs={{0,1},{1,2},{2,3},{3,0},{4,5},{5,6},{6,7},{7,4},{8,9},{9,10},{10,1... | collective-permute-start | bytes 393224 | tf_op jit(solution)/shard_map/ppermute | solution.py:338
  50.7 10.5 %copy-start.5 = (bf16[2,32,8,128]{3,2,1,0:T(8,128)(2,1)S(1)}, bf16[2,32,8,128]{3,2,1,0:T(8,128)(2,1)}, u32[]{:S(2)}) copy-start(bf16[2,32,8,128]{3,2,1,0:T(8,128)(2,1)} %get-tuple-element.68) | copy-start | bytes 393220
  52.3 52.7 %copy-start.1 = (bf16[128,2048]{1,0:T(8,128)(2,1)S(1)}, bf16[128,2048]{1,0:T(8,128)(2,1)}, u32[]{:S(2)}) copy-start(bf16[128,2048]{1,0:T(8,128)(2,1)} %get-tuple-element.36.refs_4_) | copy-start | bytes 1572868
  52.3 23.8 %all-to-all-start.2 = ((bf16[32,8,8,128]{3,2,1,0:T(8,128)(2,1)}), bf16[32,8,8,128]{3,2,1,0:T(8,128)(2,1)S(1)}, u32[]{:S(2)}, u32[]{:S(2)}) async-start(bf16[32,8,8,128]{3,2,1,0:T(8,128)(2,1)} %bitcast.40), calls=%async_computation.2 | async-start | bytes 1048576 | tf_op jit(solution)/shard_map/all_to_all | solution.py:391
  61.2 10.5 %collective-permute-start.3 = (bf16[2,32,8,128]{3,2,1,0:T(8,128)(2,1)S(1)}, bf16[2,32,8,128]{3,2,1,0:T(8,128)(2,1)S(1)}, u32[]{:S(2)}, u32[]{:S(2)}) collective-permute-start(bf16[2,32,8,128]{3,2,1,0:T(8,128)(2,1)S(1)} %copy-done.5), channel_id=1, source_target_pairs={{0,2},{1,3},{2,0},{3,1},{4,6},{5,7},{6,4},{7,5},{8,10},{9,11},{10,... | collective-permute-start | bytes 393224 | tf_op jit(solution)/shard_map/ppermute | solution.py:338
  63.5 8.3 %collective-permute-start.4 = (bf16[2,32,8,128]{3,2,1,0:T(8,128)(2,1)S(1)}, bf16[2,32,8,128]{3,2,1,0:T(8,128)(2,1)S(1)}, u32[]{:S(2)}, u32[]{:S(2)}) collective-permute-start(bf16[2,32,8,128]{3,2,1,0:T(8,128)(2,1)S(1)} %get-tuple-element.69), channel_id=1, source_target_pairs={{0,3},{1,0},{2,1},{3,2},{4,7},{5,4},{6,5},{7,6},{8,11},{9,8},{10,9... | collective-permute-start | bytes 393224 | tf_op jit(solution)/shard_map/ppermute | solution.py:338
  66.6 14.3 %collective-permute-start.11 = (bf16[128,2048]{1,0:T(8,128)(2,1)}, bf16[128,2048]{1,0:T(8,128)(2,1)}, u32[]{:S(2)}, u32[]{:S(2)}) collective-permute-start(bf16[128,2048]{1,0:T(8,128)(2,1)} %get-tuple-element.39), channel_id=1, source_target_pairs={{0,5},{1,6},{2,7},{3,4},{4,1},{5,2},{6,3},{7,0},{8,13},{9,14},{10,... | collective-permute-start | bytes 1572872 | tf_op jit(solution)/shard_map/ppermute | solution.py:338
  68.5 15.2 %collective-permute-start.16 = (bf16[128,2048]{1,0:T(8,128)(2,1)}, bf16[128,2048]{1,0:T(8,128)(2,1)}, u32[]{:S(2)}, u32[]{:S(2)}) collective-permute-start(bf16[128,2048]{1,0:T(8,128)(2,1)} %get-tuple-element.42), channel_id=1, source_target_pairs={{0,3},{1,0},{2,1},{3,2},{4,7},{5,4},{6,5},{7,6},{8,11},{9,8},{10,9... | collective-permute-start | bytes 1572872 | tf_op jit(solution)/shard_map/ppermute | solution.py:338
  71.7 3.4 %copy-start.4 = (bf16[2,32,8,128]{3,2,1,0:T(8,128)(2,1)}, bf16[2,32,8,128]{3,2,1,0:T(8,128)(2,1)S(1)}, u32[]{:S(2)}) copy-start(bf16[2,32,8,128]{3,2,1,0:T(8,128)(2,1)S(1)} %collective-permute-done.2) | copy-start | bytes 393220
  71.7 23.5 %collective-permute-start.17 = (bf16[128,2048]{1,0:T(8,128)(2,1)}, bf16[128,2048]{1,0:T(8,128)(2,1)}, u32[]{:S(2)}, u32[]{:S(2)}) collective-permute-start(bf16[128,2048]{1,0:T(8,128)(2,1)} %get-tuple-element.43), channel_id=1, source_target_pairs={{0,7},{1,4},{2,5},{3,6},{4,3},{5,0},{6,1},{7,2},{8,15},{9,12},{10,... | collective-permute-start | bytes 1572872 | tf_op jit(solution)/shard_map/ppermute | solution.py:338
  71.7 23.5 %collective-permute-start.13 = (bf16[128,2048]{1,0:T(8,128)(2,1)}, bf16[128,2048]{1,0:T(8,128)(2,1)}, u32[]{:S(2)}, u32[]{:S(2)}) collective-permute-start(bf16[128,2048]{1,0:T(8,128)(2,1)} %collective-permute-done.12), channel_id=1, source_target_pairs={{0,1},{1,2},{2,3},{3,0},{4,5},{5,6},{6,7},{7,4},{8,9},{9,10},{10,1... | collective-permute-start | bytes 1572872 | tf_op jit(solution)/shard_map/ppermute | solution.py:338
  71.8 33.2 %collective-permute-start.15 = (bf16[128,2048]{1,0:T(8,128)(2,1)}, bf16[128,2048]{1,0:T(8,128)(2,1)}, u32[]{:S(2)}, u32[]{:S(2)}) collective-permute-start(bf16[128,2048]{1,0:T(8,128)(2,1)} %collective-permute-done.14), channel_id=1, source_target_pairs={{0,7},{1,4},{2,5},{3,6},{4,3},{5,0},{6,1},{7,2},{8,15},{9,12},{10,... | collective-permute-start | bytes 1572872 | tf_op jit(solution)/shard_map/ppermute | solution.py:338
  76.1 0.8 copy-start.3
  131.1 31.6 %all-to-all-start.4 = ((bf16[8,128,1024]{2,1,0:T(8,128)(2,1)}), bf16[8,128,1024]{2,1,0:T(8,128)(2,1)}, u32[]{:S(2)}, u32[]{:S(2)}) async-start(bf16[8,128,1024]{2,1,0:T(8,128)(2,1)} %attend.3), calls=%async_computation.4 | async-start | bytes 4194304 | tf_op jit(solution)/shard_map/all_to_all | solution.py:321
  162.8 30.8 %all-to-all-start.3 = ((bf16[8,128,1024]{2,1,0:T(8,128)(2,1)}), bf16[8,128,1024]{2,1,0:T(8,128)(2,1)S(1)}, u32[]{:S(2)}, u32[]{:S(2)}) async-start(bf16[8,128,1024]{2,1,0:T(8,128)(2,1)} %attend.2), calls=%async_computation.3 | async-start | bytes 4194304 | tf_op jit(solution)/shard_map/all_to_all | solution.py:321
  193.6 1.4 copy-start.2
